TPU v7x, 32 devices: a whole 2x2x4 slice. The times are simulated.
32 devices in a mesh: gx: 8 (over z, core), gy: 4 (over y, x).
Axes of the slice: x: 2, y: 2, z: 4, core: 2. Of those that a mesh axis runs over, the one named last changes fastest.
Arguments:
- populations: float32 [19, 128, 32, 256], P(None, 'gx', 'gy'), may hold values from 0 to 0.5, as said below
- relax_rate: float32 [128, 32, 256], P('gx', 'gy'), may hold values from 0.6 to 1.6
- solid_mask: int32 [128, 32, 256], P('gx', 'gy'), may hold values 0 or 1
- singular_values: float32 [64], replicated, may hold values from 1 to 4
- basis: float32 [64, 3, 64, 16, 128], P(None, None, 'gx', 'gy'), may hold values from -60 to 60
- snapshots: float32 [15, 3, 64, 16, 128], P(None, None, 'gx', 'gy'), may hold values from -60 to 60
Outputs:
- populations_out: float32 [19, 128, 32, 256], P(None, 'gx', 'gy')
- upper_factor: float32 [80, 80], replicated
- new_basis: float32 [80, 3, 64, 16, 128], P(None, None, 'gx', 'gy')
Inputs may be any that keep to these rules, and one draw needn't show every extreme that they name: `populations`: each entry is w_i times a factor between 0.7 and 1.3.
All inputs are finite; a program needn't handle non-finite values. No bound on the sum of `solid_mask` on one device may be relied on, other than what follows from the above.
Results may differ from a plain program's by a relative error of at most 0.00012.
Values sent between devices are 32-bit elements; how exact they have to be, the bound alone decides.
No kernel may reach another device: no remote copies, remote signals or barrier semaphores. Data moves between devices by JAX's collectives and lax.ppermute only.
A program may use at most 128 MiB of HBM per device.

v0:
```python
import jax
import jax.numpy as jnp
from jax import lax
from jax.experimental import pallas as pl
from jax.experimental.pallas import tpu as pltpu
from jax.sharding import PartitionSpec as P

velocity_table = [
    (0, 0, 0),
    (1, 0, 0),
    (-1, 0, 0),
    (0, 1, 0),
    (0, -1, 0),
    (0, 0, 1),
    (0, 0, -1),
    (1, 1, 0),
    (-1, -1, 0),
    (1, -1, 0),
    (-1, 1, 0),
    (1, 0, 1),
    (-1, 0, -1),
    (1, 0, -1),
    (-1, 0, 1),
    (0, 1, 1),
    (0, -1, -1),
    (0, 1, -1),
    (0, -1, 1),
]
NVEL = 19
PAIRS = [(i, i + 1) for i in range(1, NVEL, 2)]
W_REST, W_FACE, W_EDGE = 1.0 / 3.0, 1.0 / 18.0, 1.0 / 36.0
UP_X = [i for i in range(NVEL) if velocity_table[i][0] == 1]
DOWN_X = [i for i in range(NVEL) if velocity_table[i][0] == -1]
UP_Y = [i for i in range(NVEL) if velocity_table[i][1] == 1]
DOWN_Y = [i for i in range(NVEL) if velocity_table[i][1] == -1]
SPEED_SCALE = 10.0
HIGHEST = lax.Precision.HIGHEST
F32 = jnp.float32
BF16 = jnp.bfloat16


def params(mib=40):
    return pltpu.CompilerParams(vmem_limit_bytes=mib << 20)


def shifted(value, axis, steps):
    count = lax.axis_size(axis)
    return lax.ppermute(value, axis, [(s, (s + steps) % count) for s in range(count)])


def moments(f):
    plus = [f[a] + f[b] for a, b in PAIRS]
    minus = [f[a] - f[b] for a, b in PAIRS]
    rho = f[0] + plus[0]
    for p in plus[1:]:
        rho = rho + p
    mx, my, mz, m7, m9, m11, m13, m15, m17 = minus
    jx = (mx + m7) + (m9 + m11) + m13
    jy = (my + m7) + (m15 + m17) - m9
    jz = (mz + m11) + (m15 - m13) - m17
    r = 1.0 / rho
    return rho, (jx * r, jy * r, jz * r)


def collide(f, omega, solid):
    rho, u = moments(f)
    base = 1.0 - 1.5 * (u[0] * u[0] + u[1] * u[1] + u[2] * u[2])
    keep = 1.0 - omega
    wr = omega * rho
    post = [None] * NVEL
    post[0] = jnp.where(solid, f[0], keep * f[0] + (W_REST * wr) * base)
    w_face, w_edge = W_FACE * wr, W_EDGE * wr
    for a, b in PAIRS:
        vel = velocity_table[a]
        along = None
        for axis in range(3):
            if vel[axis] == 1:
                along = u[axis] if along is None else along + u[axis]
            elif vel[axis] == -1:
                along = along - u[axis]
        w = w_face if a < 7 else w_edge
        even = w * (base + 4.5 * (along * along))
        odd = w * (3.0 * along)
        post[a] = jnp.where(solid, f[b], keep * f[a] + (even + odd))
        post[b] = jnp.where(solid, f[a], keep * f[b] + (even - odd))
    return post


def emit_post(post, x, nx, post_ref, xup_ref, xdn_ref, yup_ref, ydn_ref):
    ny = post_ref.shape[2]
    for i in range(NVEL):
        cz = velocity_table[i][2]
        value = post[i] if cz == 0 else pltpu.roll(post[i], cz % post[i].shape[1], 1)
        post_ref[i, x] = value
        cx = velocity_table[i][0]
        row = lax.rem(x + (cx + nx), nx)
        if i in UP_Y:
            yup_ref[pl.ds(UP_Y.index(i) * nx + row, 1), :] = value[ny - 1 : ny, :]
        if i in DOWN_Y:
            ydn_ref[pl.ds(DOWN_Y.index(i) * nx + row, 1), :] = value[0:1, :]


def emit_faces(nx, post_ref, xup_ref, xdn_ref):
    for k, i in enumerate(UP_X):
        xup_ref[k] = post_ref[i, nx - 1]
    for k, i in enumerate(DOWN_X):
        xdn_ref[k] = post_ref[i, 0]


def first_kernel(f_ref, om_ref, so_ref, post_ref, xup_ref, xdn_ref, yup_ref, ydn_ref):
    nx = f_ref.shape[1]

    def step(x, carry):
        post = collide([f_ref[i, x] for i in range(NVEL)], om_ref[x], so_ref[x] > 0)
        emit_post(post, x, nx, post_ref, xup_ref, xdn_ref, yup_ref, ydn_ref)
        return carry

    lax.fori_loop(0, nx, step, 0)
    emit_faces(nx, post_ref, xup_ref, xdn_ref)


def streamed(x, nx, post_ref, xup_ref, xdn_ref, yup_ref, ydn_ref):
    ny = post_ref.shape[2]
    row_id = lax.broadcasted_iota(jnp.int32, (ny, post_ref.shape[3]), 0)
    f = []
    for i in range(NVEL):
        cx, cy, _ = velocity_table[i]
        if cx == 1:
            value = jnp.where(x == 0, xup_ref[UP_X.index(i)], post_ref[i, lax.rem(x + nx - 1, nx)])
        elif cx == -1:
            value = jnp.where(
                x == nx - 1, xdn_ref[DOWN_X.index(i)], post_ref[i, lax.rem(x + 1, nx)]
            )
        else:
            value = post_ref[i, x]
        if cy == 1:
            edge = yup_ref[pl.ds(UP_Y.index(i) * nx + x, 1), :]
            value = jnp.where(row_id == 0, edge, pltpu.roll(value, 1, 0))
        elif cy == -1:
            edge = ydn_ref[pl.ds(DOWN_Y.index(i) * nx + x, 1), :]
            value = jnp.where(row_id == ny - 1, edge, pltpu.roll(value, ny - 1, 0))
        f.append(value)
    return f


def second_kernel(
    p_ref, xu_ref, xd_ref, yu_ref, yd_ref, om_ref, so_ref, post_ref, xup_ref, xdn_ref, yup_ref, ydn_ref
):
    nx = p_ref.shape[1]

    def step(x, carry):
        f = streamed(x, nx, p_ref, xu_ref, xd_ref, yu_ref, yd_ref)
        post = collide(f, om_ref[x], so_ref[x] > 0)
        emit_post(post, x, nx, post_ref, xup_ref, xdn_ref, yup_ref, ydn_ref)
        return carry

    lax.fori_loop(0, nx, step, 0)
    emit_faces(nx, post_ref, xup_ref, xdn_ref)


def pack_kernel(xu_ref, xd_ref, yup_ref, ydn_ref, ou_ref, od_ref):
    nx = yup_ref.shape[0] // len(UP_Y)
    ny = xu_ref.shape[1]
    ou_ref[...] = yup_ref[...]
    od_ref[...] = ydn_ref[...]
    for ids, out, row in ((UP_Y, ou_ref, ny - 1), (DOWN_Y, od_ref, 0)):
        for k, i in enumerate(ids):
            if velocity_table[i][0] == 1:
                out[k * nx : k * nx + 1, :] = xu_ref[UP_X.index(i), row : row + 1, :]
            elif velocity_table[i][0] == -1:
                at = k * nx + nx - 1
                out[at : at + 1, :] = xd_ref[DOWN_X.index(i), row : row + 1, :]


def gram_kernel(s_ref, basis_ref, snap_ref, a_ref, h_ref, g_ref):
    rank = basis_ref.shape[0]
    depth = basis_ref.shape[1]
    extra = snap_ref.shape[0]
    cols = a_ref.shape[1]
    basis = basis_ref.reshape(rank * depth, 128)
    snaps = snap_ref.reshape(extra * depth, 128)
    scale = jnp.broadcast_to(s_ref[...], (rank, 128))
    zero = jnp.zeros((cols - rank - extra, 128), F32)

    def step(q, acc):
        for t in range(2):
            r = 2 * q + t
            a_ref[r, 0:rank, :] = basis[pl.ds(r, rank, stride=depth), :] * scale
            a_ref[r, rank : rank + extra, :] = snaps[pl.ds(r, extra, stride=depth), :]
            a_ref[r, rank + extra : cols, :] = zero
        rows = jnp.concatenate([a_ref[2 * q], a_ref[2 * q + 1]], axis=1)
        high = rows.astype(BF16)
        low = (rows - high.astype(F32)).astype(BF16)
        both = jnp.concatenate([high, low], axis=0)
        h_ref[q] = both
        return acc + lax.dot_general(
            both, high, (((1,), (1,)), ((), ())), preferred_element_type=F32
        )

    acc = lax.fori_loop(0, depth // 2, step, jnp.zeros((2 * cols, cols), F32))
    cross = acc[cols:, :]
    eye = (
        lax.broadcasted_iota(jnp.int32, (cols, cols), 0)
        == lax.broadcasted_iota(jnp.int32, (cols, cols), 1)
    ).astype(F32)
    flipped = lax.dot_general(
        eye, cross, (((1,), (1,)), ((), ())), precision=HIGHEST, preferred_element_type=F32
    )
    g_ref[...] = acc[:cols, :] + cross + flipped


def factor_kernel(inv_rows, g_ref, u_ref, li_ref, w_ref):
    cols = g_ref.shape[0]
    known = cols - 1
    row_id = lax.broadcasted_iota(jnp.int32, (cols, cols), 0)
    col_id = lax.broadcasted_iota(jnp.int32, (cols, cols), 1)
    left = g_ref[...] * inv_rows
    right = (row_id == col_id).astype(F32)
    down = lax.broadcasted_iota(jnp.int32, (cols, 1), 0)
    for j in range(known):
        column = left[:, j : j + 1]
        pivot = lax.rsqrt(left[j : j + 1, j : j + 1])
        scaled = column * pivot
        step = jnp.where(down > j, scaled, 0.0)
        top = left[j : j + 1, :] * pivot
        aug = right[j : j + 1, :] * pivot
        here = down == j
        left = jnp.where(here, top, left - step * top)
        right = jnp.where(here, aug, right - step * aug)
    keep = jnp.logical_and(row_id <= col_id, col_id < known)
    u_ref[...] = jnp.where(keep, left, 0.0)
    inverse = jnp.where(jnp.logical_and(row_id >= col_id, row_id < known), right, 0.0)
    li_ref[...] = inverse
    high = inverse.astype(BF16)
    w_ref[0] = high
    w_ref[1] = (inverse - high.astype(F32)).astype(BF16)


def rotate_kernel(w_ref, h_ref, o_ref):
    cols = w_ref.shape[1]
    depth = o_ref.shape[1]
    out = o_ref.reshape(cols * depth, 128)
    whigh, wlow = w_ref[0], w_ref[1]

    def step(q, carry):
        high = h_ref[q, 0:cols, :]
        low = h_ref[q, cols:, :]
        dims = (((1,), (0,)), ((), ()))
        res = lax.dot_general(whigh, high, dims, preferred_element_type=F32)
        res = res + lax.dot_general(wlow, high, dims, preferred_element_type=F32)
        res = res + lax.dot_general(whigh, low, dims, preferred_element_type=F32)
        out[pl.ds(2 * q, cols, stride=depth), :] = res[:, :128]
        out[pl.ds(2 * q + 1, cols, stride=depth), :] = res[:, 128:]
        return carry

    lax.fori_loop(0, depth // 2, step, 0)


def final_kernel(
    p_ref, xu_ref, xd_ref, yu_ref, yd_ref, so_ref, a_ref, f_ref, c_ref, v_ref, vel_ref
):
    nx, ny, nz = p_ref.shape[1:]
    nxc, nyc = nx // 2, ny // 2

    def step(xc, carry):
        total = [None] * 3
        for t in range(2):
            x = 2 * xc + t
            f = streamed(x, nx, p_ref, xu_ref, xd_ref, yu_ref, yd_ref)
            for i in range(NVEL):
                f_ref[i, x] = f[i]
            _, u = moments(f)
            fluid = (so_ref[x] == 0).astype(F32)
            for k in range(3):
                part = u[k] * fluid
                total[k] = part if t == 0 else total[k] + part
        for k in range(3):
            at = pl.multiple_of((k * nxc + xc) * ny, ny)
            for t in range(nz // 128):
                vel_ref[t, pl.ds(at, ny), :] = total[k][:, t * 128 : (t + 1) * 128]
        return carry

    lax.fori_loop(0, nxc, step, 0)
    depth = 3 * nxc * nyc
    pairs = []
    for t in range(nz // 128):
        half = vel_ref.at[t]
        pairs.append(half[pl.ds(0, depth, stride=2), :] + half[pl.ds(1, depth, stride=2), :])
    pairs = jnp.concatenate(pairs, axis=1)
    pick = (
        lax.broadcasted_iota(jnp.int32, (nz, nz // 2), 0) // 2
        == lax.broadcasted_iota(jnp.int32, (nz, nz // 2), 1)
    ).astype(F32)
    coarse = lax.dot_general(
        pairs, pick, (((1,), (0,)), ((), ())), precision=HIGHEST, preferred_element_type=F32
    )
    c_ref[...] = coarse * (SPEED_SCALE / 8.0)
    cols = a_ref.shape[1]

    def inner(r, acc):
        return acc + a_ref[r] * c_ref[pl.ds(r, 1), :]

    acc = lax.fori_loop(0, depth, inner, jnp.zeros((cols, 128), F32))
    dots = jnp.sum(acc, axis=1, keepdims=True)
    own = jnp.sum(c_ref[...] * c_ref[...])
    down = lax.broadcasted_iota(jnp.int32, (cols, 1), 0)
    dots = jnp.where(down == cols - 1, own, dots)
    across = lax.broadcasted_iota(jnp.int32, (cols, 128), 1)
    diag = jnp.where(across == lax.broadcasted_iota(jnp.int32, (cols, 128), 0), dots, 0.0)
    line = jnp.sum(diag, axis=0, keepdims=True)
    v_ref[...] = jnp.broadcast_to(line, v_ref.shape)


def last_kernel(inv_rows, v_ref, li_ref, u_ref, a_ref, c_ref, q_ref, uo_ref, o_ref, row_ref, sem):
    cols = li_ref.shape[0]
    known = cols - 1
    depth = c_ref.shape[0]
    line = jnp.sum(v_ref[...], axis=0, keepdims=True)[:, :cols] * inv_rows
    across = lax.broadcasted_iota(jnp.int32, (1, cols), 1)
    norm = jnp.sum(jnp.where(across == known, line, 0.0), axis=1, keepdims=True)
    inverse = li_ref[...]
    coef = jnp.sum(inverse * jnp.where(across == known, 0.0, line), axis=1, keepdims=True)
    pivot = lax.rsqrt(norm - jnp.sum(coef * coef, axis=0, keepdims=True))
    left = norm - jnp.sum(coef * coef, axis=0, keepdims=True)
    col_id = lax.broadcasted_iota(jnp.int32, (cols, cols), 1)
    row_id = lax.broadcasted_iota(jnp.int32, (cols, cols), 0)
    edge = jnp.where(row_id == known, left * pivot, coef)
    uo_ref[...] = jnp.where(col_id == known, edge, u_ref[...])
    weight = jnp.sum(inverse * coef, axis=0, keepdims=True) * (-pivot)
    diag = jnp.where(row_id == col_id, weight, 0.0)
    tall = jnp.sum(diag, axis=1, keepdims=True)
    tall = jnp.broadcast_to(tall, (cols, 128))

    def step(r, carry):
        part = jnp.sum(a_ref[r] * tall, axis=0, keepdims=True)
        row_ref[pl.ds(r, 1), :] = part + c_ref[pl.ds(r, 1), :] * pivot
        return carry

    lax.fori_loop(0, depth, step, 0)
    copy = pltpu.make_async_copy(row_ref, o_ref.at[known], sem)
    copy.start()
    copy.wait()


def shape(dims, dtype=F32):
    return jax.ShapeDtypeStruct(dims, dtype)


def halo_x(xup, xdn):
    return shifted(xup, "gx", 1), shifted(xdn, "gx", -1)


def halo_y(xu, xd, yup, ydn):
    send_up, send_dn = pl.pallas_call(
        pack_kernel, out_shape=(shape(yup.shape), shape(ydn.shape)), name="pack", compiler_params=params(8)
    )(xu, xd, yup, ydn)
    return shifted(send_up, "gy", 1), shifted(send_dn, "gy", -1)


def sum_everywhere(value):
    for axis in ("gy", "gx"):
        count = lax.axis_size(axis)
        bit = 1
        while bit < count:
            value = value + lax.ppermute(value, axis, [(s, s ^ bit) for s in range(count)])
            bit *= 2
    return value


def on_device(populations, relax_rate, solid_mask, singular_values, basis, snapshots):
    _, nx, ny, nz = populations.shape
    rank, extra = basis.shape[0], snapshots.shape[0]
    cols = rank + extra + 1
    tail = basis.shape[1:]
    depth = tail[0] * tail[1] * tail[2]
    n_dev = lax.axis_size("gx") * lax.axis_size("gy")
    inv_rows = 1.0 / (depth * tail[3] * n_dev)
    edges = len(UP_Y) * nx
    post_shapes = (
        shape((NVEL, nx, ny, nz)),
        shape((len(UP_X), ny, nz)),
        shape((len(DOWN_X), ny, nz)),
        shape((edges, nz)),
        shape((edges, nz)),
    )
    post, xup, xdn, yup, ydn = pl.pallas_call(
        first_kernel, out_shape=post_shapes, name="first", compiler_params=params(16)
    )(populations, relax_rate, solid_mask)
    xu, xd = halo_x(xup, xdn)
    rows, halves, gram = pl.pallas_call(
        gram_kernel,
        out_shape=(
            shape((depth, cols, 128)),
            shape((depth // 2, 2 * cols, 256), BF16),
            shape((cols, cols)),
        ),
        name="gram",
        compiler_params=params(24),
    )(
        singular_values.reshape(rank, 1),
        basis.reshape(rank, depth, 128),
        snapshots.reshape(extra, depth, 128),
    )
    yu, yd = halo_y(xu, xd, yup, ydn)
    gram = sum_everywhere(gram)
    post, xup, xdn, yup, ydn = pl.pallas_call(
        second_kernel, out_shape=post_shapes, name="second", compiler_params=params(16)
    )(post, xu, xd, yu, yd, relax_rate, solid_mask)
    xu, xd = halo_x(xup, xdn)
    upper, inverse, split = pl.pallas_call(
        lambda *refs: factor_kernel(inv_rows, *refs),
        out_shape=(shape((cols, cols)), shape((cols, cols)), shape((2, cols, cols), BF16)),
        name="factor",
        compiler_params=params(8),
    )(gram)
    yu, yd = halo_y(xu, xd, yup, ydn)
    rotated = pl.pallas_call(
        rotate_kernel, out_shape=shape((cols, depth, 128)), name="rotate", compiler_params=params(16)
    )(split, halves)
    field, coarse, line = pl.pallas_call(
        final_kernel,
        out_shape=(shape((NVEL, nx, ny, nz)), shape((depth, 128)), shape((n_dev, 128))),
        scratch_shapes=[pltpu.VMEM((nz // 128, 3 * (nx // 2) * ny, 128), F32)],
        name="final",
        compiler_params=params(24),
    )(post, xu, xd, yu, yd, solid_mask, rows)
    lines = lax.all_to_all(line, ("gx", "gy"), 0, 0, tiled=True)
    vmem = pl.BlockSpec(memory_space=pltpu.VMEM)
    hbm = pl.BlockSpec(memory_space=pl.ANY)
    upper, rotated = pl.pallas_call(
        lambda *refs: last_kernel(inv_rows, *refs),
        out_shape=(shape((cols, cols)), shape((cols, depth, 128))),
        in_specs=[vmem] * 5 + [hbm],
        out_specs=(vmem, hbm),
        scratch_shapes=[pltpu.VMEM((depth, 128), F32), pltpu.SemaphoreType.DMA],
        input_output_aliases={5: 1},
        name="last",
        compiler_params=params(16),
    )(lines, inverse, upper, rows, coarse, rotated)
    return field, upper, rotated.reshape((cols,) + tail)


def solution(mesh):
    return jax.shard_map(
        on_device,
        mesh=mesh,
        in_specs=(
            P(None, "gx", "gy", None),
            P("gx", "gy", None),
            P("gx", "gy", None),
            P(),
            P(None, None, "gx", "gy", None),
            P(None, None, "gx", "gy", None),
        ),
        out_specs=(P(None, "gx", "gy", None), P(), P(None, None, "gx", "gy", None)),
        check_vma=False,
    )
```

profile of v0, /device:TPU:0, one launch (start us, length us, event | category | flops | bytes accessed | tf_op | source)
XLA Modules:
  0.0 92.0 jit_solution(15725580853427991056)
XLA Ops:
  0.6 1.7 %copy-done.7 = f32[19,16,8,256]{3,2,1,0:T(8,128)S(1)} copy-done((f32[19,16,8,256]{3,2,1,0:T(8,128)S(1)}, f32[19,16,8,256]{3,2,1,0:T(8,128)}, u32[]{:S(2)}) %copy-start.7) | copy-done | bytes 2490392
  2.3 0.9 copy-done.8
  3.2 0.9 copy-done.12
  4.1 2.2 %first.1 = (f32[19,16,8,256]{3,2,1,0:T(8,128)S(1)}, f32[5,8,256]{2,1,0:T(8,128)S(1)}, f32[5,8,256]{2,1,0:T(8,128)S(1)}, f32[80,256]{1,0:T(8,128)S(1)}, f32[80,256]{1,0:T(8,128)S(1)}) custom-call(f32[19,16,8,256]{3,2,1,0:T(8,128)S(1)} %copy-done.7, f32[16,8,256]{2,1,0:T(8,128)S(1)} %copy-done.12, s32[16,8,256]{2,1,0:T(8,128)S(1)} %copy-done.8), custom_call_target="tpu_custom_call" | custom-call | tf_op jit(solution)/shard_map/first/pallas_call | solution.py:386
  6.4 0.5 collective-permute-start
  6.9 4.1 %collective-permute-start.1 = (f32[5,8,256]{2,1,0:T(8,128)S(1)}, f32[5,8,256]{2,1,0:T(8,128)S(1)}, u32[]{:S(2)}, u32[]{:S(2)}) collective-permute-start(f32[5,8,256]{2,1,0:T(8,128)S(1)} %get-tuple-element.30), channel_id=1, source_target_pairs={{0,28},{4,0},{8,4},{12,8},{16,12},{20,16},{24,20},{28,24},{1,29},{... | collective-permute-start | bytes 122888 | tf_op jit(solution)/shard_map/ppermute | solution.py:48
  11.0 1.6 %collective-permute-done.xu_ref = f32[5,8,256]{2,1,0:T(8,128)S(1)} collective-permute-done((f32[5,8,256]{2,1,0:T(8,128)S(1)}, f32[5,8,256]{2,1,0:T(8,128)S(1)}, u32[]{:S(2)}, u32[]{:S(2)}) %collective-permute-start) | collective-permute-done | bytes 40992 | tf_op jit(solution)/shard_map/ppermute | solution.py:48
  12.6 0.1 collective-permute-done.1.xd_ref
  12.7 2.0 %collective-permute-start.2 = (f32[80,256]{1,0:T(8,128)S(1)}, f32[80,256]{1,0:T(8,128)S(1)}, u32[]{:S(2)}, u32[]{:S(2)}) collective-permute-start(f32[80,256]{1,0:T(8,128)S(1)} %get-tuple-element.33), channel_id=1, source_target_pairs={{0,1},{1,2},{2,3},{3,0},{4,5},{5,6},{6,7},{7,4},{8,9},{9,10},{10,1... | collective-permute-start | bytes 245768 | tf_op jit(solution)/shard_map/ppermute | solution.py:48
  14.7 1.0 %collective-permute-start.3 = (f32[80,256]{1,0:T(8,128)S(1)}, f32[80,256]{1,0:T(8,128)S(1)}, u32[]{:S(2)}, u32[]{:S(2)}) collective-permute-start(f32[80,256]{1,0:T(8,128)S(1)} %get-tuple-element.34), channel_id=1, source_target_pairs={{0,3},{1,0},{2,1},{3,2},{4,7},{5,4},{6,5},{7,6},{8,11},{9,8},{10,9... | collective-permute-start | bytes 245768 | tf_op jit(solution)/shard_map/ppermute | solution.py:48
  15.8 3.0 %collective-permute-done.2.yu_ref = f32[80,256]{1,0:T(8,128)S(1)} collective-permute-done((f32[80,256]{1,0:T(8,128)S(1)}, f32[80,256]{1,0:T(8,128)S(1)}, u32[]{:S(2)}, u32[]{:S(2)}) %collective-permute-start.2) | collective-permute-done | bytes 81952 | tf_op jit(solution)/shard_map/ppermute | solution.py:48
  18.8 1.7 %collective-permute-done.3.yd_ref = f32[80,256]{1,0:T(8,128)S(1)} collective-permute-done((f32[80,256]{1,0:T(8,128)S(1)}, f32[80,256]{1,0:T(8,128)S(1)}, u32[]{:S(2)}, u32[]{:S(2)}) %collective-permute-start.3) | collective-permute-done | bytes 81952 | tf_op jit(solution)/shard_map/ppermute | solution.py:48
  20.5 0.9 copy-done.9
  21.4 3.1 %second.1 = (f32[19,16,8,256]{3,2,1,0:T(8,128)S(1)}, f32[5,8,256]{2,1,0:T(8,128)}, f32[5,8,256]{2,1,0:T(8,128)}, f32[80,256]{1,0:T(8,128)S(1)}, f32[80,256]{1,0:T(8,128)S(1)}) custom-call(f32[19,16,8,256]{3,2,1,0:T(8,128)S(1)} %get-tuple-element.28.p_ref, f32[5,8,256]{2,1,0:T(8,128)S(1)} %collective-permute-done.xu_ref, ...), custom_call_target="tpu_custom_call" | custom-call | tf_op jit(solution)/shard_map/second/pallas_call | solution.py:406
  24.5 1.4 %copy-done.5 = f32[19,16,8,256]{3,2,1,0:T(8,128)} copy-done((f32[19,16,8,256]{3,2,1,0:T(8,128)}, f32[19,16,8,256]{3,2,1,0:T(8,128)S(1)}, u32[]{:S(2)}) %copy-start.5) | copy-done | bytes 2490392
  25.9 0.0 collective-permute-start.4
  25.9 3.5 %collective-permute-start.5 = (f32[5,8,256]{2,1,0:T(8,128)}, f32[5,8,256]{2,1,0:T(8,128)S(1)}, u32[]{:S(2)}, u32[]{:S(2)}) collective-permute-start(f32[5,8,256]{2,1,0:T(8,128)} %get-tuple-element.37), channel_id=1, source_target_pairs={{0,28},{4,0},{8,4},{12,8},{16,12},{20,16},{24,20},{28,24},{1,29},{... | collective-permute-start | bytes 122888 | tf_op jit(solution)/shard_map/ppermute | solution.py:48
  29.5 0.7 copy.11.s_ref
  30.2 0.0 copy-start.11
  30.3 1.3 %copy-done.11 = f32[15,3,8,4,128]{4,3,2,1,0:T(4,128)S(1)} copy-done((f32[15,3,8,4,128]{4,3,2,1,0:T(4,128)S(1)}, f32[15,3,8,4,128]{4,3,2,1,0:T(4,128)}, u32[]{:S(2)}) %copy-start.11) | copy-done | bytes 737304
  31.5 10.3 %gram.1 = (f32[96,80,128]{2,1,0:T(8,128)S(1)}, bf16[48,160,256]{2,1,0:T(8,128)(2,1)S(1)}, f32[80,80]{1,0:T(8,128)S(1)}) custom-call(f32[64,1]{1,0:T(8,128)S(1)} %copy.11.s_ref, f32[64,96,128]{2,1,0:T(8,128)S(1)} %bitcast.8, f32[15,96,128]{2,1,0:T(8,128)S(1)} %bitcast.9), custom_call_target="tpu_custom_call" | custom-call | tf_op jit(solution)/shard_map/gram/pallas_call | solution.py:390
  41.8 0.0 copy-start.2
  41.8 1.9 %copy-done.2 = bf16[48,160,256]{2,1,0:T(8,128)(2,1)} copy-done((bf16[48,160,256]{2,1,0:T(8,128)(2,1)}, bf16[48,160,256]{2,1,0:T(8,128)(2,1)S(1)}, u32[]{:S(2)}) %copy-start.2) | copy-done | bytes 3932184
  43.7 1.5 %collective-permute-start.8 = (f32[80,80]{1,0:T(8,128)S(1)}, f32[80,80]{1,0:T(8,128)S(1)}, u32[]{:S(2)}, u32[]{:S(2)}) collective-permute-start(f32[80,80]{1,0:T(8,128)S(1)} %get-tuple-element.45), channel_id=1, source_target_pairs={{0,1},{1,0},{2,3},{3,2},{4,5},{5,4},{6,7},{7,6},{8,9},{9,8},{10,11... | collective-permute-start | bytes 76808 | tf_op jit(solution)/shard_map/ppermute | solution.py:365
  45.2 0.0 collective-permute-done.4.xu_ref
  45.2 0.0 collective-permute-done.5.xd_ref
  45.2 0.6 collective-permute-start.6
  45.8 2.4 %collective-permute-start.7 = (f32[80,256]{1,0:T(8,128)S(1)}, f32[80,256]{1,0:T(8,128)S(1)}, u32[]{:S(2)}, u32[]{:S(2)}) collective-permute-start(f32[80,256]{1,0:T(8,128)S(1)} %get-tuple-element.41), channel_id=1, source_target_pairs={{0,3},{1,0},{2,1},{3,2},{4,7},{5,4},{6,5},{7,6},{8,11},{9,8},{10,9... | collective-permute-start | bytes 245768 | tf_op jit(solution)/shard_map/ppermute | solution.py:48
  48.2 0.0 collective-permute-done.8
  48.2 0.6 collective-permute-start.9
  48.8 3.5 %collective-permute-done.9 = f32[80,80]{1,0:T(8,128)S(1)} collective-permute-done((f32[80,80]{1,0:T(8,128)S(1)}, f32[80,80]{1,0:T(8,128)S(1)}, u32[]{:S(2)}, u32[]{:S(2)}) %collective-permute-start.9) | collective-permute-done | bytes 25632 | tf_op jit(solution)/shard_map/ppermute | solution.py:365
  52.3 0.0 collective-permute-start.10
  52.3 1.2 %collective-permute-done.10 = f32[80,80]{1,0:T(8,128)S(1)} collective-permute-done((f32[80,80]{1,0:T(8,128)S(1)}, f32[80,80]{1,0:T(8,128)S(1)}, u32[]{:S(2)}, u32[]{:S(2)}) %collective-permute-start.10) | collective-permute-done | bytes 25632 | tf_op jit(solution)/shard_map/ppermute | solution.py:365
  53.5 0.0 collective-permute-start.11
  53.5 0.0 collective-permute-done.6.yu_ref
  53.5 0.0 collective-permute-done.7.yd_ref
  53.6 3.0 %final.1 = (f32[19,16,8,256]{3,2,1,0:T(8,128)}, f32[96,128]{1,0:T(8,128)S(1)}, f32[32,128]{1,0:T(8,128)}) custom-call(f32[19,16,8,256]{3,2,1,0:T(8,128)S(1)} %copy-done.6, f32[5,8,256]{2,1,0:T(8,128)S(1)} %collective-permute-done.4.xu_ref, f32[5,8,256]{2,1,0:T(8,128)S(1)} %collective-permute-done.5.xd_ref, f32[80,256]{1,0:T(8,128)S(1)} %collective-permute-done.6.yu_ref, ...), custom_call_target="tpu_custom_call" | custom-call | tf_op jit(solution)/shard_map/final/pallas_call | solution.py:420
  56.6 3.5 %all-to-all-start = ((f32[32,1,128]{2,1,0:T(1,128)}), f32[32,1,128]{2,1,0:T(1,128)S(1)}, u32[]{:S(2)}, u32[]{:S(2)}) async-start(f32[32,1,128]{2,1,0:T(1,128)} %bitcast.4), calls=%async_computation | async-start | bytes 32768 | tf_op jit(solution)/shard_map/all_to_all | solution.py:427
  60.1 0.0 collective-permute-done.11
  60.1 2.7 %collective-permute-start.12 = (f32[80,80]{1,0:T(8,128)S(1)}, f32[80,80]{1,0:T(8,128)S(1)}, u32[]{:S(2)}, u32[]{:S(2)}) collective-permute-start(f32[80,80]{1,0:T(8,128)S(1)} %add.18), channel_id=1, source_target_pairs={{0,16},{4,20},{8,24},{12,28},{16,0},{20,4},{24,8},{28,12},{1,17},{... | collective-permute-start | bytes 76808 | tf_op jit(solution)/shard_map/ppermute | solution.py:365
  62.9 2.8 %collective-permute-done.12 = f32[80,80]{1,0:T(8,128)S(1)} collective-permute-done((f32[80,80]{1,0:T(8,128)S(1)}, f32[80,80]{1,0:T(8,128)S(1)}, u32[]{:S(2)}, u32[]{:S(2)}) %collective-permute-start.12) | collective-permute-done | bytes 25632 | tf_op jit(solution)/shard_map/ppermute | solution.py:365
  65.7 6.6 %factor.1 = (f32[80,80]{1,0:T(8,128)S(1)}, f32[80,80]{1,0:T(8,128)S(1)}, bf16[2,80,80]{2,1,0:T(8,128)(2,1)S(1)}) custom-call(f32[80,80]{1,0:T(8,128)S(1)} %add.19.refs_0_), custom_call_target="tpu_custom_call" | custom-call | tf_op jit(solution)/shard_map/factor/pallas_call | solution.py:410
  72.4 0.0 copy-start.3
  72.4 2.1 %copy-done.3 = bf16[48,160,256]{2,1,0:T(8,128)(2,1)S(1)} copy-done((bf16[48,160,256]{2,1,0:T(8,128)(2,1)S(1)}, bf16[48,160,256]{2,1,0:T(8,128)(2,1)}, u32[]{:S(2)}) %copy-start.3) | copy-done | bytes 3932184
  74.5 12.0 %rotate.1.refs_5_ = f32[80,96,128]{2,1,0:T(8,128)} custom-call(bf16[2,80,80]{2,1,0:T(8,128)(2,1)S(1)} %get-tuple-element.49.w_ref, bf16[48,160,256]{2,1,0:T(8,128)(2,1)S(1)} %copy-done.3), custom_call_target="tpu_custom_call" | custom-call | tf_op jit(solution)/shard_map/rotate/pallas_call | solution.py:417
  86.5 0.0 all-to-all-done
  86.5 2.1 %copy-done.1 = f32[96,80,128]{2,1,0:T(8,128)S(1)} copy-done((f32[96,80,128]{2,1,0:T(8,128)S(1)}, f32[96,80,128]{2,1,0:T(8,128)}, u32[]{:S(2)}) %copy-start.1) | copy-done | bytes 3932184
  88.6 3.4 %last.1 = (f32[80,80]{1,0:T(8,128)}, f32[80,96,128]{2,1,0:T(8,128)}) custom-call(f32[32,128]{1,0:T(8,128)S(1)} %bitcast.10, f32[80,80]{1,0:T(8,128)S(1)} %get-tuple-element.46.refs_1_, f32[80,80]{1,0:T(8,128)S(1)} %get-tuple-element.47.refs_2_, f32[96,80,128]{2,1,0:T(8,128)S(1)} %copy-done.1, ...), custom_call_target="tpu_custom_call", output_to_operand_aliasing={{1}: (5, {})} | custom-call | tf_op jit(solution)/shard_map/last/pallas_call | solution.py:430
  (21 shorter events, 0.1 us)
Async XLA Ops:
  0.6 1.7 %copy-start.7 = (f32[19,16,8,256]{3,2,1,0:T(8,128)S(1)}, f32[19,16,8,256]{3,2,1,0:T(8,128)}, u32[]{:S(2)}) copy-start(f32[19,16,8,256]{3,2,1,0:T(8,128)} %f_ref.1) | copy-start | bytes 7471108
  2.3 0.9 copy-start.8
  3.2 0.9 copy-start.12
  4.1 26.1 %copy-start.4 = (f32[64,3,8,4,128]{4,3,2,1,0:T(4,128)S(1)}, f32[64,3,8,4,128]{4,3,2,1,0:T(4,128)}, u32[]{:S(2)}) copy-start(f32[64,3,8,4,128]{4,3,2,1,0:T(4,128)} %param.10) | copy-start | bytes 9437188
  6.4 6.3 %collective-permute-start = (f32[5,8,256]{2,1,0:T(8,128)S(1)}, f32[5,8,256]{2,1,0:T(8,128)S(1)}, u32[]{:S(2)}, u32[]{:S(2)}) collective-permute-start(f32[5,8,256]{2,1,0:T(8,128)S(1)} %get-tuple-element.29), channel_id=1, source_target_pairs={{0,4},{4,8},{8,12},{12,16},{16,20},{20,24},{24,28},{28,0},{1,5},{5... | collective-permute-start | bytes 122888 | tf_op jit(solution)/shard_map/ppermute | solution.py:48
  6.9 5.8 %collective-permute-start.1 = (f32[5,8,256]{2,1,0:T(8,128)S(1)}, f32[5,8,256]{2,1,0:T(8,128)S(1)}, u32[]{:S(2)}, u32[]{:S(2)}) collective-permute-start(f32[5,8,256]{2,1,0:T(8,128)S(1)} %get-tuple-element.30), channel_id=1, source_target_pairs={{0,28},{4,0},{8,4},{12,8},{16,12},{20,16},{24,20},{28,24},{1,29},{... | collective-permute-start | bytes 122888 | tf_op jit(solution)/shard_map/ppermute | solution.py:48
  12.7 6.1 %collective-permute-start.2 = (f32[80,256]{1,0:T(8,128)S(1)}, f32[80,256]{1,0:T(8,128)S(1)}, u32[]{:S(2)}, u32[]{:S(2)}) collective-permute-start(f32[80,256]{1,0:T(8,128)S(1)} %get-tuple-element.33), channel_id=1, source_target_pairs={{0,1},{1,2},{2,3},{3,0},{4,5},{5,6},{6,7},{7,4},{8,9},{9,10},{10,1... | collective-permute-start | bytes 245768 | tf_op jit(solution)/shard_map/ppermute | solution.py:48
  14.7 5.8 %collective-permute-start.3 = (f32[80,256]{1,0:T(8,128)S(1)}, f32[80,256]{1,0:T(8,128)S(1)}, u32[]{:S(2)}, u32[]{:S(2)}) collective-permute-start(f32[80,256]{1,0:T(8,128)S(1)} %get-tuple-element.34), channel_id=1, source_target_pairs={{0,3},{1,0},{2,1},{3,2},{4,7},{5,4},{6,5},{7,6},{8,11},{9,8},{10,9... | collective-permute-start | bytes 245768 | tf_op jit(solution)/shard_map/ppermute | solution.py:48
  20.5 0.9 copy-start.9
  21.4 32.1 %copy-start.10 = (s32[16,8,256]{2,1,0:T(8,128)S(1)}, s32[16,8,256]{2,1,0:T(8,128)}, u32[]{:S(2)}) copy-start(s32[16,8,256]{2,1,0:T(8,128)} %so_ref.5) | copy-start | bytes 393220
  24.5 1.4 %copy-start.5 = (f32[19,16,8,256]{3,2,1,0:T(8,128)}, f32[19,16,8,256]{3,2,1,0:T(8,128)S(1)}, u32[]{:S(2)}) copy-start(f32[19,16,8,256]{3,2,1,0:T(8,128)S(1)} %get-tuple-element.35.p_ref) | copy-start | bytes 7471108
  25.9 19.3 %collective-permute-start.4 = (f32[5,8,256]{2,1,0:T(8,128)}, f32[5,8,256]{2,1,0:T(8,128)S(1)}, u32[]{:S(2)}, u32[]{:S(2)}) collective-permute-start(f32[5,8,256]{2,1,0:T(8,128)} %get-tuple-element.36), channel_id=1, source_target_pairs={{0,4},{4,8},{8,12},{12,16},{16,20},{20,24},{24,28},{28,0},{1,5},{5... | collective-permute-start | bytes 122888 | tf_op jit(solution)/shard_map/ppermute | solution.py:48
  25.9 19.3 %collective-permute-start.5 = (f32[5,8,256]{2,1,0:T(8,128)}, f32[5,8,256]{2,1,0:T(8,128)S(1)}, u32[]{:S(2)}, u32[]{:S(2)}) collective-permute-start(f32[5,8,256]{2,1,0:T(8,128)} %get-tuple-element.37), channel_id=1, source_target_pairs={{0,28},{4,0},{8,4},{12,8},{16,12},{20,16},{24,20},{28,24},{1,29},{... | collective-permute-start | bytes 122888 | tf_op jit(solution)/shard_map/ppermute | solution.py:48
  30.2 23.3 %copy-start.6 = (f32[19,16,8,256]{3,2,1,0:T(8,128)S(1)}, f32[19,16,8,256]{3,2,1,0:T(8,128)}, u32[]{:S(2)}) copy-start(f32[19,16,8,256]{3,2,1,0:T(8,128)} %copy-done.5) | copy-start | bytes 7471108
  30.2 1.3 %copy-start.11 = (f32[15,3,8,4,128]{4,3,2,1,0:T(4,128)S(1)}, f32[15,3,8,4,128]{4,3,2,1,0:T(4,128)}, u32[]{:S(2)}) copy-start(f32[15,3,8,4,128]{4,3,2,1,0:T(4,128)} %param.11) | copy-start | bytes 2211844
  41.8 1.9 %copy-start.2 = (bf16[48,160,256]{2,1,0:T(8,128)(2,1)}, bf16[48,160,256]{2,1,0:T(8,128)(2,1)S(1)}, u32[]{:S(2)}) copy-start(bf16[48,160,256]{2,1,0:T(8,128)(2,1)S(1)} %get-tuple-element.50.h_ref) | copy-start | bytes 11796484
  43.7 12.9 %copy-start = (f32[96,80,128]{2,1,0:T(8,128)}, f32[96,80,128]{2,1,0:T(8,128)S(1)}, u32[]{:S(2)}) copy-start(f32[96,80,128]{2,1,0:T(8,128)S(1)} %get-tuple-element.42.a_ref.refs_3_) | copy-start | bytes 11796484
  43.7 4.5 %collective-permute-start.8 = (f32[80,80]{1,0:T(8,128)S(1)}, f32[80,80]{1,0:T(8,128)S(1)}, u32[]{:S(2)}, u32[]{:S(2)}) collective-permute-start(f32[80,80]{1,0:T(8,128)S(1)} %get-tuple-element.45), channel_id=1, source_target_pairs={{0,1},{1,0},{2,3},{3,2},{4,5},{5,4},{6,7},{7,6},{8,9},{9,8},{10,11... | collective-permute-start | bytes 76808 | tf_op jit(solution)/shard_map/ppermute | solution.py:365
  45.2 8.3 %collective-permute-start.6 = (f32[80,256]{1,0:T(8,128)S(1)}, f32[80,256]{1,0:T(8,128)S(1)}, u32[]{:S(2)}, u32[]{:S(2)}) collective-permute-start(f32[80,256]{1,0:T(8,128)S(1)} %get-tuple-element.40), channel_id=1, source_target_pairs={{0,1},{1,2},{2,3},{3,0},{4,5},{5,6},{6,7},{7,4},{8,9},{9,10},{10,1... | collective-permute-start | bytes 245768 | tf_op jit(solution)/shard_map/ppermute | solution.py:48
  45.8 7.7 %collective-permute-start.7 = (f32[80,256]{1,0:T(8,128)S(1)}, f32[80,256]{1,0:T(8,128)S(1)}, u32[]{:S(2)}, u32[]{:S(2)}) collective-permute-start(f32[80,256]{1,0:T(8,128)S(1)} %get-tuple-element.41), channel_id=1, source_target_pairs={{0,3},{1,0},{2,1},{3,2},{4,7},{5,4},{6,5},{7,6},{8,11},{9,8},{10,9... | collective-permute-start | bytes 245768 | tf_op jit(solution)/shard_map/ppermute | solution.py:48
  48.2 4.1 %collective-permute-start.9 = (f32[80,80]{1,0:T(8,128)S(1)}, f32[80,80]{1,0:T(8,128)S(1)}, u32[]{:S(2)}, u32[]{:S(2)}) collective-permute-start(f32[80,80]{1,0:T(8,128)S(1)} %add.15), channel_id=1, source_target_pairs={{0,2},{1,3},{2,0},{3,1},{4,6},{5,7},{6,4},{7,5},{8,10},{9,11},{10,... | collective-permute-start | bytes 76808 | tf_op jit(solution)/shard_map/ppermute | solution.py:365
  52.3 1.2 %collective-permute-start.10 = (f32[80,80]{1,0:T(8,128)S(1)}, f32[80,80]{1,0:T(8,128)S(1)}, u32[]{:S(2)}, u32[]{:S(2)}) collective-permute-start(f32[80,80]{1,0:T(8,128)S(1)} %add.16), channel_id=1, source_target_pairs={{0,4},{4,0},{8,12},{12,8},{16,20},{20,16},{24,28},{28,24},{1,5},{5... | collective-permute-start | bytes 76808 | tf_op jit(solution)/shard_map/ppermute | solution.py:365
  53.5 6.6 %collective-permute-start.11 = (f32[80,80]{1,0:T(8,128)S(1)}, f32[80,80]{1,0:T(8,128)S(1)}, u32[]{:S(2)}, u32[]{:S(2)}) collective-permute-start(f32[80,80]{1,0:T(8,128)S(1)} %add.17), channel_id=1, source_target_pairs={{0,8},{4,12},{8,0},{12,4},{16,24},{20,28},{24,16},{28,20},{1,9},{5... | collective-permute-start | bytes 76808 | tf_op jit(solution)/shard_map/ppermute | solution.py:365
  56.6 29.9 %all-to-all-start = ((f32[32,1,128]{2,1,0:T(1,128)}), f32[32,1,128]{2,1,0:T(1,128)S(1)}, u32[]{:S(2)}, u32[]{:S(2)}) async-start(f32[32,1,128]{2,1,0:T(1,128)} %bitcast.4), calls=%async_computation | async-start | bytes 32768 | tf_op jit(solution)/shard_map/all_to_all | solution.py:427
  60.1 5.6 %collective-permute-start.12 = (f32[80,80]{1,0:T(8,128)S(1)}, f32[80,80]{1,0:T(8,128)S(1)}, u32[]{:S(2)}, u32[]{:S(2)}) collective-permute-start(f32[80,80]{1,0:T(8,128)S(1)} %add.18), channel_id=1, source_target_pairs={{0,16},{4,20},{8,24},{12,28},{16,0},{20,4},{24,8},{28,12},{1,17},{... | collective-permute-start | bytes 76808 | tf_op jit(solution)/shard_map/ppermute | solution.py:365
  72.4 2.1 %copy-start.3 = (bf16[48,160,256]{2,1,0:T(8,128)(2,1)S(1)}, bf16[48,160,256]{2,1,0:T(8,128)(2,1)}, u32[]{:S(2)}) copy-start(bf16[48,160,256]{2,1,0:T(8,128)(2,1)} %copy-done.2) | copy-start | bytes 11796484
  86.5 2.1 %copy-start.1 = (f32[96,80,128]{2,1,0:T(8,128)S(1)}, f32[96,80,128]{2,1,0:T(8,128)}, u32[]{:S(2)}) copy-start(f32[96,80,128]{2,1,0:T(8,128)} %copy-done) | copy-start | bytes 11796484
where the time goes:
time: 92.3 us; the launch traced here: 92 us
  Pallas kernels  40.6 us (44%)
  starting transfers between devices  22.5 us (24%)
  local copies, waits for them, and re-layouts  14 us (15%)
  waiting for transfers between devices  14 us (15%)
    ppermute x8, starting transfers between devices, shifted(): lax.ppermute(value, axis, [(s, (s + steps) % count) for s in range(count)])  14.2 us
    unnamed x26, local copies, waits for them, and re-layouts  13.3 us
    pallas_call x1, Pallas kernels, on_device(): pl.pallas_call(rotate_kernel, out_shape=shape((cols, depth, 128)), name='...  12 us
    pallas_call x1, Pallas kernels, on_device(): pl.pallas_call(gram_kernel, out_shape=(shape((depth, cols, 128)), shape((...  10.3 us
    ppermute x5, waiting for transfers between devices, sum_everywhere(): lax.ppermute(value, axis, [(s, s ^ bit) for s in range(count)])  7.56 us
    pallas_call x1, Pallas kernels, on_device(): pl.pallas_call(lambda *refs: factor_kernel(inv_rows, *refs), out_shape=(s...  6.65 us
    ppermute x8, waiting for transfers between devices, shifted(): lax.ppermute(value, axis, [(s, (s + steps) % count) for s in range(count)])  6.45 us
    ppermute x5, starting transfers between devices, sum_everywhere(): lax.ppermute(value, axis, [(s, s ^ bit) for s in range(count)])  4.81 us
  transfers between devices with their start and end apart: 14, of which 7 were waited for; matrix products, arithmetic and copies ran while one was open for 1% of the time, Pallas kernels for 35%

commit v1 on v0

--- a/solution.py
+++ b/solution.py
@@ -37,6 +37,9 @@
 HIGHEST = lax.Precision.HIGHEST
 F32 = jnp.float32
 BF16 = jnp.bfloat16
+VMEM = pl.BlockSpec(memory_space=pltpu.VMEM)
+ANY = pl.BlockSpec(memory_space=pl.ANY)
+HBM = pl.BlockSpec(memory_space=pltpu.HBM)
 
 
 def params(mib=40):
@@ -107,15 +110,37 @@
         xdn_ref[k] = post_ref[i, 0]
 
 
-def first_kernel(f_ref, om_ref, so_ref, post_ref, xup_ref, xdn_ref, yup_ref, ydn_ref):
+def first_kernel(
+    f_hbm, om_hbm, so_hbm, post_ref, xup_ref, xdn_ref, yup_ref, ydn_ref, om_ref, so_ref, f_ref, sem
+):
     nx = f_ref.shape[1]
+    parts = sem.shape[0] - 2
+    rows = nx // parts
+
+    def load(k):
+        at = pl.ds(k * rows, rows)
+        return pltpu.make_async_copy(f_hbm.at[:, at], f_ref.at[:, at], sem.at[k])
+
+    loads = [load(k) for k in range(parts)]
+    omega = pltpu.make_async_copy(om_hbm, om_ref, sem.at[parts])
+    solid = pltpu.make_async_copy(so_hbm, so_ref, sem.at[parts + 1])
+    loads[0].start()
+    omega.start()
+    solid.start()
+    for k in range(1, parts):
+        loads[k].start()
 
     def step(x, carry):
         post = collide([f_ref[i, x] for i in range(NVEL)], om_ref[x], so_ref[x] > 0)
         emit_post(post, x, nx, post_ref, xup_ref, xdn_ref, yup_ref, ydn_ref)
         return carry
 
-    lax.fori_loop(0, nx, step, 0)
+    for k in range(parts):
+        loads[k].wait()
+        if k == 0:
+            omega.wait()
+            solid.wait()
+        lax.fori_loop(k * rows, (k + 1) * rows, step, 0)
     emit_faces(nx, post_ref, xup_ref, xdn_ref)
 
 
@@ -144,7 +169,19 @@
 
 
 def second_kernel(
-    p_ref, xu_ref, xd_ref, yu_ref, yd_ref, om_ref, so_ref, post_ref, xup_ref, xdn_ref, yup_ref, ydn_ref
+    p_ref,
+    xu_ref,
+    xd_ref,
+    yu_ref,
+    yd_ref,
+    om_ref,
+    so_ref,
+    gate_ref,
+    post_ref,
+    xup_ref,
+    xdn_ref,
+    yup_ref,
+    ydn_ref,
 ):
     nx = p_ref.shape[1]
 
@@ -158,7 +195,7 @@
     emit_faces(nx, post_ref, xup_ref, xdn_ref)
 
 
-def pack_kernel(xu_ref, xd_ref, yup_ref, ydn_ref, ou_ref, od_ref):
+def pack_kernel(xu_ref, xd_ref, yup_ref, ydn_ref, gate_ref, ou_ref, od_ref):
     nx = yup_ref.shape[0] // len(UP_Y)
     ny = xu_ref.shape[1]
     ou_ref[...] = yup_ref[...]
@@ -172,32 +209,36 @@
                 out[at : at + 1, :] = xd_ref[DOWN_X.index(i), row : row + 1, :]
 
 
-def gram_kernel(s_ref, basis_ref, snap_ref, a_ref, h_ref, g_ref):
+def gram_kernel(s_ref, basis_ref, snap_ref, gate_ref, a_ref, h_ref, g_ref):
     rank = basis_ref.shape[0]
     depth = basis_ref.shape[1]
     extra = snap_ref.shape[0]
     cols = a_ref.shape[1]
-    basis = basis_ref.reshape(rank * depth, 128)
-    snaps = snap_ref.reshape(extra * depth, 128)
-    scale = jnp.broadcast_to(s_ref[...], (rank, 128))
-    zero = jnp.zeros((cols - rank - extra, 128), F32)
-
-    def step(q, acc):
-        for t in range(2):
-            r = 2 * q + t
-            a_ref[r, 0:rank, :] = basis[pl.ds(r, rank, stride=depth), :] * scale
-            a_ref[r, rank : rank + extra, :] = snaps[pl.ds(r, extra, stride=depth), :]
-            a_ref[r, rank + extra : cols, :] = zero
-        rows = jnp.concatenate([a_ref[2 * q], a_ref[2 * q + 1]], axis=1)
-        high = rows.astype(BF16)
-        low = (rows - high.astype(F32)).astype(BF16)
-        both = jnp.concatenate([high, low], axis=0)
-        h_ref[q] = both
-        return acc + lax.dot_general(
-            both, high, (((1,), (1,)), ((), ())), preferred_element_type=F32
-        )
-
-    acc = lax.fori_loop(0, depth // 2, step, jnp.zeros((2 * cols, cols), F32))
+    same = lax.broadcasted_iota(jnp.int32, (rank, rank), 0) == lax.broadcasted_iota(
+        jnp.int32, (rank, rank), 1
+    )
+    scale = jnp.sum(jnp.where(same, s_ref[...], 0.0), axis=1, keepdims=True)
+    scale = jnp.broadcast_to(scale, (rank, 128))
+    zero = jnp.zeros((cols - rank - extra, 8, 128), F32)
+
+    def step(q, carry):
+        r = pl.multiple_of(q * 8, 8)
+        top = jnp.swapaxes(basis_ref[:, pl.ds(r, 8), :], 0, 1)
+        low = jnp.concatenate([snap_ref[:, pl.ds(r, 8), :], zero], axis=0)
+        low = jnp.swapaxes(low, 0, 1)
+        for t in range(8):
+            rows = jnp.concatenate([top[t] * scale, low[t]], axis=0)
+            a_ref[r + t] = rows
+            at = pl.ds(pl.multiple_of((r + t) * 128, 128), 128)
+            high = rows.astype(BF16)
+            h_ref[0:cols, at] = high
+            h_ref[cols : 2 * cols, at] = (rows - high.astype(F32)).astype(BF16)
+        return carry
+
+    lax.fori_loop(0, depth // 8, step, 0)
+    acc = lax.dot_general(
+        h_ref[...], h_ref[0:cols, :], (((1,), (1,)), ((), ())), preferred_element_type=F32
+    )
     cross = acc[cols:, :]
     eye = (
         lax.broadcasted_iota(jnp.int32, (cols, cols), 0)
@@ -212,55 +253,99 @@
 def factor_kernel(inv_rows, g_ref, u_ref, li_ref, w_ref):
     cols = g_ref.shape[0]
     known = cols - 1
-    row_id = lax.broadcasted_iota(jnp.int32, (cols, cols), 0)
-    col_id = lax.broadcasted_iota(jnp.int32, (cols, cols), 1)
-    left = g_ref[...] * inv_rows
-    right = (row_id == col_id).astype(F32)
-    down = lax.broadcasted_iota(jnp.int32, (cols, 1), 0)
-    for j in range(known):
-        column = left[:, j : j + 1]
-        pivot = lax.rsqrt(left[j : j + 1, j : j + 1])
-        scaled = column * pivot
-        step = jnp.where(down > j, scaled, 0.0)
-        top = left[j : j + 1, :] * pivot
-        aug = right[j : j + 1, :] * pivot
-        here = down == j
-        left = jnp.where(here, top, left - step * top)
-        right = jnp.where(here, aug, right - step * aug)
-    keep = jnp.logical_and(row_id <= col_id, col_id < known)
-    u_ref[...] = jnp.where(keep, left, 0.0)
-    inverse = jnp.where(jnp.logical_and(row_id >= col_id, row_id < known), right, 0.0)
-    li_ref[...] = inverse
-    high = inverse.astype(BF16)
-    w_ref[0] = high
-    w_ref[1] = (inverse - high.astype(F32)).astype(BF16)
-
-
-def rotate_kernel(w_ref, h_ref, o_ref):
-    cols = w_ref.shape[1]
-    depth = o_ref.shape[1]
-    out = o_ref.reshape(cols * depth, 128)
-    whigh, wlow = w_ref[0], w_ref[1]
+    blocks = cols // 8
+    pad = jnp.zeros((8, 128 - cols), F32)
+    sub = lax.broadcasted_iota(jnp.int32, (8, 128), 0)
+    lane = lax.broadcasted_iota(jnp.int32, (8, 128), 1)
+    left = [
+        jnp.concatenate([g_ref[8 * b : 8 * b + 8, :] * inv_rows, pad], axis=1) for b in range(blocks)
+    ]
+    right = [(sub + 8 * b == lane).astype(F32) for b in range(blocks)]
+    for p in range(blocks):
+        live = range(p, blocks)
+        width = min(8, known - 8 * p)
+        col = [
+            {
+                b: jnp.broadcast_to(left[b][:, 8 * p + t : 8 * p + t + 1], (8, 128))
+                for b in live
+            }
+            for t in range(width)
+        ]
+        for t in range(width):
+            pivot = lax.rsqrt(jnp.broadcast_to(col[t][p][t : t + 1, :], (8, 128)))
+            lcol = {b: col[t][b] * pivot for b in live}
+            lcol[p] = jnp.where(sub > t, lcol[p], 0.0)
+            for v in range(t + 1, width):
+                m = jnp.broadcast_to(lcol[p][v : v + 1, :], (8, 128))
+                for b in live:
+                    col[v][b] = col[v][b] - lcol[b] * m
+            top = jnp.broadcast_to(left[p][t : t + 1, :], (8, 128)) * pivot
+            aug = jnp.broadcast_to(right[p][t : t + 1, :], (8, 128)) * pivot
+            for b in live:
+                left[b] = left[b] - lcol[b] * top
+                right[b] = right[b] - lcol[b] * aug
+            left[p] = jnp.where(sub == t, top, left[p])
+            right[p] = jnp.where(sub == t, aug, right[p])
+    fill = jnp.zeros((8, 128), F32)
+    for b in range(blocks):
+        row = sub + 8 * b
+        upper = jnp.where(jnp.logical_and(row <= lane, lane < known), left[b], 0.0)
+        inverse = jnp.where(jnp.logical_and(row >= lane, row < known), right[b], 0.0)
+        u_ref[8 * b : 8 * b + 8, :] = upper[:, :cols]
+        li_ref[8 * b : 8 * b + 8, :] = inverse[:, :cols]
+        high = inverse.astype(BF16).astype(F32)
+        wide = jnp.concatenate([high, fill], axis=1)
+        rest = jnp.concatenate([inverse - high, fill], axis=1)
+        wide = wide + pltpu.roll(rest, cols, 1) + pltpu.roll(wide, 2 * cols, 1)
+        w_ref[8 * b : 8 * b + 8, :] = wide[:, : 3 * cols]
+
+
+def rotate_kernel(w_ref, h_ref, o_ref, out_ref, sem):
+    cols = w_ref.shape[0]
+    depth = out_ref.shape[1]
+    weight = w_ref[...].astype(BF16)
+
+    def copy(q):
+        at = pl.ds(pl.multiple_of(q * 8, 8), 8)
+        return pltpu.make_async_copy(out_ref.at[:, at, :], o_ref.at[:, at, :], sem.at[q])
 
     def step(q, carry):
-        high = h_ref[q, 0:cols, :]
-        low = h_ref[q, cols:, :]
-        dims = (((1,), (0,)), ((), ()))
-        res = lax.dot_general(whigh, high, dims, preferred_element_type=F32)
-        res = res + lax.dot_general(wlow, high, dims, preferred_element_type=F32)
-        res = res + lax.dot_general(whigh, low, dims, preferred_element_type=F32)
-        out[pl.ds(2 * q, cols, stride=depth), :] = res[:, :128]
-        out[pl.ds(2 * q + 1, cols, stride=depth), :] = res[:, 128:]
-        return carry
-
-    lax.fori_loop(0, depth // 2, step, 0)
+        at = pl.ds(pl.multiple_of(q * 1024, 1024), 1024)
+        high = h_ref[0:cols, at]
+        low = h_ref[cols : 2 * cols, at]
+        res = lax.dot_general(
+            weight,
+            jnp.concatenate([high, high, low], axis=0),
+            (((1,), (0,)), ((), ())),
+            preferred_element_type=F32,
+        )
+        res = jnp.stack([res[:, t * 128 : (t + 1) * 128] for t in range(8)], axis=0)
+        out_ref[:, pl.ds(pl.multiple_of(q * 8, 8), 8), :] = jnp.swapaxes(res, 0, 1)
+        copy(q).start()
+        return carry
+
+    lax.fori_loop(0, depth // 8, step, 0)
+
+    def finish(q, carry):
+        copy(q).wait()
+        return carry
+
+    lax.fori_loop(0, depth // 8, finish, 0)
 
 
 def final_kernel(
-    p_ref, xu_ref, xd_ref, yu_ref, yd_ref, so_ref, a_ref, f_ref, c_ref, v_ref, vel_ref
+    p_ref, xu_ref, xd_ref, yu_ref, yd_ref, so_ref, a_ref, f_hbm, c_ref, v_ref, vel_ref, f_ref, sem
 ):
     nx, ny, nz = p_ref.shape[1:]
     nxc, nyc = nx // 2, ny // 2
+
+    def copy(xc):
+        at = pl.ds(2 * xc, 2)
+        return pltpu.make_async_copy(f_ref.at[:, at], f_hbm.at[:, at], sem.at[xc])
+
+    def finish(xc, carry):
+        copy(xc).wait()
+        return carry
 
     def step(xc, carry):
         total = [None] * 3
@@ -278,6 +363,7 @@
             at = pl.multiple_of((k * nxc + xc) * ny, ny)
             for t in range(nz // 128):
                 vel_ref[t, pl.ds(at, ny), :] = total[k][:, t * 128 : (t + 1) * 128]
+        copy(xc).start()
         return carry
 
     lax.fori_loop(0, nxc, step, 0)
@@ -300,7 +386,7 @@
     def inner(r, acc):
         return acc + a_ref[r] * c_ref[pl.ds(r, 1), :]
 
-    acc = lax.fori_loop(0, depth, inner, jnp.zeros((cols, 128), F32))
+    acc = lax.fori_loop(0, depth, inner, jnp.zeros((cols, 128), F32), unroll=8)
     dots = jnp.sum(acc, axis=1, keepdims=True)
     own = jnp.sum(c_ref[...] * c_ref[...])
     down = lax.broadcasted_iota(jnp.int32, (cols, 1), 0)
@@ -309,6 +395,7 @@
     diag = jnp.where(across == lax.broadcasted_iota(jnp.int32, (cols, 128), 0), dots, 0.0)
     line = jnp.sum(diag, axis=0, keepdims=True)
     v_ref[...] = jnp.broadcast_to(line, v_ref.shape)
+    lax.fori_loop(0, nxc, finish, 0)
 
 
 def last_kernel(inv_rows, v_ref, li_ref, u_ref, a_ref, c_ref, q_ref, uo_ref, o_ref, row_ref, sem):
@@ -336,7 +423,7 @@
         row_ref[pl.ds(r, 1), :] = part + c_ref[pl.ds(r, 1), :] * pivot
         return carry
 
-    lax.fori_loop(0, depth, step, 0)
+    lax.fori_loop(0, depth, step, 0, unroll=8)
     copy = pltpu.make_async_copy(row_ref, o_ref.at[known], sem)
     copy.start()
     copy.wait()
@@ -350,20 +437,31 @@
     return shifted(xup, "gx", 1), shifted(xdn, "gx", -1)
 
 
-def halo_y(xu, xd, yup, ydn):
+def halo_y(xu, xd, yup, ydn, gate):
     send_up, send_dn = pl.pallas_call(
-        pack_kernel, out_shape=(shape(yup.shape), shape(ydn.shape)), name="pack", compiler_params=params(8)
-    )(xu, xd, yup, ydn)
+        pack_kernel,
+        out_shape=(shape(yup.shape), shape(ydn.shape)),
+        in_specs=[VMEM] * 4 + [ANY],
+        name="pack",
+        compiler_params=params(2),
+    )(xu, xd, yup, ydn, gate)
     return shifted(send_up, "gy", 1), shifted(send_dn, "gy", -1)
 
 
-def sum_everywhere(value):
-    for axis in ("gy", "gx"):
-        count = lax.axis_size(axis)
+def rounds():
+    steps = []
+    for axis in ("gx", "gy"):
         bit = 1
-        while bit < count:
-            value = value + lax.ppermute(value, axis, [(s, s ^ bit) for s in range(count)])
+        while bit < lax.axis_size(axis):
+            steps.append((axis, bit))
             bit *= 2
+    return steps
+
+
+def exchange(value, steps):
+    for axis, bit in steps:
+        pairs = [(s, s ^ bit) for s in range(lax.axis_size(axis))]
+        value = value + lax.ppermute(value, axis, pairs)
     return value
 
 
@@ -383,59 +481,86 @@
         shape((edges, nz)),
         shape((edges, nz)),
     )
-    post, xup, xdn, yup, ydn = pl.pallas_call(
-        first_kernel, out_shape=post_shapes, name="first", compiler_params=params(16)
+    post, xup, xdn, yup, ydn, omega, solid = pl.pallas_call(
+        first_kernel,
+        out_shape=post_shapes + (shape((nx, ny, nz)), shape((nx, ny, nz), jnp.int32)),
+        in_specs=[HBM] * 3,
+        scratch_shapes=[pltpu.VMEM((NVEL, nx, ny, nz), F32), pltpu.SemaphoreType.DMA((6,))],
+        name="first",
+        compiler_params=params(6),
     )(populations, relax_rate, solid_mask)
     xu, xd = halo_x(xup, xdn)
     rows, halves, gram = pl.pallas_call(
         gram_kernel,
         out_shape=(
-            shape((depth, cols, 128)),
-            shape((depth // 2, 2 * cols, 256), BF16),
+            pltpu.VMEM((depth, cols, 128), F32),
+            pltpu.VMEM((2 * cols, depth * 128), BF16),
             shape((cols, cols)),
         ),
+        in_specs=[VMEM] * 3 + [ANY],
         name="gram",
-        compiler_params=params(24),
+        compiler_params=params(4),
     )(
-        singular_values.reshape(rank, 1),
+        singular_values.reshape(1, rank),
         basis.reshape(rank, depth, 128),
         snapshots.reshape(extra, depth, 128),
-    )
-    yu, yd = halo_y(xu, xd, yup, ydn)
-    gram = sum_everywhere(gram)
+        omega,
+    )
+    yu, yd = halo_y(xu, xd, yup, ydn, gram)
+    steps = rounds()
+    gram = exchange(gram, steps[:2])
     post, xup, xdn, yup, ydn = pl.pallas_call(
-        second_kernel, out_shape=post_shapes, name="second", compiler_params=params(16)
-    )(post, xu, xd, yu, yd, relax_rate, solid_mask)
+        second_kernel,
+        out_shape=post_shapes,
+        in_specs=[VMEM] * 7 + [ANY],
+        name="second",
+        compiler_params=params(4),
+    )(post, xu, xd, yu, yd, omega, solid, gram)
     xu, xd = halo_x(xup, xdn)
-    upper, inverse, split = pl.pallas_call(
-        lambda *refs: factor_kernel(inv_rows, *refs),
-        out_shape=(shape((cols, cols)), shape((cols, cols)), shape((2, cols, cols), BF16)),
-        name="factor",
-        compiler_params=params(8),
-    )(gram)
-    yu, yd = halo_y(xu, xd, yup, ydn)
-    rotated = pl.pallas_call(
-        rotate_kernel, out_shape=shape((cols, depth, 128)), name="rotate", compiler_params=params(16)
-    )(split, halves)
+    gram = exchange(gram, steps[2:4])
+    yu, yd = halo_y(xu, xd, yup, ydn, gram)
+    gram = exchange(gram, steps[4:])
     field, coarse, line = pl.pallas_call(
         final_kernel,
         out_shape=(shape((NVEL, nx, ny, nz)), shape((depth, 128)), shape((n_dev, 128))),
-        scratch_shapes=[pltpu.VMEM((nz // 128, 3 * (nx // 2) * ny, 128), F32)],
+        in_specs=[VMEM] * 7,
+        out_specs=(ANY, VMEM, VMEM),
+        scratch_shapes=[
+            pltpu.VMEM((nz // 128, 3 * (nx // 2) * ny, 128), F32),
+            pltpu.VMEM((NVEL, nx, ny, nz), F32),
+            pltpu.SemaphoreType.DMA((nx // 2,)),
+        ],
         name="final",
-        compiler_params=params(24),
-    )(post, xu, xd, yu, yd, solid_mask, rows)
+        compiler_params=params(6),
+    )(post, xu, xd, yu, yd, solid, rows)
     lines = lax.all_to_all(line, ("gx", "gy"), 0, 0, tiled=True)
-    vmem = pl.BlockSpec(memory_space=pltpu.VMEM)
-    hbm = pl.BlockSpec(memory_space=pl.ANY)
+    upper, inverse, split = pl.pallas_call(
+        lambda *refs: factor_kernel(inv_rows, *refs),
+        out_shape=(shape((cols, cols)), shape((cols, cols)), shape((cols, 3 * cols))),
+        name="factor",
+        compiler_params=params(4),
+    )(gram)
+    rotated = pl.pallas_call(
+        rotate_kernel,
+        out_shape=shape((cols, depth, 128)),
+        in_specs=[VMEM] * 2,
+        out_specs=ANY,
+        scratch_shapes=[
+            pltpu.VMEM((cols, depth, 128), F32),
+            pltpu.SemaphoreType.DMA((depth // 8,)),
+        ],
+        name="rotate",
+        compiler_params=params(8),
+    )(split, halves)
     upper, rotated = pl.pallas_call(
         lambda *refs: last_kernel(inv_rows, *refs),
         out_shape=(shape((cols, cols)), shape((cols, depth, 128))),
-        in_specs=[vmem] * 5 + [hbm],
-        out_specs=(vmem, hbm),
+        in_specs=[VMEM] * 5 + [ANY],
+        out_specs=(VMEM, ANY),
         scratch_shapes=[pltpu.VMEM((depth, 128), F32), pltpu.SemaphoreType.DMA],
         input_output_aliases={5: 1},
         name="last",
-        compiler_params=params(16),
+        compiler_params=params(4),
     )(lines, inverse, upper, rows, coarse, rotated)
     return field, upper, rotated.reshape((cols,) + tail)
 

time: 92.3 us -> 67.2 us (0.73)
  Pallas kernels: 40.6 us -> 19 us
  local copies, waits for them, and re-layouts: 14 us -> 12.2 us
  starting transfers between devices: 22.5 us -> 20.8 us
    pallas_call x4, Pallas kernels: 27.6 us -> 12.6 us  [the longest x1 3.8 us: on_device(): pl.pallas_call(rotate_kernel, out_shape=shape((cols, depth, 128)), in_spe...]
    pallas_call x1, Pallas kernels: 6.65 us -> 2.33 us  [on_device(): pl.pallas_call(lambda *refs: factor_kernel(inv_rows, *refs), out_shape=(s...]
    ppermute x5, waiting for transfers between devices: 7.56 us -> 10.7 us  [exchange(): value = value + lax.ppermute(value, axis, pairs)]
    ppermute x8, waiting for transfers between devices: 6.45 us -> 3.37 us  [shifted(): lax.ppermute(value, axis, [(s, (s + steps) % count) for s in range(count)])]
    pallas_call x1, Pallas kernels: 3.36 us -> 1.93 us  [on_device(): pl.pallas_call(lambda *refs: last_kernel(inv_rows, *refs), out_shape=(sha...]
    unnamed x26 -> x20, local copies, waits for them, and re-layouts: 13.3 us -> 12.2 us
  transfers between devices with their start and end apart: 14 -> 14, of which waited for: 7 -> 6; matrix products, arithmetic and copies ran while one was open for 1% -> 0% of each run, Pallas kernels for 35% -> 18%
where the time goes in v1:
time: 67.2 us; the launch traced here: 66.9 us
  starting transfers between devices  20.8 us (31%)
  Pallas kernels  19 us (28%)
  waiting for transfers between devices  14.1 us (21%)
  local copies, waits for them, and re-layouts  12.2 us (18%)
  between operations  0.78 us (1%)
    ppermute x8, starting transfers between devices, shifted(): lax.ppermute(value, axis, [(s, (s + steps) % count) for s in range(count)])  14.2 us
    unnamed x20, local copies, waits for them, and re-layouts  12.2 us
    ppermute x5, waiting for transfers between devices, exchange(): value = value + lax.ppermute(value, axis, pairs)  10.7 us
    ppermute x5, starting transfers between devices, exchange(): value = value + lax.ppermute(value, axis, pairs)  3.89 us
    pallas_call x1, Pallas kernels, on_device(): pl.pallas_call(rotate_kernel, out_shape=shape((cols, depth, 128)), in_spe...  3.8 us
    pallas_call x1, Pallas kernels, on_device(): pl.pallas_call(gram_kernel, out_shape=(pltpu.VMEM((depth, cols, 128), F32...  3.55 us
    ppermute x8, waiting for transfers between devices, shifted(): lax.ppermute(value, axis, [(s, (s + steps) % count) for s in range(count)])  3.37 us
    pallas_call x1, Pallas kernels, on_device(): pl.pallas_call(first_kernel, out_shape=post_shapes + (shape((nx, ny, nz))...  2.77 us
  transfers between devices with their start and end apart: 14, of which 6 were waited for; matrix products, arithmetic and copies ran while one was open for 0% of the time, Pallas kernels for 18%

profile of v1, /device:TPU:0, one launch (start us, length us, event | category | flops | bytes accessed | tf_op | source)
XLA Modules:
  0.0 66.9 jit_solution(8567428596721165377)
XLA Ops:
  0.6 0.0 copy-start.5
  0.6 1.7 %copy-done.5 = f32[19,16,8,256]{3,2,1,0:T(8,128)S(1)} copy-done((f32[19,16,8,256]{3,2,1,0:T(8,128)S(1)}, f32[19,16,8,256]{3,2,1,0:T(8,128)}, u32[]{:S(2)}) %copy-start.5) | copy-done | bytes 2490392
  2.3 0.9 %copy-done.7 = f32[16,8,256]{2,1,0:T(8,128)S(1)} copy-done((f32[16,8,256]{2,1,0:T(8,128)S(1)}, f32[16,8,256]{2,1,0:T(8,128)}, u32[]{:S(2)}) %copy-start.7) | copy-done | bytes 131096
  3.2 0.9 %copy-done.8 = s32[16,8,256]{2,1,0:T(8,128)S(1)} copy-done((s32[16,8,256]{2,1,0:T(8,128)S(1)}, s32[16,8,256]{2,1,0:T(8,128)}, u32[]{:S(2)}) %copy-start.8) | copy-done | bytes 131096
  4.1 2.8 %first.1 = (f32[19,16,8,256]{3,2,1,0:T(8,128)S(1)}, f32[5,8,256]{2,1,0:T(8,128)S(1)}, f32[5,8,256]{2,1,0:T(8,128)S(1)}, f32[80,256]{1,0:T(8,128)S(1)}, f32[80,25...) custom-call(f32[19,16,8,256]{3,2,1,0:T(8,128)S(1)} %copy-done.5, f32[16,8,256]{2,1,0:T(8,128)S(1)} %copy-done.7, ...), custom_call_target="tpu_custom_call" | custom-call | tf_op jit(solution)/shard_map/first/pallas_call | solution.py:484
  6.9 0.5 collective-permute-start
  7.5 4.1 %collective-permute-start.1 = (f32[5,8,256]{2,1,0:T(8,128)S(1)}, f32[5,8,256]{2,1,0:T(8,128)S(1)}, u32[]{:S(2)}, u32[]{:S(2)}) collective-permute-start(f32[5,8,256]{2,1,0:T(8,128)S(1)} %get-tuple-element.32), channel_id=1, source_target_pairs={{0,28},{4,0},{8,4},{12,8},{16,12},{20,16},{24,20},{28,24},{1,29},{... | collective-permute-start | bytes 122888 | tf_op jit(solution)/shard_map/ppermute | solution.py:51
  11.6 0.0 copy-done.6
  11.6 1.9 %copy-done.4 = f32[64,3,8,4,128]{4,3,2,1,0:T(4,128)S(1)} copy-done((f32[64,3,8,4,128]{4,3,2,1,0:T(4,128)S(1)}, f32[64,3,8,4,128]{4,3,2,1,0:T(4,128)}, u32[]{:S(2)}) %copy-start.4) | copy-done | bytes 3145752
  13.5 0.7 copy-done.9
  14.1 3.6 %gram.1 = (f32[96,80,128]{2,1,0:T(8,128)S(1)}, bf16[160,12288]{1,0:T(8,128)(2,1)S(1)}, f32[80,80]{1,0:T(8,128)S(1)}) custom-call(f32[1,64]{1,0:T(1,128)S(1)} %bitcast.11, f32[64,96,128]{2,1,0:T(8,128)S(1)} %bitcast.8, f32[15,96,128]{2,1,0:T(8,128)S(1)} %bitcast.9, f32[16,8,256]{2,1,0:T(8,128)S(1)} %get-tuple-element.35.gate_ref.om_ref), custom_call_target="tpu_custom_call" | custom-call | tf_op jit(solution)/shard_map/gram/pallas_call | solution.py:493
  17.7 0.0 copy-start.2
  17.7 1.9 %copy-done.2 = bf16[160,12288]{1,0:T(8,128)(2,1)} copy-done((bf16[160,12288]{1,0:T(8,128)(2,1)}, bf16[160,12288]{1,0:T(8,128)(2,1)S(1)}, u32[]{:S(2)}) %copy-start.2) | copy-done | bytes 3932184
  19.6 0.0 collective-permute-done.xu_ref
  19.6 0.0 collective-permute-done.1.xd_ref
  19.6 2.0 %collective-permute-start.2 = (f32[80,256]{1,0:T(8,128)S(1)}, f32[80,256]{1,0:T(8,128)S(1)}, u32[]{:S(2)}, u32[]{:S(2)}) collective-permute-start(f32[80,256]{1,0:T(8,128)S(1)} %get-tuple-element.37), channel_id=1, source_target_pairs={{0,1},{1,2},{2,3},{3,0},{4,5},{5,6},{6,7},{7,4},{8,9},{9,10},{10,1... | collective-permute-start | bytes 245768 | tf_op jit(solution)/shard_map/ppermute | solution.py:51
  21.6 1.0 %collective-permute-start.3 = (f32[80,256]{1,0:T(8,128)S(1)}, f32[80,256]{1,0:T(8,128)S(1)}, u32[]{:S(2)}, u32[]{:S(2)}) collective-permute-start(f32[80,256]{1,0:T(8,128)S(1)} %get-tuple-element.38), channel_id=1, source_target_pairs={{0,3},{1,0},{2,1},{3,2},{4,7},{5,4},{6,5},{7,6},{8,11},{9,8},{10,9... | collective-permute-start | bytes 245768 | tf_op jit(solution)/shard_map/ppermute | solution.py:51
  22.6 0.0 collective-permute-start.4
  22.6 1.2 %collective-permute-done.4 = f32[80,80]{1,0:T(8,128)S(1)} collective-permute-done((f32[80,80]{1,0:T(8,128)S(1)}, f32[80,80]{1,0:T(8,128)S(1)}, u32[]{:S(2)}, u32[]{:S(2)}) %collective-permute-start.4) | collective-permute-done | bytes 25632 | tf_op jit(solution)/shard_map/ppermute | solution.py:464
  23.9 0.2 collective-permute-start.5
  24.1 3.8 %collective-permute-done.5 = f32[80,80]{1,0:T(8,128)S(1)} collective-permute-done((f32[80,80]{1,0:T(8,128)S(1)}, f32[80,80]{1,0:T(8,128)S(1)}, u32[]{:S(2)}, u32[]{:S(2)}) %collective-permute-start.5) | collective-permute-done | bytes 25632 | tf_op jit(solution)/shard_map/ppermute | solution.py:464
  27.9 1.2 %collective-permute-start.8 = (f32[80,80]{1,0:T(8,128)S(1)}, f32[80,80]{1,0:T(8,128)S(1)}, u32[]{:S(2)}, u32[]{:S(2)}) collective-permute-start(f32[80,80]{1,0:T(8,128)S(1)} %add.16.gate_ref), channel_id=1, source_target_pairs={{0,16},{4,20},{8,24},{12,28},{16,0},{20,4},{24,8},{28,12},{1,17},{... | collective-permute-start | bytes 76808 | tf_op jit(solution)/shard_map/ppermute | solution.py:464
  29.1 0.0 collective-permute-done.2.yu_ref
  29.1 0.0 collective-permute-done.3.yd_ref
  29.1 2.4 %second.1 = (f32[19,16,8,256]{3,2,1,0:T(8,128)S(1)}, f32[5,8,256]{2,1,0:T(8,128)S(1)}, f32[5,8,256]{2,1,0:T(8,128)S(1)}, f32[80,256]{1,0:T(8,128)S(1)}, f32[80,256]{1,0:T(8,128)S(1)}) custom-call(f32[19,16,8,256]{3,2,1,0:T(8,128)S(1)} %get-tuple-element.30.p_ref, f32[5,8,256]{2,1,0:T(8,128)S(1)} %collective-permute-done.xu_ref, ...), custom_call_target="tpu_custom_call" | custom-call | tf_op jit(solution)/shard_map/second/pallas_call | solution.py:512
  31.5 0.1 collective-permute-start.6
  31.6 3.5 %collective-permute-start.7 = (f32[5,8,256]{2,1,0:T(8,128)S(1)}, f32[5,8,256]{2,1,0:T(8,128)S(1)}, u32[]{:S(2)}, u32[]{:S(2)}) collective-permute-start(f32[5,8,256]{2,1,0:T(8,128)S(1)} %get-tuple-element.42), channel_id=1, source_target_pairs={{0,28},{4,0},{8,4},{12,8},{16,12},{20,16},{24,20},{28,24},{1,29},{... | collective-permute-start | bytes 122888 | tf_op jit(solution)/shard_map/ppermute | solution.py:51
  35.1 0.0 collective-permute-done.8
  35.1 0.7 collective-permute-start.9
  35.8 3.4 %collective-permute-done.9 = f32[80,80]{1,0:T(8,128)S(1)} collective-permute-done((f32[80,80]{1,0:T(8,128)S(1)}, f32[80,80]{1,0:T(8,128)S(1)}, u32[]{:S(2)}, u32[]{:S(2)}) %collective-permute-start.9) | collective-permute-done | bytes 25632 | tf_op jit(solution)/shard_map/ppermute | solution.py:464
  39.2 0.0 collective-permute-done.6.xu_ref
  39.2 0.0 collective-permute-done.7.xd_ref
  39.3 0.6 collective-permute-start.10
  39.9 2.3 %collective-permute-start.11 = (f32[80,256]{1,0:T(8,128)S(1)}, f32[80,256]{1,0:T(8,128)S(1)}, u32[]{:S(2)}, u32[]{:S(2)}) collective-permute-start(f32[80,256]{1,0:T(8,128)S(1)} %get-tuple-element.46), channel_id=1, source_target_pairs={{0,3},{1,0},{2,1},{3,2},{4,7},{5,4},{6,5},{7,6},{8,11},{9,8},{10,9... | collective-permute-start | bytes 245768 | tf_op jit(solution)/shard_map/ppermute | solution.py:51
  42.2 2.4 %collective-permute-done.10.yu_ref = f32[80,256]{1,0:T(8,128)S(1)} collective-permute-done((f32[80,256]{1,0:T(8,128)S(1)}, f32[80,256]{1,0:T(8,128)S(1)}, u32[]{:S(2)}, u32[]{:S(2)}) %collective-permute-start.10) | collective-permute-done | bytes 81952 | tf_op jit(solution)/shard_map/ppermute | solution.py:51
  44.7 0.9 %collective-permute-done.11.yd_ref = f32[80,256]{1,0:T(8,128)S(1)} collective-permute-done((f32[80,256]{1,0:T(8,128)S(1)}, f32[80,256]{1,0:T(8,128)S(1)}, u32[]{:S(2)}, u32[]{:S(2)}) %collective-permute-start.11) | collective-permute-done | bytes 81952 | tf_op jit(solution)/shard_map/ppermute | solution.py:51
  45.6 2.2 %final.1 = (f32[19,16,8,256]{3,2,1,0:T(8,128)}, f32[96,128]{1,0:T(8,128)S(1)}, f32[32,128]{1,0:T(8,128)}) custom-call(f32[19,16,8,256]{3,2,1,0:T(8,128)S(1)} %get-tuple-element.40.p_ref, f32[5,8,256]{2,1,0:T(8,128)S(1)} %collective-permute-done.6.xu_ref, f32[5,8,256]{2,1,0:T(8,128)S(1)} %collective-permute-done.7.xd_ref, ...), custom_call_target="tpu_custom_call" | custom-call | tf_op jit(solution)/shard_map/final/pallas_call | solution.py:523
  47.8 0.0 copy-done
  47.8 2.7 %all-to-all-start = ((f32[32,1,128]{2,1,0:T(1,128)}), f32[32,1,128]{2,1,0:T(1,128)S(1)}, u32[]{:S(2)}, u32[]{:S(2)}) async-start(f32[32,1,128]{2,1,0:T(1,128)} %bitcast.4), calls=%async_computation | async-start | bytes 32768 | tf_op jit(solution)/shard_map/all_to_all | solution.py:536
  50.5 1.8 %collective-permute-start.12 = (f32[80,80]{1,0:T(8,128)S(1)}, f32[80,80]{1,0:T(8,128)S(1)}, u32[]{:S(2)}, u32[]{:S(2)}) collective-permute-start(f32[80,80]{1,0:T(8,128)S(1)} %add.18.gate_ref), channel_id=1, source_target_pairs={{0,2},{1,3},{2,0},{3,1},{4,6},{5,7},{6,4},{7,5},{8,10},{9,11},{10,... | collective-permute-start | bytes 76808 | tf_op jit(solution)/shard_map/ppermute | solution.py:464
  52.3 2.3 %collective-permute-done.12 = f32[80,80]{1,0:T(8,128)S(1)} collective-permute-done((f32[80,80]{1,0:T(8,128)S(1)}, f32[80,80]{1,0:T(8,128)S(1)}, u32[]{:S(2)}, u32[]{:S(2)}) %collective-permute-start.12) | collective-permute-done | bytes 25632 | tf_op jit(solution)/shard_map/ppermute | solution.py:464
  54.6 2.3 %factor.1 = (f32[80,80]{1,0:T(8,128)S(1)}, f32[80,80]{1,0:T(8,128)S(1)}, f32[80,240]{1,0:T(8,128)S(1)}) custom-call(f32[80,80]{1,0:T(8,128)S(1)} %add.19.refs_0_), custom_call_target="tpu_custom_call" | custom-call | tf_op jit(solution)/shard_map/factor/pallas_call | solution.py:537
  56.9 2.1 %copy-done.3 = bf16[160,12288]{1,0:T(8,128)(2,1)S(1)} copy-done((bf16[160,12288]{1,0:T(8,128)(2,1)S(1)}, bf16[160,12288]{1,0:T(8,128)(2,1)}, u32[]{:S(2)}) %copy-start.3) | copy-done | bytes 3932184
  59.0 3.8 %rotate.1.refs_5_ = f32[80,96,128]{2,1,0:T(8,128)} custom-call(f32[80,240]{1,0:T(8,128)S(1)} %get-tuple-element.53.w_ref, bf16[160,12288]{1,0:T(8,128)(2,1)S(1)} %copy-done.3), custom_call_target="tpu_custom_call" | custom-call | tf_op jit(solution)/shard_map/rotate/pallas_call | solution.py:543
  62.8 0.0 all-to-all-done
  62.8 0.0 copy-start.1
  62.9 2.1 %copy-done.1 = f32[96,80,128]{2,1,0:T(8,128)S(1)} copy-done((f32[96,80,128]{2,1,0:T(8,128)S(1)}, f32[96,80,128]{2,1,0:T(8,128)}, u32[]{:S(2)}) %copy-start.1) | copy-done | bytes 3932184
  65.0 1.9 %last.1 = (f32[80,80]{1,0:T(8,128)}, f32[80,96,128]{2,1,0:T(8,128)}) custom-call(f32[32,128]{1,0:T(8,128)S(1)} %bitcast.10, f32[80,80]{1,0:T(8,128)S(1)} %get-tuple-element.50.refs_1_, f32[80,80]{1,0:T(8,128)S(1)} %get-tuple-element.51.refs_2_, f32[96,80,128]{2,1,0:T(8,128)S(1)} %copy-done.1, ...), custom_call_target="tpu_custom_call", output_to_operand_aliasing={{1}: (5, {})} | custom-call | tf_op jit(solution)/shard_map/last/pallas_call | solution.py:555
  (14 shorter events, 0.1 us)
Async XLA Ops:
  0.6 1.7 %copy-start.5 = (f32[19,16,8,256]{3,2,1,0:T(8,128)S(1)}, f32[19,16,8,256]{3,2,1,0:T(8,128)}, u32[]{:S(2)}) copy-start(f32[19,16,8,256]{3,2,1,0:T(8,128)} %f_hbm.1) | copy-start | bytes 7471108
  2.3 0.9 %copy-start.7 = (f32[16,8,256]{2,1,0:T(8,128)S(1)}, f32[16,8,256]{2,1,0:T(8,128)}, u32[]{:S(2)}) copy-start(f32[16,8,256]{2,1,0:T(8,128)} %om_hbm.1) | copy-start | bytes 393220
  3.2 0.9 %copy-start.8 = (s32[16,8,256]{2,1,0:T(8,128)S(1)}, s32[16,8,256]{2,1,0:T(8,128)}, u32[]{:S(2)}) copy-start(s32[16,8,256]{2,1,0:T(8,128)} %so_hbm.1) | copy-start | bytes 393220
  4.1 7.4 %copy-start.6 = (f32[15,3,8,4,128]{4,3,2,1,0:T(4,128)S(1)}, f32[15,3,8,4,128]{4,3,2,1,0:T(4,128)}, u32[]{:S(2)}) copy-start(f32[15,3,8,4,128]{4,3,2,1,0:T(4,128)} %param.11) | copy-start | bytes 2211844
  6.9 12.7 %collective-permute-start = (f32[5,8,256]{2,1,0:T(8,128)S(1)}, f32[5,8,256]{2,1,0:T(8,128)S(1)}, u32[]{:S(2)}, u32[]{:S(2)}) collective-permute-start(f32[5,8,256]{2,1,0:T(8,128)S(1)} %get-tuple-element.31), channel_id=1, source_target_pairs={{0,4},{4,8},{8,12},{12,16},{16,20},{20,24},{24,28},{28,0},{1,5},{5... | collective-permute-start | bytes 122888 | tf_op jit(solution)/shard_map/ppermute | solution.py:51
  7.5 12.1 %collective-permute-start.1 = (f32[5,8,256]{2,1,0:T(8,128)S(1)}, f32[5,8,256]{2,1,0:T(8,128)S(1)}, u32[]{:S(2)}, u32[]{:S(2)}) collective-permute-start(f32[5,8,256]{2,1,0:T(8,128)S(1)} %get-tuple-element.32), channel_id=1, source_target_pairs={{0,28},{4,0},{8,4},{12,8},{16,12},{20,16},{24,20},{28,24},{1,29},{... | collective-permute-start | bytes 122888 | tf_op jit(solution)/shard_map/ppermute | solution.py:51
  11.6 1.9 %copy-start.4 = (f32[64,3,8,4,128]{4,3,2,1,0:T(4,128)S(1)}, f32[64,3,8,4,128]{4,3,2,1,0:T(4,128)}, u32[]{:S(2)}) copy-start(f32[64,3,8,4,128]{4,3,2,1,0:T(4,128)} %param.10) | copy-start | bytes 9437188
  13.5 0.7 copy-start.9
  17.7 1.9 %copy-start.2 = (bf16[160,12288]{1,0:T(8,128)(2,1)}, bf16[160,12288]{1,0:T(8,128)(2,1)S(1)}, u32[]{:S(2)}) copy-start(bf16[160,12288]{1,0:T(8,128)(2,1)S(1)} %get-tuple-element.54.h_ref) | copy-start | bytes 11796484
  19.6 28.2 %copy-start = (f32[96,80,128]{2,1,0:T(8,128)}, f32[96,80,128]{2,1,0:T(8,128)S(1)}, u32[]{:S(2)}) copy-start(f32[96,80,128]{2,1,0:T(8,128)S(1)} %get-tuple-element.47.a_ref.refs_3_) | copy-start | bytes 11796484
  19.6 9.4 %collective-permute-start.2 = (f32[80,256]{1,0:T(8,128)S(1)}, f32[80,256]{1,0:T(8,128)S(1)}, u32[]{:S(2)}, u32[]{:S(2)}) collective-permute-start(f32[80,256]{1,0:T(8,128)S(1)} %get-tuple-element.37), channel_id=1, source_target_pairs={{0,1},{1,2},{2,3},{3,0},{4,5},{5,6},{6,7},{7,4},{8,9},{9,10},{10,1... | collective-permute-start | bytes 245768 | tf_op jit(solution)/shard_map/ppermute | solution.py:51
  21.6 7.5 %collective-permute-start.3 = (f32[80,256]{1,0:T(8,128)S(1)}, f32[80,256]{1,0:T(8,128)S(1)}, u32[]{:S(2)}, u32[]{:S(2)}) collective-permute-start(f32[80,256]{1,0:T(8,128)S(1)} %get-tuple-element.38), channel_id=1, source_target_pairs={{0,3},{1,0},{2,1},{3,2},{4,7},{5,4},{6,5},{7,6},{8,11},{9,8},{10,9... | collective-permute-start | bytes 245768 | tf_op jit(solution)/shard_map/ppermute | solution.py:51
  22.6 1.2 %collective-permute-start.4 = (f32[80,80]{1,0:T(8,128)S(1)}, f32[80,80]{1,0:T(8,128)S(1)}, u32[]{:S(2)}, u32[]{:S(2)}) collective-permute-start(f32[80,80]{1,0:T(8,128)S(1)} %get-tuple-element.36.gate_ref), channel_id=1, source_target_pairs={{0,4},{4,0},{8,12},{12,8},{16,20},{20,16},{24,28},{28,24},{1,5},{5... | collective-permute-start | bytes 76808 | tf_op jit(solution)/shard_map/ppermute | solution.py:464
  23.9 4.0 %collective-permute-start.5 = (f32[80,80]{1,0:T(8,128)S(1)}, f32[80,80]{1,0:T(8,128)S(1)}, u32[]{:S(2)}, u32[]{:S(2)}) collective-permute-start(f32[80,80]{1,0:T(8,128)S(1)} %add.15), channel_id=1, source_target_pairs={{0,8},{4,12},{8,0},{12,4},{16,24},{20,28},{24,16},{28,20},{1,9},{5... | collective-permute-start | bytes 76808 | tf_op jit(solution)/shard_map/ppermute | solution.py:464
  27.9 7.3 %collective-permute-start.8 = (f32[80,80]{1,0:T(8,128)S(1)}, f32[80,80]{1,0:T(8,128)S(1)}, u32[]{:S(2)}, u32[]{:S(2)}) collective-permute-start(f32[80,80]{1,0:T(8,128)S(1)} %add.16.gate_ref), channel_id=1, source_target_pairs={{0,16},{4,20},{8,24},{12,28},{16,0},{20,4},{24,8},{28,12},{1,17},{... | collective-permute-start | bytes 76808 | tf_op jit(solution)/shard_map/ppermute | solution.py:464
  31.5 7.7 %collective-permute-start.6 = (f32[5,8,256]{2,1,0:T(8,128)S(1)}, f32[5,8,256]{2,1,0:T(8,128)S(1)}, u32[]{:S(2)}, u32[]{:S(2)}) collective-permute-start(f32[5,8,256]{2,1,0:T(8,128)S(1)} %get-tuple-element.41), channel_id=1, source_target_pairs={{0,4},{4,8},{8,12},{12,16},{16,20},{20,24},{24,28},{28,0},{1,5},{5... | collective-permute-start | bytes 122888 | tf_op jit(solution)/shard_map/ppermute | solution.py:51
  31.6 7.6 %collective-permute-start.7 = (f32[5,8,256]{2,1,0:T(8,128)S(1)}, f32[5,8,256]{2,1,0:T(8,128)S(1)}, u32[]{:S(2)}, u32[]{:S(2)}) collective-permute-start(f32[5,8,256]{2,1,0:T(8,128)S(1)} %get-tuple-element.42), channel_id=1, source_target_pairs={{0,28},{4,0},{8,4},{12,8},{16,12},{20,16},{24,20},{28,24},{1,29},{... | collective-permute-start | bytes 122888 | tf_op jit(solution)/shard_map/ppermute | solution.py:51
  35.1 4.1 %collective-permute-start.9 = (f32[80,80]{1,0:T(8,128)S(1)}, f32[80,80]{1,0:T(8,128)S(1)}, u32[]{:S(2)}, u32[]{:S(2)}) collective-permute-start(f32[80,80]{1,0:T(8,128)S(1)} %add.17), channel_id=1, source_target_pairs={{0,1},{1,0},{2,3},{3,2},{4,5},{5,4},{6,7},{7,6},{8,9},{9,8},{10,11... | collective-permute-start | bytes 76808 | tf_op jit(solution)/shard_map/ppermute | solution.py:464
  39.3 5.4 %collective-permute-start.10 = (f32[80,256]{1,0:T(8,128)S(1)}, f32[80,256]{1,0:T(8,128)S(1)}, u32[]{:S(2)}, u32[]{:S(2)}) collective-permute-start(f32[80,256]{1,0:T(8,128)S(1)} %get-tuple-element.45), channel_id=1, source_target_pairs={{0,1},{1,2},{2,3},{3,0},{4,5},{5,6},{6,7},{7,4},{8,9},{9,10},{10,1... | collective-permute-start | bytes 245768 | tf_op jit(solution)/shard_map/ppermute | solution.py:51
  39.9 5.7 %collective-permute-start.11 = (f32[80,256]{1,0:T(8,128)S(1)}, f32[80,256]{1,0:T(8,128)S(1)}, u32[]{:S(2)}, u32[]{:S(2)}) collective-permute-start(f32[80,256]{1,0:T(8,128)S(1)} %get-tuple-element.46), channel_id=1, source_target_pairs={{0,3},{1,0},{2,1},{3,2},{4,7},{5,4},{6,5},{7,6},{8,11},{9,8},{10,9... | collective-permute-start | bytes 245768 | tf_op jit(solution)/shard_map/ppermute | solution.py:51
  47.8 15.1 %all-to-all-start = ((f32[32,1,128]{2,1,0:T(1,128)}), f32[32,1,128]{2,1,0:T(1,128)S(1)}, u32[]{:S(2)}, u32[]{:S(2)}) async-start(f32[32,1,128]{2,1,0:T(1,128)} %bitcast.4), calls=%async_computation | async-start | bytes 32768 | tf_op jit(solution)/shard_map/all_to_all | solution.py:536
  50.5 4.1 %collective-permute-start.12 = (f32[80,80]{1,0:T(8,128)S(1)}, f32[80,80]{1,0:T(8,128)S(1)}, u32[]{:S(2)}, u32[]{:S(2)}) collective-permute-start(f32[80,80]{1,0:T(8,128)S(1)} %add.18.gate_ref), channel_id=1, source_target_pairs={{0,2},{1,3},{2,0},{3,1},{4,6},{5,7},{6,4},{7,5},{8,10},{9,11},{10,... | collective-permute-start | bytes 76808 | tf_op jit(solution)/shard_map/ppermute | solution.py:464
  56.9 2.1 %copy-start.3 = (bf16[160,12288]{1,0:T(8,128)(2,1)S(1)}, bf16[160,12288]{1,0:T(8,128)(2,1)}, u32[]{:S(2)}) copy-start(bf16[160,12288]{1,0:T(8,128)(2,1)} %copy-done.2) | copy-start | bytes 11796484
  62.8 2.1 %copy-start.1 = (f32[96,80,128]{2,1,0:T(8,128)S(1)}, f32[96,80,128]{2,1,0:T(8,128)}, u32[]{:S(2)}) copy-start(f32[96,80,128]{2,1,0:T(8,128)} %copy-done) | copy-start | bytes 11796484

commit v2 on v1

--- a/solution.py
+++ b/solution.py
@@ -46,9 +46,28 @@
     return pltpu.CompilerParams(vmem_limit_bytes=mib << 20)
 
 
-def shifted(value, axis, steps):
+def ring_pairs(axis):
     count = lax.axis_size(axis)
-    return lax.ppermute(value, axis, [(s, (s + steps) % count) for s in range(count)])
+    partner = [(s, s ^ 1) for s in range(count)]
+    other = [(s, (s + 1 if s % 2 else s - 1) % count) for s in range(count)]
+    return partner, other
+
+
+def swap(values, axis):
+    partner, other = ring_pairs(axis)
+    return lax.ppermute(values[0], axis, partner), lax.ppermute(values[1], axis, other)
+
+
+def by_parity(axis, place):
+    odd = lax.rem(lax.axis_index(axis), 2)
+
+    @pl.when(odd == 0)
+    def _():
+        place(0)
+
+    @pl.when(odd == 1)
+    def _():
+        place(1)
 
 
 def moments(f):
@@ -89,7 +108,7 @@
     return post
 
 
-def emit_post(post, x, nx, post_ref, xup_ref, xdn_ref, yup_ref, ydn_ref):
+def emit_post(post, x, nx, post_ref, yup_ref, ydn_ref):
     ny = post_ref.shape[2]
     for i in range(NVEL):
         cz = velocity_table[i][2]
@@ -103,15 +122,31 @@
             ydn_ref[pl.ds(DOWN_Y.index(i) * nx + row, 1), :] = value[0:1, :]
 
 
-def emit_faces(nx, post_ref, xup_ref, xdn_ref):
-    for k, i in enumerate(UP_X):
-        xup_ref[k] = post_ref[i, nx - 1]
-    for k, i in enumerate(DOWN_X):
-        xdn_ref[k] = post_ref[i, 0]
+def emit_faces(nx, post_ref, faces):
+    def place(odd):
+        for k, i in enumerate(UP_X):
+            faces[odd][k] = post_ref[i, nx - 1]
+        for k, i in enumerate(DOWN_X):
+            faces[1 - odd][k] = post_ref[i, 0]
+
+    by_parity("gx", place)
+
+
+def sort_halos(xa_ref, xb_ref, ya_ref, yb_ref, xup_ref, xdn_ref, yup_ref, ydn_ref):
+    def place_x(odd):
+        xup_ref[...] = (xb_ref, xa_ref)[odd][...]
+        xdn_ref[...] = (xa_ref, xb_ref)[odd][...]
+
+    def place_y(odd):
+        yup_ref[...] = (yb_ref, ya_ref)[odd][...]
+        ydn_ref[...] = (ya_ref, yb_ref)[odd][...]
+
+    by_parity("gx", place_x)
+    by_parity("gy", place_y)
 
 
 def first_kernel(
-    f_hbm, om_hbm, so_hbm, post_ref, xup_ref, xdn_ref, yup_ref, ydn_ref, om_ref, so_ref, f_ref, sem
+    f_hbm, om_hbm, so_hbm, post_ref, xa_ref, xb_ref, yup_ref, ydn_ref, om_ref, so_ref, f_ref, sem
 ):
     nx = f_ref.shape[1]
     parts = sem.shape[0] - 2
@@ -132,7 +167,7 @@
 
     def step(x, carry):
         post = collide([f_ref[i, x] for i in range(NVEL)], om_ref[x], so_ref[x] > 0)
-        emit_post(post, x, nx, post_ref, xup_ref, xdn_ref, yup_ref, ydn_ref)
+        emit_post(post, x, nx, post_ref, yup_ref, ydn_ref)
         return carry
 
     for k in range(parts):
@@ -141,7 +176,7 @@
             omega.wait()
             solid.wait()
         lax.fori_loop(k * rows, (k + 1) * rows, step, 0)
-    emit_faces(nx, post_ref, xup_ref, xdn_ref)
+    emit_faces(nx, post_ref, (xa_ref, xb_ref))
 
 
 def streamed(x, nx, post_ref, xup_ref, xdn_ref, yup_ref, ydn_ref):
@@ -170,37 +205,39 @@
 
 def second_kernel(
     p_ref,
-    xu_ref,
-    xd_ref,
-    yu_ref,
-    yd_ref,
+    ra_ref,
+    rb_ref,
+    sa_ref,
+    sb_ref,
     om_ref,
     so_ref,
     gate_ref,
     post_ref,
-    xup_ref,
-    xdn_ref,
+    xa_ref,
+    xb_ref,
     yup_ref,
     ydn_ref,
+    *halos,
 ):
     nx = p_ref.shape[1]
+    sort_halos(ra_ref, rb_ref, sa_ref, sb_ref, *halos)
 
     def step(x, carry):
-        f = streamed(x, nx, p_ref, xu_ref, xd_ref, yu_ref, yd_ref)
+        f = streamed(x, nx, p_ref, *halos)
         post = collide(f, om_ref[x], so_ref[x] > 0)
-        emit_post(post, x, nx, post_ref, xup_ref, xdn_ref, yup_ref, ydn_ref)
+        emit_post(post, x, nx, post_ref, yup_ref, ydn_ref)
         return carry
 
     lax.fori_loop(0, nx, step, 0)
-    emit_faces(nx, post_ref, xup_ref, xdn_ref)
-
-
-def pack_kernel(xu_ref, xd_ref, yup_ref, ydn_ref, gate_ref, ou_ref, od_ref):
+    emit_faces(nx, post_ref, (xa_ref, xb_ref))
+
+
+def pack_kernel(xa_ref, xb_ref, yup_ref, ydn_ref, gate_ref, oa_ref, ob_ref):
     nx = yup_ref.shape[0] // len(UP_Y)
-    ny = xu_ref.shape[1]
-    ou_ref[...] = yup_ref[...]
-    od_ref[...] = ydn_ref[...]
-    for ids, out, row in ((UP_Y, ou_ref, ny - 1), (DOWN_Y, od_ref, 0)):
+    ny = xa_ref.shape[1]
+
+    def corners(ids, out, row, odd):
+        xu_ref, xd_ref = ((xb_ref, xa_ref), (xa_ref, xb_ref))[odd]
         for k, i in enumerate(ids):
             if velocity_table[i][0] == 1:
                 out[k * nx : k * nx + 1, :] = xu_ref[UP_X.index(i), row : row + 1, :]
@@ -208,8 +245,19 @@
                 at = k * nx + nx - 1
                 out[at : at + 1, :] = xd_ref[DOWN_X.index(i), row : row + 1, :]
 
-
-def gram_kernel(s_ref, basis_ref, snap_ref, gate_ref, a_ref, h_ref, g_ref):
+    def place(odd):
+        up, down = (oa_ref, ob_ref)[odd], (ob_ref, oa_ref)[odd]
+        up[...] = yup_ref[...]
+        down[...] = ydn_ref[...]
+        by_parity("gx", lambda x_odd: corners(UP_Y, up, ny - 1, x_odd))
+        by_parity("gx", lambda x_odd: corners(DOWN_Y, down, 0, x_odd))
+
+    by_parity("gy", place)
+
+
+def gram_kernel(
+    s_ref, basis_hbm, snap_hbm, gate_ref, a_ref, h_hbm, g_ref, basis_ref, snap_ref, h_ref, ins, outs
+):
     rank = basis_ref.shape[0]
     depth = basis_ref.shape[1]
     extra = snap_ref.shape[0]
@@ -221,7 +269,31 @@
     scale = jnp.broadcast_to(scale, (rank, 128))
     zero = jnp.zeros((cols - rank - extra, 8, 128), F32)
 
+    def load(q):
+        at = pl.ds(pl.multiple_of(q * 8, 8), 8)
+        return (
+            pltpu.make_async_copy(basis_hbm.at[:, at], basis_ref.at[:, at], ins.at[0, q]),
+            pltpu.make_async_copy(snap_hbm.at[:, at], snap_ref.at[:, at], ins.at[1, q]),
+        )
+
+    def save(q):
+        at = pl.ds(pl.multiple_of(q * 1024, 1024), 1024)
+        return pltpu.make_async_copy(h_ref.at[:, at], h_hbm.at[:, at], outs.at[q])
+
+    def begin(q, carry):
+        for copy in load(q):
+            copy.start()
+        return carry
+
+    def finish(q, carry):
+        save(q).wait()
+        return carry
+
+    lax.fori_loop(0, depth // 8, begin, 0)
+
     def step(q, carry):
+        for copy in load(q):
+            copy.wait()
         r = pl.multiple_of(q * 8, 8)
         top = jnp.swapaxes(basis_ref[:, pl.ds(r, 8), :], 0, 1)
         low = jnp.concatenate([snap_ref[:, pl.ds(r, 8), :], zero], axis=0)
@@ -233,6 +305,7 @@
             high = rows.astype(BF16)
             h_ref[0:cols, at] = high
             h_ref[cols : 2 * cols, at] = (rows - high.astype(F32)).astype(BF16)
+        save(q).start()
         return carry
 
     lax.fori_loop(0, depth // 8, step, 0)
@@ -248,6 +321,7 @@
         eye, cross, (((1,), (1,)), ((), ())), precision=HIGHEST, preferred_element_type=F32
     )
     g_ref[...] = acc[:cols, :] + cross + flipped
+    lax.fori_loop(0, depth // 8, finish, 0)
 
 
 def factor_kernel(inv_rows, g_ref, u_ref, li_ref, w_ref):
@@ -300,7 +374,7 @@
         w_ref[8 * b : 8 * b + 8, :] = wide[:, : 3 * cols]
 
 
-def rotate_kernel(w_ref, h_ref, o_ref, out_ref, sem):
+def rotate_kernel(w_ref, h_hbm, o_ref, h_ref, out_ref, ins, sem):
     cols = w_ref.shape[0]
     depth = out_ref.shape[1]
     weight = w_ref[...].astype(BF16)
@@ -309,7 +383,18 @@
         at = pl.ds(pl.multiple_of(q * 8, 8), 8)
         return pltpu.make_async_copy(out_ref.at[:, at, :], o_ref.at[:, at, :], sem.at[q])
 
+    def load(q):
+        at = pl.ds(pl.multiple_of(q * 1024, 1024), 1024)
+        return pltpu.make_async_copy(h_hbm.at[:, at], h_ref.at[:, at], ins.at[q])
+
+    def begin(q, carry):
+        load(q).start()
+        return carry
+
+    lax.fori_loop(0, depth // 8, begin, 0)
+
     def step(q, carry):
+        load(q).wait()
         at = pl.ds(pl.multiple_of(q * 1024, 1024), 1024)
         high = h_ref[0:cols, at]
         low = h_ref[cols : 2 * cols, at]
@@ -334,10 +419,11 @@
 
 
 def final_kernel(
-    p_ref, xu_ref, xd_ref, yu_ref, yd_ref, so_ref, a_ref, f_hbm, c_ref, v_ref, vel_ref, f_ref, sem
+    p_ref, ra_ref, rb_ref, sa_ref, sb_ref, so_ref, a_ref, gate_ref, f_hbm, c_ref, v_ref, vel_ref, f_ref, sem, *halos
 ):
     nx, ny, nz = p_ref.shape[1:]
     nxc, nyc = nx // 2, ny // 2
+    sort_halos(ra_ref, rb_ref, sa_ref, sb_ref, *halos)
 
     def copy(xc):
         at = pl.ds(2 * xc, 2)
@@ -351,7 +437,7 @@
         total = [None] * 3
         for t in range(2):
             x = 2 * xc + t
-            f = streamed(x, nx, p_ref, xu_ref, xd_ref, yu_ref, yd_ref)
+            f = streamed(x, nx, p_ref, *halos)
             for i in range(NVEL):
                 f_ref[i, x] = f[i]
             _, u = moments(f)
@@ -398,54 +484,94 @@
     lax.fori_loop(0, nxc, finish, 0)
 
 
-def last_kernel(inv_rows, v_ref, li_ref, u_ref, a_ref, c_ref, q_ref, uo_ref, o_ref, row_ref, sem):
+def last_kernel(
+    inv_rows,
+    v_ref,
+    li_ref,
+    u_ref,
+    s_ref,
+    c_ref,
+    basis_hbm,
+    snap_hbm,
+    q_ref,
+    uo_ref,
+    o_ref,
+    basis_ref,
+    snap_ref,
+    tall_ref,
+    row_ref,
+    ins,
+    sem,
+):
     cols = li_ref.shape[0]
     known = cols - 1
-    depth = c_ref.shape[0]
+    rank, depth = basis_ref.shape[:2]
+    extra = snap_ref.shape[0]
+    parts = ins.shape[1]
+    size = depth // parts
+    loads = []
+    for k in range(parts):
+        at = pl.ds(k * size, size)
+        loads.append(
+            (
+                pltpu.make_async_copy(basis_hbm.at[:, at], basis_ref.at[:, at], ins.at[0, k]),
+                pltpu.make_async_copy(snap_hbm.at[:, at], snap_ref.at[:, at], ins.at[1, k]),
+            )
+        )
+        for copy in loads[-1]:
+            copy.start()
     line = jnp.sum(v_ref[...], axis=0, keepdims=True)[:, :cols] * inv_rows
     across = lax.broadcasted_iota(jnp.int32, (1, cols), 1)
     norm = jnp.sum(jnp.where(across == known, line, 0.0), axis=1, keepdims=True)
     inverse = li_ref[...]
     coef = jnp.sum(inverse * jnp.where(across == known, 0.0, line), axis=1, keepdims=True)
-    pivot = lax.rsqrt(norm - jnp.sum(coef * coef, axis=0, keepdims=True))
     left = norm - jnp.sum(coef * coef, axis=0, keepdims=True)
+    pivot = lax.rsqrt(left)
     col_id = lax.broadcasted_iota(jnp.int32, (cols, cols), 1)
     row_id = lax.broadcasted_iota(jnp.int32, (cols, cols), 0)
     edge = jnp.where(row_id == known, left * pivot, coef)
     uo_ref[...] = jnp.where(col_id == known, edge, u_ref[...])
     weight = jnp.sum(inverse * coef, axis=0, keepdims=True) * (-pivot)
-    diag = jnp.where(row_id == col_id, weight, 0.0)
-    tall = jnp.sum(diag, axis=1, keepdims=True)
-    tall = jnp.broadcast_to(tall, (cols, 128))
-
-    def step(r, carry):
-        part = jnp.sum(a_ref[r] * tall, axis=0, keepdims=True)
-        row_ref[pl.ds(r, 1), :] = part + c_ref[pl.ds(r, 1), :] * pivot
-        return carry
-
-    lax.fori_loop(0, depth, step, 0, unroll=8)
+    scale = jnp.concatenate([s_ref[...], jnp.ones((1, cols - rank), F32)], axis=1)
+    diag = jnp.where(row_id == col_id, weight * scale, 0.0)
+    tall_ref[...] = jnp.broadcast_to(jnp.sum(diag, axis=1, keepdims=True), (cols, 128))
+
+    def step(q, carry):
+        at = pl.ds(pl.multiple_of(q * 16, 16), 16)
+        total = [c_ref[at, :] * pivot] + [None] * 3
+        for k in range(rank + extra):
+            value = basis_ref[k, at, :] if k < rank else snap_ref[k - rank, at, :]
+            value = value * tall_ref[k : k + 1, :]
+            total[k % 4] = value if total[k % 4] is None else total[k % 4] + value
+        row_ref[at, :] = (total[0] + total[1]) + (total[2] + total[3])
+        return carry
+
+    for k in range(parts):
+        for copy in loads[k]:
+            copy.wait()
+        lax.fori_loop(k * size // 16, (k + 1) * size // 16, step, 0)
     copy = pltpu.make_async_copy(row_ref, o_ref.at[known], sem)
     copy.start()
     copy.wait()
 
 
+def in_hbm(value):
+    return pltpu.with_memory_space_constraint(value, pltpu.HBM)
+
+
 def shape(dims, dtype=F32):
     return jax.ShapeDtypeStruct(dims, dtype)
 
 
-def halo_x(xup, xdn):
-    return shifted(xup, "gx", 1), shifted(xdn, "gx", -1)
-
-
-def halo_y(xu, xd, yup, ydn, gate):
-    send_up, send_dn = pl.pallas_call(
+def halo_y(xa, xb, yup, ydn, gate):
+    sends = pl.pallas_call(
         pack_kernel,
         out_shape=(shape(yup.shape), shape(ydn.shape)),
         in_specs=[VMEM] * 4 + [ANY],
         name="pack",
         compiler_params=params(2),
-    )(xu, xd, yup, ydn, gate)
-    return shifted(send_up, "gy", 1), shifted(send_dn, "gy", -1)
+    )(xa, xb, yup, ydn, gate)
+    return swap(sends, "gy")
 
 
 def rounds():
@@ -481,87 +607,106 @@
         shape((edges, nz)),
         shape((edges, nz)),
     )
-    post, xup, xdn, yup, ydn, omega, solid = pl.pallas_call(
+    halos = [pltpu.VMEM(post_shapes[k].shape, F32) for k in range(1, 5)]
+    post, xa, xb, yup, ydn, omega, solid = pl.pallas_call(
         first_kernel,
         out_shape=post_shapes + (shape((nx, ny, nz)), shape((nx, ny, nz), jnp.int32)),
         in_specs=[HBM] * 3,
         scratch_shapes=[pltpu.VMEM((NVEL, nx, ny, nz), F32), pltpu.SemaphoreType.DMA((6,))],
         name="first",
         compiler_params=params(6),
-    )(populations, relax_rate, solid_mask)
-    xu, xd = halo_x(xup, xdn)
+    )(*[in_hbm(value) for value in (populations, relax_rate, solid_mask)])
+    xa, xb = swap((xa, xb), "gx")
+    weights = singular_values.reshape(1, rank)
+    modes = in_hbm(basis.reshape(rank, depth, 128))
+    earlier = in_hbm(snapshots.reshape(extra, depth, 128))
+    blocks = depth // 8
     rows, halves, gram = pl.pallas_call(
         gram_kernel,
         out_shape=(
-            pltpu.VMEM((depth, cols, 128), F32),
-            pltpu.VMEM((2 * cols, depth * 128), BF16),
+            shape((depth, cols, 128)),
+            pltpu.HBM((2 * cols, depth * 128), BF16),
             shape((cols, cols)),
         ),
-        in_specs=[VMEM] * 3 + [ANY],
+        in_specs=[VMEM, HBM, HBM, ANY],
+        out_specs=(VMEM, HBM, VMEM),
+        scratch_shapes=[
+            pltpu.VMEM((rank, depth, 128), F32),
+            pltpu.VMEM((extra, depth, 128), F32),
+            pltpu.VMEM((2 * cols, depth * 128), BF16),
+            pltpu.SemaphoreType.DMA((2, blocks)),
+            pltpu.SemaphoreType.DMA((blocks,)),
+        ],
         name="gram",
-        compiler_params=params(4),
-    )(
-        singular_values.reshape(1, rank),
-        basis.reshape(rank, depth, 128),
-        snapshots.reshape(extra, depth, 128),
-        omega,
-    )
-    yu, yd = halo_y(xu, xd, yup, ydn, gram)
+        compiler_params=params(12),
+    )(weights, modes, earlier, omega)
+    ya, yb = halo_y(xa, xb, yup, ydn, gram)
     steps = rounds()
     gram = exchange(gram, steps[:2])
-    post, xup, xdn, yup, ydn = pl.pallas_call(
+    post, xa, xb, yup, ydn = pl.pallas_call(
         second_kernel,
         out_shape=post_shapes,
         in_specs=[VMEM] * 7 + [ANY],
+        scratch_shapes=halos,
         name="second",
         compiler_params=params(4),
-    )(post, xu, xd, yu, yd, omega, solid, gram)
-    xu, xd = halo_x(xup, xdn)
-    gram = exchange(gram, steps[2:4])
-    yu, yd = halo_y(xu, xd, yup, ydn, gram)
-    gram = exchange(gram, steps[4:])
-    field, coarse, line = pl.pallas_call(
-        final_kernel,
-        out_shape=(shape((NVEL, nx, ny, nz)), shape((depth, 128)), shape((n_dev, 128))),
-        in_specs=[VMEM] * 7,
-        out_specs=(ANY, VMEM, VMEM),
-        scratch_shapes=[
-            pltpu.VMEM((nz // 128, 3 * (nx // 2) * ny, 128), F32),
-            pltpu.VMEM((NVEL, nx, ny, nz), F32),
-            pltpu.SemaphoreType.DMA((nx // 2,)),
-        ],
-        name="final",
-        compiler_params=params(6),
-    )(post, xu, xd, yu, yd, solid, rows)
-    lines = lax.all_to_all(line, ("gx", "gy"), 0, 0, tiled=True)
+    )(post, xa, xb, ya, yb, omega, solid, gram)
+    xa, xb = swap((xa, xb), "gx")
+    gram = exchange(gram, steps[2:-1])
+    ya, yb = halo_y(xa, xb, yup, ydn, gram)
+    gram = exchange(gram, steps[-1:])
     upper, inverse, split = pl.pallas_call(
         lambda *refs: factor_kernel(inv_rows, *refs),
         out_shape=(shape((cols, cols)), shape((cols, cols)), shape((cols, 3 * cols))),
         name="factor",
         compiler_params=params(4),
     )(gram)
+    field, coarse, line = pl.pallas_call(
+        final_kernel,
+        out_shape=(shape((NVEL, nx, ny, nz)), shape((depth, 128)), shape((n_dev, 128))),
+        in_specs=[VMEM] * 7 + [ANY],
+        out_specs=(ANY, VMEM, VMEM),
+        scratch_shapes=[
+            pltpu.VMEM((nz // 128, 3 * (nx // 2) * ny, 128), F32),
+            pltpu.VMEM((NVEL, nx, ny, nz), F32),
+            pltpu.SemaphoreType.DMA((nx // 2,)),
+        ]
+        + halos,
+        name="final",
+        compiler_params=params(6),
+    )(post, xa, xb, ya, yb, solid, rows, inverse)
+    lines = lax.all_to_all(line, ("gx", "gy"), 0, 0, tiled=True)
     rotated = pl.pallas_call(
         rotate_kernel,
         out_shape=shape((cols, depth, 128)),
-        in_specs=[VMEM] * 2,
+        in_specs=[VMEM, HBM],
         out_specs=ANY,
         scratch_shapes=[
+            pltpu.VMEM((2 * cols, depth * 128), BF16),
             pltpu.VMEM((cols, depth, 128), F32),
-            pltpu.SemaphoreType.DMA((depth // 8,)),
+            pltpu.SemaphoreType.DMA((blocks,)),
+            pltpu.SemaphoreType.DMA((blocks,)),
         ],
         name="rotate",
-        compiler_params=params(8),
-    )(split, halves)
+        compiler_params=params(12),
+    )(split, in_hbm(halves))
     upper, rotated = pl.pallas_call(
         lambda *refs: last_kernel(inv_rows, *refs),
         out_shape=(shape((cols, cols)), shape((cols, depth, 128))),
-        in_specs=[VMEM] * 5 + [ANY],
+        in_specs=[VMEM] * 5 + [HBM] * 2 + [ANY],
         out_specs=(VMEM, ANY),
-        scratch_shapes=[pltpu.VMEM((depth, 128), F32), pltpu.SemaphoreType.DMA],
-        input_output_aliases={5: 1},
+        scratch_shapes=[
+            pltpu.VMEM((rank, depth, 128), F32),
+            pltpu.VMEM((extra, depth, 128), F32),
+            pltpu.VMEM((cols, 128), F32),
+            pltpu.VMEM((depth, 128), F32),
+            pltpu.SemaphoreType.DMA((2, 3)),
+            pltpu.SemaphoreType.DMA,
+        ],
+        input_output_aliases={7: 1},
         name="last",
-        compiler_params=params(4),
-    )(lines, inverse, upper, rows, coarse, rotated)
+        compiler_params=params(8),
+    )(lines, inverse, upper, weights, coarse, modes, earlier, rotated)
     return field, upper, rotated.reshape((cols,) + tail)
 
 

time: 67.2 us -> 58.3 us (0.87)
  local copies, waits for them, and re-layouts: 12.2 us -> 0.66 us
  Pallas kernels: 19 us -> 24 us
  waiting for transfers between devices: 14.1 us -> 12.5 us
    unnamed x20 -> x4, local copies, waits for them, and re-layouts: 12.2 us -> 0.66 us
    ppermute x8, waiting for transfers between devices: 3.37 us -> 0.03 us  [the longest x4 0.02 us: swap(): lax.ppermute(values[1], axis, other)]
    all_to_all x1, waiting for transfers between devices: 0.01 us -> 2.22 us  [on_device(): lines = lax.all_to_all(line, ('gx', 'gy'), 0, 0, tiled=True)]
    pallas_call x1, Pallas kernels: 1.93 us -> 3.64 us  [on_device(): pl.pallas_call(lambda *refs: last_kernel(inv_rows, *refs), out_shape=(sha...]
    all_to_all x1, starting transfers between devices: 2.69 us -> 4.27 us  [on_device(): lines = lax.all_to_all(line, ('gx', 'gy'), 0, 0, tiled=True)]
    pallas_call x1, Pallas kernels: 3.55 us -> 4.93 us  [on_device(): pl.pallas_call(gram_kernel, out_shape=(shape((depth, cols, 128)), pltpu.H...]
    ppermute x8, starting transfers between devices: 14.2 us -> 12.8 us  [the longest x4 9.09 us: swap(): lax.ppermute(values[1], axis, other)]
    pallas_call x1, Pallas kernels: 3.8 us -> 4.88 us  [on_device(): pl.pallas_call(rotate_kernel, out_shape=shape((cols, depth, 128)), in_spe...]
  transfers between devices with their start and end apart: 14 -> 14, of which waited for: 6 -> 5; matrix products, arithmetic and copies ran while one was open for 0% -> 0% of each run, Pallas kernels for 18% -> 25%
where the time goes in v2:
time: 58.3 us; the launch traced here: 58.1 us
  Pallas kernels  24 us (41%)
  starting transfers between devices  20.2 us (35%)
  waiting for transfers between devices  12.5 us (21%)
  between operations  0.79 us (1%)
  local copies, waits for them, and re-layouts  0.66 us (1%)
    ppermute x5, waiting for transfers between devices, exchange(): value = value + lax.ppermute(value, axis, pairs)  10.2 us
    ppermute x4, starting transfers between devices, swap(): lax.ppermute(values[1], axis, other)  9.09 us
    pallas_call x1, Pallas kernels, on_device(): pl.pallas_call(gram_kernel, out_shape=(shape((depth, cols, 128)), pltpu.H...  4.93 us
    pallas_call x1, Pallas kernels, on_device(): pl.pallas_call(rotate_kernel, out_shape=shape((cols, depth, 128)), in_spe...  4.88 us
    all_to_all x1, starting transfers between devices, on_device(): lines = lax.all_to_all(line, ('gx', 'gy'), 0, 0, tiled=True)  4.27 us
    ppermute x4, starting transfers between devices, swap(): lax.ppermute(values[0], axis, partner)  3.75 us
    pallas_call x1, Pallas kernels, on_device(): pl.pallas_call(lambda *refs: last_kernel(inv_rows, *refs), out_shape=(sha...  3.64 us
    pallas_call x1, Pallas kernels, on_device(): pl.pallas_call(first_kernel, out_shape=post_shapes + (shape((nx, ny, nz))...  3.4 us
  transfers between devices with their start and end apart: 14, of which 5 were waited for; matrix products, arithmetic and copies ran while one was open for 0% of the time, Pallas kernels for 25%

profile of v2, /device:TPU:0, one launch (start us, length us, event | category | flops | bytes accessed | tf_op | source)
XLA Modules:
  0.0 58.1 jit_solution(14019161504588011110)
XLA Ops:
  0.6 3.4 %first.1 = (f32[19,16,8,256]{3,2,1,0:T(8,128)S(1)}, f32[5,8,256]{2,1,0:T(8,128)S(1)}, f32[5,8,256]{2,1,0:T(8,128)S(1)}, f32[80,256]{1,0:T(8,128)S(1)}, f32[80,25...) custom-call(f32[19,16,8,256]{3,2,1,0:T(8,128)} %f_hbm.1, f32[16,8,256]{2,1,0:T(8,128)} %om_hbm.1, ...), custom_call_target="tpu_custom_call" | custom-call | tf_op jit(solution)/shard_map/first/pallas_call | solution.py:611
  4.0 0.6 collective-permute-start
  4.6 4.7 %collective-permute-start.1 = (f32[5,8,256]{2,1,0:T(8,128)S(1)}, f32[5,8,256]{2,1,0:T(8,128)S(1)}, u32[]{:S(2)}, u32[]{:S(2)}) collective-permute-start(f32[5,8,256]{2,1,0:T(8,128)S(1)} %get-tuple-element.32), channel_id=1, source_target_pairs={{0,28},{4,8},{8,4},{12,16},{16,12},{20,24},{24,20},{28,0},{1,29},{... | collective-permute-start | bytes 122888 | tf_op jit(solution)/shard_map/ppermute | solution.py:58
  9.3 0.0 copy-start
  9.3 0.7 %copy-done = f32[64]{0:T(128)S(1)} copy-done((f32[64]{0:T(128)S(1)}, f32[64]{0:T(128)}, u32[]{:S(2)}) %copy-start) | copy-done | bytes 280
  10.0 4.9 %gram.1 = (f32[96,80,128]{2,1,0:T(8,128)S(1)}, bf16[160,12288]{1,0:T(8,128)(2,1)}, f32[80,80]{1,0:T(8,128)S(1)}) custom-call(f32[1,64]{1,0:T(1,128)S(1)} %bitcast.9, f32[64,96,128]{2,1,0:T(8,128)} %bitcast.12, f32[15,96,128]{2,1,0:T(8,128)} %bitcast.14, f32[16,8,256]{2,1,0:T(8,128)S(1)} %get-tuple-element.35.gate_ref.om_ref), custom_call_target="tpu_custom_call" | custom-call | tf_op jit(solution)/shard_map/gram/pallas_call | solution.py:624
  14.9 0.0 collective-permute-done.xa_ref.ra_ref
  14.9 0.0 collective-permute-done.1.xb_ref.rb_ref
  15.0 1.6 %collective-permute-start.2 = (f32[80,256]{1,0:T(8,128)S(1)}, f32[80,256]{1,0:T(8,128)S(1)}, u32[]{:S(2)}, u32[]{:S(2)}) collective-permute-start(f32[80,256]{1,0:T(8,128)S(1)} %get-tuple-element.37), channel_id=1, source_target_pairs={{0,1},{1,0},{2,3},{3,2},{4,5},{5,4},{6,7},{7,6},{8,9},{9,8},{10,11... | collective-permute-start | bytes 245768 | tf_op jit(solution)/shard_map/ppermute | solution.py:58
  16.5 1.5 %collective-permute-start.3 = (f32[80,256]{1,0:T(8,128)S(1)}, f32[80,256]{1,0:T(8,128)S(1)}, u32[]{:S(2)}, u32[]{:S(2)}) collective-permute-start(f32[80,256]{1,0:T(8,128)S(1)} %get-tuple-element.38), channel_id=1, source_target_pairs={{0,3},{1,2},{2,1},{3,0},{4,7},{5,6},{6,5},{7,4},{8,11},{9,10},{10,... | collective-permute-start | bytes 245768 | tf_op jit(solution)/shard_map/ppermute | solution.py:58
  18.0 0.0 collective-permute-start.4
  18.0 1.2 %collective-permute-done.4 = f32[80,80]{1,0:T(8,128)S(1)} collective-permute-done((f32[80,80]{1,0:T(8,128)S(1)}, f32[80,80]{1,0:T(8,128)S(1)}, u32[]{:S(2)}, u32[]{:S(2)}) %collective-permute-start.4) | collective-permute-done | bytes 25632 | tf_op jit(solution)/shard_map/ppermute | solution.py:590
  19.2 0.0 collective-permute-start.5
  19.2 4.0 %collective-permute-done.5 = f32[80,80]{1,0:T(8,128)S(1)} collective-permute-done((f32[80,80]{1,0:T(8,128)S(1)}, f32[80,80]{1,0:T(8,128)S(1)}, u32[]{:S(2)}, u32[]{:S(2)}) %collective-permute-start.5) | collective-permute-done | bytes 25632 | tf_op jit(solution)/shard_map/ppermute | solution.py:590
  23.3 0.0 collective-permute-start.8
  23.3 0.0 collective-permute-done.2.sa_ref
  23.3 0.0 collective-permute-done.3.sb_ref
  23.3 2.5 %second.1 = (f32[19,16,8,256]{3,2,1,0:T(8,128)S(1)}, f32[5,8,256]{2,1,0:T(8,128)S(1)}, f32[5,8,256]{2,1,0:T(8,128)S(1)}, f32[80,256]{1,0:T(8,128)S(1)}, f32[80,256]{1,0:T(8,128)S(1)}) custom-call(f32[19,16,8,256]{3,2,1,0:T(8,128)S(1)} %get-tuple-element.30.p_ref, f32[5,8,256]{2,1,0:T(8,128)S(1)} %collective-permute-done.xa_ref.ra_ref, ...), custom_call_target="tpu_custom_call" | custom-call | tf_op jit(solution)/shard_map/second/pallas_call | solution.py:646
  25.8 0.1 collective-permute-start.6
  25.9 2.4 %collective-permute-start.7 = (f32[5,8,256]{2,1,0:T(8,128)S(1)}, f32[5,8,256]{2,1,0:T(8,128)S(1)}, u32[]{:S(2)}, u32[]{:S(2)}) collective-permute-start(f32[5,8,256]{2,1,0:T(8,128)S(1)} %get-tuple-element.42), channel_id=1, source_target_pairs={{0,28},{4,8},{8,4},{12,16},{16,12},{20,24},{24,20},{28,0},{1,29},{... | collective-permute-start | bytes 122888 | tf_op jit(solution)/shard_map/ppermute | solution.py:58
  28.3 0.0 collective-permute-done.8
  28.3 1.6 %collective-permute-start.9 = (f32[80,80]{1,0:T(8,128)S(1)}, f32[80,80]{1,0:T(8,128)S(1)}, u32[]{:S(2)}, u32[]{:S(2)}) collective-permute-start(f32[80,80]{1,0:T(8,128)S(1)} %add.17), channel_id=1, source_target_pairs={{0,1},{1,0},{2,3},{3,2},{4,5},{5,4},{6,7},{7,6},{8,9},{9,8},{10,11... | collective-permute-start | bytes 76808 | tf_op jit(solution)/shard_map/ppermute | solution.py:590
  29.9 2.5 %collective-permute-done.9 = f32[80,80]{1,0:T(8,128)S(1)} collective-permute-done((f32[80,80]{1,0:T(8,128)S(1)}, f32[80,80]{1,0:T(8,128)S(1)}, u32[]{:S(2)}, u32[]{:S(2)}) %collective-permute-start.9) | collective-permute-done | bytes 25632 | tf_op jit(solution)/shard_map/ppermute | solution.py:590
  32.4 0.0 collective-permute-done.6.xa_ref.ra_ref
  32.4 0.0 collective-permute-done.7.xb_ref.rb_ref
  32.4 1.6 %collective-permute-start.10 = (f32[80,256]{1,0:T(8,128)S(1)}, f32[80,256]{1,0:T(8,128)S(1)}, u32[]{:S(2)}, u32[]{:S(2)}) collective-permute-start(f32[80,256]{1,0:T(8,128)S(1)} %get-tuple-element.45), channel_id=1, source_target_pairs={{0,1},{1,0},{2,3},{3,2},{4,5},{5,4},{6,7},{7,6},{8,9},{9,8},{10,11... | collective-permute-start | bytes 245768 | tf_op jit(solution)/shard_map/ppermute | solution.py:58
  34.0 0.5 collective-permute-start.11
  34.5 1.5 %collective-permute-start.12 = (f32[80,80]{1,0:T(8,128)S(1)}, f32[80,80]{1,0:T(8,128)S(1)}, u32[]{:S(2)}, u32[]{:S(2)}) collective-permute-start(f32[80,80]{1,0:T(8,128)S(1)} %add.18.gate_ref), channel_id=1, source_target_pairs={{0,2},{1,3},{2,0},{3,1},{4,6},{5,7},{6,4},{7,5},{8,10},{9,11},{10,... | collective-permute-start | bytes 76808 | tf_op jit(solution)/shard_map/ppermute | solution.py:590
  36.0 2.5 %collective-permute-done.12 = f32[80,80]{1,0:T(8,128)S(1)} collective-permute-done((f32[80,80]{1,0:T(8,128)S(1)}, f32[80,80]{1,0:T(8,128)S(1)}, u32[]{:S(2)}, u32[]{:S(2)}) %collective-permute-start.12) | collective-permute-done | bytes 25632 | tf_op jit(solution)/shard_map/ppermute | solution.py:590
  38.5 2.3 %factor.1 = (f32[80,80]{1,0:T(8,128)S(1)}, f32[80,80]{1,0:T(8,128)S(1)}, f32[80,240]{1,0:T(8,128)S(1)}) custom-call(f32[80,80]{1,0:T(8,128)S(1)} %add.19.refs_0_), custom_call_target="tpu_custom_call" | custom-call | tf_op jit(solution)/shard_map/factor/pallas_call | solution.py:658
  40.8 0.0 collective-permute-done.10.sa_ref
  40.8 0.0 collective-permute-done.11.sb_ref
  40.9 2.2 %final.1 = (f32[19,16,8,256]{3,2,1,0:T(8,128)}, f32[96,128]{1,0:T(8,128)S(1)}, f32[32,128]{1,0:T(8,128)}) custom-call(f32[19,16,8,256]{3,2,1,0:T(8,128)S(1)} %get-tuple-element.40.p_ref, f32[5,8,256]{2,1,0:T(8,128)S(1)} %collective-permute-done.6.xa_ref.ra_ref, f32[5,8,256]{2,1,0:T(8,128)S(1)} %collective-permute-done.7.xb_ref.rb_ref, ...), custom_call_target="tpu_custom_call" | custom-call | tf_op jit(solution)/shard_map/final/pallas_call | solution.py:664
  43.1 4.3 %all-to-all-start = ((f32[32,1,128]{2,1,0:T(1,128)}), f32[32,1,128]{2,1,0:T(1,128)S(1)}, u32[]{:S(2)}, u32[]{:S(2)}) async-start(f32[32,1,128]{2,1,0:T(1,128)} %bitcast.4), calls=%async_computation | async-start | bytes 32768 | tf_op jit(solution)/shard_map/all_to_all | solution.py:678
  47.3 0.0 copy-start.1
  47.3 4.9 %rotate.1.refs_7_ = f32[80,96,128]{2,1,0:T(8,128)} custom-call(f32[80,240]{1,0:T(8,128)S(1)} %get-tuple-element.53.w_ref, bf16[160,12288]{1,0:T(8,128)(2,1)} %get-tuple-element.54.h_hbm), custom_call_target="tpu_custom_call" | custom-call | tf_op jit(solution)/shard_map/rotate/pallas_call | solution.py:679
  52.2 2.2 %all-to-all-done = f32[32,1,128]{2,1,0:T(1,128)S(1)} async-done(((f32[32,1,128]{2,1,0:T(1,128)}), f32[32,1,128]{2,1,0:T(1,128)S(1)}, u32[]{:S(2)}, u32[]{:S(2)}) %all-to-all-start) | async-done | bytes 16416 | tf_op jit(solution)/shard_map/all_to_all | solution.py:678
  54.5 0.0 copy-done.1
  54.5 3.6 %last.1 = (f32[80,80]{1,0:T(8,128)}, f32[80,96,128]{2,1,0:T(8,128)}) custom-call(f32[32,128]{1,0:T(8,128)S(1)} %bitcast.8, f32[80,80]{1,0:T(8,128)S(1)} %get-tuple-element.48.gate_ref.refs_1_, f32[80,80]{1,0:T(8,128)S(1)} %get-tuple-element.51.refs_2_, f32[1,64]{1,0:T(1,128)S(1)} %bitcast.10, ...), custom_call_target="tpu_custom_call", output_to_operand_aliasing={{1}: (7, {})} | custom-call | tf_op jit(solution)/shard_map/last/pallas_call | solution.py:693
  (7 shorter events, 0.1 us)
Async XLA Ops:
  4.0 10.9 %collective-permute-start = (f32[5,8,256]{2,1,0:T(8,128)S(1)}, f32[5,8,256]{2,1,0:T(8,128)S(1)}, u32[]{:S(2)}, u32[]{:S(2)}) collective-permute-start(f32[5,8,256]{2,1,0:T(8,128)S(1)} %get-tuple-element.31), channel_id=1, source_target_pairs={{0,4},{4,0},{8,12},{12,8},{16,20},{20,16},{24,28},{28,24},{1,5},{5... | collective-permute-start | bytes 122888 | tf_op jit(solution)/shard_map/ppermute | solution.py:58
  4.6 10.3 %collective-permute-start.1 = (f32[5,8,256]{2,1,0:T(8,128)S(1)}, f32[5,8,256]{2,1,0:T(8,128)S(1)}, u32[]{:S(2)}, u32[]{:S(2)}) collective-permute-start(f32[5,8,256]{2,1,0:T(8,128)S(1)} %get-tuple-element.32), channel_id=1, source_target_pairs={{0,28},{4,8},{8,4},{12,16},{16,12},{20,24},{24,20},{28,0},{1,29},{... | collective-permute-start | bytes 122888 | tf_op jit(solution)/shard_map/ppermute | solution.py:58
  9.3 0.7 %copy-start = (f32[64]{0:T(128)S(1)}, f32[64]{0:T(128)}, u32[]{:S(2)}) copy-start(f32[64]{0:T(128)} %param.9) | copy-start | bytes 772
  15.0 8.3 %collective-permute-start.2 = (f32[80,256]{1,0:T(8,128)S(1)}, f32[80,256]{1,0:T(8,128)S(1)}, u32[]{:S(2)}, u32[]{:S(2)}) collective-permute-start(f32[80,256]{1,0:T(8,128)S(1)} %get-tuple-element.37), channel_id=1, source_target_pairs={{0,1},{1,0},{2,3},{3,2},{4,5},{5,4},{6,7},{7,6},{8,9},{9,8},{10,11... | collective-permute-start | bytes 245768 | tf_op jit(solution)/shard_map/ppermute | solution.py:58
  16.5 6.7 %collective-permute-start.3 = (f32[80,256]{1,0:T(8,128)S(1)}, f32[80,256]{1,0:T(8,128)S(1)}, u32[]{:S(2)}, u32[]{:S(2)}) collective-permute-start(f32[80,256]{1,0:T(8,128)S(1)} %get-tuple-element.38), channel_id=1, source_target_pairs={{0,3},{1,2},{2,1},{3,0},{4,7},{5,6},{6,5},{7,4},{8,11},{9,10},{10,... | collective-permute-start | bytes 245768 | tf_op jit(solution)/shard_map/ppermute | solution.py:58
  18.0 1.2 %collective-permute-start.4 = (f32[80,80]{1,0:T(8,128)S(1)}, f32[80,80]{1,0:T(8,128)S(1)}, u32[]{:S(2)}, u32[]{:S(2)}) collective-permute-start(f32[80,80]{1,0:T(8,128)S(1)} %get-tuple-element.36.gate_ref), channel_id=1, source_target_pairs={{0,4},{4,0},{8,12},{12,8},{16,20},{20,16},{24,28},{28,24},{1,5},{5... | collective-permute-start | bytes 76808 | tf_op jit(solution)/shard_map/ppermute | solution.py:590
  19.2 4.0 %collective-permute-start.5 = (f32[80,80]{1,0:T(8,128)S(1)}, f32[80,80]{1,0:T(8,128)S(1)}, u32[]{:S(2)}, u32[]{:S(2)}) collective-permute-start(f32[80,80]{1,0:T(8,128)S(1)} %add.15), channel_id=1, source_target_pairs={{0,8},{4,12},{8,0},{12,4},{16,24},{20,28},{24,16},{28,20},{1,9},{5... | collective-permute-start | bytes 76808 | tf_op jit(solution)/shard_map/ppermute | solution.py:590
  23.3 5.0 %collective-permute-start.8 = (f32[80,80]{1,0:T(8,128)S(1)}, f32[80,80]{1,0:T(8,128)S(1)}, u32[]{:S(2)}, u32[]{:S(2)}) collective-permute-start(f32[80,80]{1,0:T(8,128)S(1)} %add.16.gate_ref), channel_id=1, source_target_pairs={{0,16},{4,20},{8,24},{12,28},{16,0},{20,4},{24,8},{28,12},{1,17},{... | collective-permute-start | bytes 76808 | tf_op jit(solution)/shard_map/ppermute | solution.py:590
  25.8 6.6 %collective-permute-start.6 = (f32[5,8,256]{2,1,0:T(8,128)S(1)}, f32[5,8,256]{2,1,0:T(8,128)S(1)}, u32[]{:S(2)}, u32[]{:S(2)}) collective-permute-start(f32[5,8,256]{2,1,0:T(8,128)S(1)} %get-tuple-element.41), channel_id=1, source_target_pairs={{0,4},{4,0},{8,12},{12,8},{16,20},{20,16},{24,28},{28,24},{1,5},{5... | collective-permute-start | bytes 122888 | tf_op jit(solution)/shard_map/ppermute | solution.py:58
  25.9 6.5 %collective-permute-start.7 = (f32[5,8,256]{2,1,0:T(8,128)S(1)}, f32[5,8,256]{2,1,0:T(8,128)S(1)}, u32[]{:S(2)}, u32[]{:S(2)}) collective-permute-start(f32[5,8,256]{2,1,0:T(8,128)S(1)} %get-tuple-element.42), channel_id=1, source_target_pairs={{0,28},{4,8},{8,4},{12,16},{16,12},{20,24},{24,20},{28,0},{1,29},{... | collective-permute-start | bytes 122888 | tf_op jit(solution)/shard_map/ppermute | solution.py:58
  28.3 4.1 %collective-permute-start.9 = (f32[80,80]{1,0:T(8,128)S(1)}, f32[80,80]{1,0:T(8,128)S(1)}, u32[]{:S(2)}, u32[]{:S(2)}) collective-permute-start(f32[80,80]{1,0:T(8,128)S(1)} %add.17), channel_id=1, source_target_pairs={{0,1},{1,0},{2,3},{3,2},{4,5},{5,4},{6,7},{7,6},{8,9},{9,8},{10,11... | collective-permute-start | bytes 76808 | tf_op jit(solution)/shard_map/ppermute | solution.py:590
  32.4 8.4 %collective-permute-start.10 = (f32[80,256]{1,0:T(8,128)S(1)}, f32[80,256]{1,0:T(8,128)S(1)}, u32[]{:S(2)}, u32[]{:S(2)}) collective-permute-start(f32[80,256]{1,0:T(8,128)S(1)} %get-tuple-element.45), channel_id=1, source_target_pairs={{0,1},{1,0},{2,3},{3,2},{4,5},{5,4},{6,7},{7,6},{8,9},{9,8},{10,11... | collective-permute-start | bytes 245768 | tf_op jit(solution)/shard_map/ppermute | solution.py:58
  34.0 6.8 %collective-permute-start.11 = (f32[80,256]{1,0:T(8,128)S(1)}, f32[80,256]{1,0:T(8,128)S(1)}, u32[]{:S(2)}, u32[]{:S(2)}) collective-permute-start(f32[80,256]{1,0:T(8,128)S(1)} %get-tuple-element.46), channel_id=1, source_target_pairs={{0,3},{1,2},{2,1},{3,0},{4,7},{5,6},{6,5},{7,4},{8,11},{9,10},{10,... | collective-permute-start | bytes 245768 | tf_op jit(solution)/shard_map/ppermute | solution.py:58
  34.5 4.0 %collective-permute-start.12 = (f32[80,80]{1,0:T(8,128)S(1)}, f32[80,80]{1,0:T(8,128)S(1)}, u32[]{:S(2)}, u32[]{:S(2)}) collective-permute-start(f32[80,80]{1,0:T(8,128)S(1)} %add.18.gate_ref), channel_id=1, source_target_pairs={{0,2},{1,3},{2,0},{3,1},{4,6},{5,7},{6,4},{7,5},{8,10},{9,11},{10,... | collective-permute-start | bytes 76808 | tf_op jit(solution)/shard_map/ppermute | solution.py:590
  43.1 11.4 %all-to-all-start = ((f32[32,1,128]{2,1,0:T(1,128)}), f32[32,1,128]{2,1,0:T(1,128)S(1)}, u32[]{:S(2)}, u32[]{:S(2)}) async-start(f32[32,1,128]{2,1,0:T(1,128)} %bitcast.4), calls=%async_computation | async-start | bytes 32768 | tf_op jit(solution)/shard_map/all_to_all | solution.py:678
  47.3 7.1 %copy-start.1 = (f32[64]{0:T(128)S(1)}, f32[64]{0:T(128)}, u32[]{:S(2)}) copy-start(f32[64]{0:T(128)} %param.9) | copy-start | bytes 772

commit v3 on v2

--- a/solution.py
+++ b/solution.py
@@ -34,6 +34,8 @@
 UP_Y = [i for i in range(NVEL) if velocity_table[i][1] == 1]
 DOWN_Y = [i for i in range(NVEL) if velocity_table[i][1] == -1]
 SPEED_SCALE = 10.0
+UNROLL = 4
+UNROLL_F = 1
 HIGHEST = lax.Precision.HIGHEST
 F32 = jnp.float32
 BF16 = jnp.bfloat16
@@ -159,10 +161,9 @@
     loads = [load(k) for k in range(parts)]
     omega = pltpu.make_async_copy(om_hbm, om_ref, sem.at[parts])
     solid = pltpu.make_async_copy(so_hbm, so_ref, sem.at[parts + 1])
-    loads[0].start()
     omega.start()
     solid.start()
-    for k in range(1, parts):
+    for k in range(parts):
         loads[k].start()
 
     def step(x, carry):
@@ -175,7 +176,7 @@
         if k == 0:
             omega.wait()
             solid.wait()
-        lax.fori_loop(k * rows, (k + 1) * rows, step, 0)
+        lax.fori_loop(k * rows, (k + 1) * rows, step, 0, unroll=UNROLL)
     emit_faces(nx, post_ref, (xa_ref, xb_ref))
 
 
@@ -228,7 +229,7 @@
         emit_post(post, x, nx, post_ref, yup_ref, ydn_ref)
         return carry
 
-    lax.fori_loop(0, nx, step, 0)
+    lax.fori_loop(0, nx, step, 0, unroll=UNROLL)
     emit_faces(nx, post_ref, (xa_ref, xb_ref))
 
 
@@ -256,17 +257,14 @@
 
 
 def gram_kernel(
-    s_ref, basis_hbm, snap_hbm, gate_ref, a_ref, h_hbm, g_ref, basis_ref, snap_ref, h_ref, ins, outs
+    s_hbm, basis_hbm, snap_hbm, gate_ref, a_ref, h_hbm, g_ref, t_ref, s_ref, basis_ref, snap_ref, h_ref, ins, outs
 ):
     rank = basis_ref.shape[0]
     depth = basis_ref.shape[1]
     extra = snap_ref.shape[0]
     cols = a_ref.shape[1]
-    same = lax.broadcasted_iota(jnp.int32, (rank, rank), 0) == lax.broadcasted_iota(
-        jnp.int32, (rank, rank), 1
-    )
-    scale = jnp.sum(jnp.where(same, s_ref[...], 0.0), axis=1, keepdims=True)
-    scale = jnp.broadcast_to(scale, (rank, 128))
+    weights = pltpu.make_async_copy(s_hbm, s_ref, outs.at[depth // 8])
+    weights.start()
     zero = jnp.zeros((cols - rank - extra, 8, 128), F32)
 
     def load(q):
@@ -290,6 +288,13 @@
         return carry
 
     lax.fori_loop(0, depth // 8, begin, 0)
+    weights.wait()
+    same = lax.broadcasted_iota(jnp.int32, (rank, rank), 0) == lax.broadcasted_iota(
+        jnp.int32, (rank, rank), 1
+    )
+    scale = jnp.sum(jnp.where(same, s_ref[...], 0.0), axis=1, keepdims=True)
+    scale = jnp.broadcast_to(scale, (rank, 128))
+    t_ref[...] = jnp.concatenate([scale, jnp.ones((cols - rank, 128), F32)], axis=0)
 
     def step(q, carry):
         for copy in load(q):
@@ -452,7 +457,7 @@
         copy(xc).start()
         return carry
 
-    lax.fori_loop(0, nxc, step, 0)
+    lax.fori_loop(0, nxc, step, 0, unroll=UNROLL_F)
     depth = 3 * nxc * nyc
     pairs = []
     for t in range(nz // 128):
@@ -494,8 +499,9 @@
     basis_hbm,
     snap_hbm,
     q_ref,
+    uo_hbm,
+    o_ref,
     uo_ref,
-    o_ref,
     basis_ref,
     snap_ref,
     tall_ref,
@@ -507,7 +513,7 @@
     known = cols - 1
     rank, depth = basis_ref.shape[:2]
     extra = snap_ref.shape[0]
-    parts = ins.shape[1]
+    parts = ins.shape[1] - 1
     size = depth // parts
     loads = []
     for k in range(parts):
@@ -531,10 +537,11 @@
     row_id = lax.broadcasted_iota(jnp.int32, (cols, cols), 0)
     edge = jnp.where(row_id == known, left * pivot, coef)
     uo_ref[...] = jnp.where(col_id == known, edge, u_ref[...])
+    factor = pltpu.make_async_copy(uo_ref, uo_hbm, ins.at[0, parts])
+    factor.start()
     weight = jnp.sum(inverse * coef, axis=0, keepdims=True) * (-pivot)
-    scale = jnp.concatenate([s_ref[...], jnp.ones((1, cols - rank), F32)], axis=1)
-    diag = jnp.where(row_id == col_id, weight * scale, 0.0)
-    tall_ref[...] = jnp.broadcast_to(jnp.sum(diag, axis=1, keepdims=True), (cols, 128))
+    diag = jnp.where(row_id == col_id, weight, 0.0)
+    tall_ref[...] = jnp.sum(diag, axis=1, keepdims=True) * s_ref[...]
 
     def step(q, carry):
         at = pl.ds(pl.multiple_of(q * 16, 16), 16)
@@ -552,6 +559,7 @@
         lax.fori_loop(k * size // 16, (k + 1) * size // 16, step, 0)
     copy = pltpu.make_async_copy(row_ref, o_ref.at[known], sem)
     copy.start()
+    factor.wait()
     copy.wait()
 
 
@@ -617,25 +625,27 @@
         compiler_params=params(6),
     )(*[in_hbm(value) for value in (populations, relax_rate, solid_mask)])
     xa, xb = swap((xa, xb), "gx")
-    weights = singular_values.reshape(1, rank)
+    weights = in_hbm(singular_values.reshape(1, rank))
     modes = in_hbm(basis.reshape(rank, depth, 128))
     earlier = in_hbm(snapshots.reshape(extra, depth, 128))
     blocks = depth // 8
-    rows, halves, gram = pl.pallas_call(
+    rows, halves, gram, scale = pl.pallas_call(
         gram_kernel,
         out_shape=(
             shape((depth, cols, 128)),
             pltpu.HBM((2 * cols, depth * 128), BF16),
             shape((cols, cols)),
+            shape((cols, 128)),
         ),
-        in_specs=[VMEM, HBM, HBM, ANY],
-        out_specs=(VMEM, HBM, VMEM),
+        in_specs=[HBM, HBM, HBM, ANY],
+        out_specs=(VMEM, HBM, VMEM, VMEM),
         scratch_shapes=[
+            pltpu.VMEM((1, rank), F32),
             pltpu.VMEM((rank, depth, 128), F32),
             pltpu.VMEM((extra, depth, 128), F32),
             pltpu.VMEM((2 * cols, depth * 128), BF16),
             pltpu.SemaphoreType.DMA((2, blocks)),
-            pltpu.SemaphoreType.DMA((blocks,)),
+            pltpu.SemaphoreType.DMA((blocks + 1,)),
         ],
         name="gram",
         compiler_params=params(12),
@@ -663,7 +673,7 @@
     )(gram)
     field, coarse, line = pl.pallas_call(
         final_kernel,
-        out_shape=(shape((NVEL, nx, ny, nz)), shape((depth, 128)), shape((n_dev, 128))),
+        out_shape=(shape((NVEL, nx, ny, nz)), shape((depth, 128)), pltpu.VMEM((n_dev, 128), F32)),
         in_specs=[VMEM] * 7 + [ANY],
         out_specs=(ANY, VMEM, VMEM),
         scratch_shapes=[
@@ -694,19 +704,20 @@
         lambda *refs: last_kernel(inv_rows, *refs),
         out_shape=(shape((cols, cols)), shape((cols, depth, 128))),
         in_specs=[VMEM] * 5 + [HBM] * 2 + [ANY],
-        out_specs=(VMEM, ANY),
+        out_specs=(ANY, ANY),
         scratch_shapes=[
+            pltpu.VMEM((cols, cols), F32),
             pltpu.VMEM((rank, depth, 128), F32),
             pltpu.VMEM((extra, depth, 128), F32),
             pltpu.VMEM((cols, 128), F32),
             pltpu.VMEM((depth, 128), F32),
-            pltpu.SemaphoreType.DMA((2, 3)),
+            pltpu.SemaphoreType.DMA((2, 4)),
             pltpu.SemaphoreType.DMA,
         ],
         input_output_aliases={7: 1},
         name="last",
         compiler_params=params(8),
-    )(lines, inverse, upper, weights, coarse, modes, earlier, rotated)
+    )(lines, inverse, upper, scale, coarse, modes, earlier, rotated)
     return field, upper, rotated.reshape((cols,) + tail)
 
 

time: 58.3 us -> 55.2 us (0.947)
  Pallas kernels: 24 us -> 21.6 us
  starting transfers between devices: 20.2 us -> 19.4 us
  waiting for transfers between devices: 12.5 us -> 13.3 us
  local copies, waits for them, and re-layouts: 0.66 us -> 0 us
    pallas_call x1, Pallas kernels: 2.5 us -> 1.53 us  [on_device(): pl.pallas_call(second_kernel, out_shape=post_shapes, in_specs=[VMEM] * 7...]
    ppermute x5, waiting for transfers between devices: 10.2 us -> 11 us  [exchange(): value = value + lax.ppermute(value, axis, pairs)]
    pallas_call x1, Pallas kernels: 3.4 us -> 2.6 us  [on_device(): pl.pallas_call(first_kernel, out_shape=post_shapes + (shape((nx, ny, nz))...]
    all_to_all x1, starting transfers between devices: 4.27 us -> 3.52 us  [on_device(): lines = lax.all_to_all(line, ('gx', 'gy'), 0, 0, tiled=True)]
    unnamed x4 -> x0, local copies, waits for them, and re-layouts: 0.66 us -> none
    pallas_call x1, Pallas kernels: 3.64 us -> 3.05 us  [on_device(): pl.pallas_call(lambda *refs: last_kernel(inv_rows, *refs), out_shape=(sha...]
  transfers between devices with their start and end apart: 14 -> 14, of which waited for: 5 -> 6; matrix products, arithmetic and copies ran while one was open for 0% -> 0% of each run, Pallas kernels for 25% -> 25%
where the time goes in v3:
time: 55.2 us; the launch traced here: 55 us
  Pallas kernels  21.6 us (39%)
  starting transfers between devices  19.4 us (35%)
  waiting for transfers between devices  13.3 us (24%)
  between operations  0.78 us (1%)
    ppermute x5, waiting for transfers between devices, exchange(): value = value + lax.ppermute(value, axis, pairs)  11 us
    ppermute x4, starting transfers between devices, swap(): lax.ppermute(values[1], axis, other)  8.73 us
    pallas_call x1, Pallas kernels, on_device(): pl.pallas_call(rotate_kernel, out_shape=shape((cols, depth, 128)), in_spe...  4.88 us
    pallas_call x1, Pallas kernels, on_device(): pl.pallas_call(gram_kernel, out_shape=(shape((depth, cols, 128)), pltpu.H...  4.87 us
    ppermute x4, starting transfers between devices, swap(): lax.ppermute(values[0], axis, partner)  3.74 us
    all_to_all x1, starting transfers between devices, on_device(): lines = lax.all_to_all(line, ('gx', 'gy'), 0, 0, tiled=True)  3.52 us
    ppermute x5, starting transfers between devices, exchange(): value = value + lax.ppermute(value, axis, pairs)  3.38 us
    pallas_call x1, Pallas kernels, on_device(): pl.pallas_call(lambda *refs: last_kernel(inv_rows, *refs), out_shape=(sha...  3.05 us
  transfers between devices with their start and end apart: 14, of which 6 were waited for; matrix products, arithmetic and copies ran while one was open for 0% of the time, Pallas kernels for 25%

profile of v3, /device:TPU:0, one launch (start us, length us, event | category | flops | bytes accessed | tf_op | source)
XLA Modules:
  0.0 55.0 jit_solution(9569576998722377094)
XLA Ops:
  0.6 2.6 %first.1 = (f32[19,16,8,256]{3,2,1,0:T(8,128)S(1)}, f32[5,8,256]{2,1,0:T(8,128)S(1)}, f32[5,8,256]{2,1,0:T(8,128)S(1)}, f32[80,256]{1,0:T(8,128)S(1)}, f32[80,25...) custom-call(f32[19,16,8,256]{3,2,1,0:T(8,128)} %f_hbm.1, f32[16,8,256]{2,1,0:T(8,128)} %om_hbm.1, ...), custom_call_target="tpu_custom_call" | custom-call | tf_op jit(solution)/shard_map/first/pallas_call | solution.py:619
  3.2 0.6 %collective-permute-start = (f32[5,8,256]{2,1,0:T(8,128)S(1)}, f32[5,8,256]{2,1,0:T(8,128)S(1)}, u32[]{:S(2)}, u32[]{:S(2)}) collective-permute-start(f32[5,8,256]{2,1,0:T(8,128)S(1)} %get-tuple-element.32), channel_id=1, source_target_pairs={{0,4},{4,0},{8,12},{12,8},{16,20},{20,16},{24,28},{28,24},{1,5},{5... | collective-permute-start | bytes 122888 | tf_op jit(solution)/shard_map/ppermute | solution.py:60
  3.8 4.7 %collective-permute-start.1 = (f32[5,8,256]{2,1,0:T(8,128)S(1)}, f32[5,8,256]{2,1,0:T(8,128)S(1)}, u32[]{:S(2)}, u32[]{:S(2)}) collective-permute-start(f32[5,8,256]{2,1,0:T(8,128)S(1)} %get-tuple-element.33), channel_id=1, source_target_pairs={{0,28},{4,8},{8,4},{12,16},{16,12},{20,24},{24,20},{28,0},{1,29},{... | collective-permute-start | bytes 122888 | tf_op jit(solution)/shard_map/ppermute | solution.py:60
  8.5 4.9 %gram.1 = (f32[96,80,128]{2,1,0:T(8,128)S(1)}, bf16[160,12288]{1,0:T(8,128)(2,1)}, f32[80,80]{1,0:T(8,128)S(1)}, f32[80,128]{1,0:T(8,128)S(1)}) custom-call(f32[1,64]{1,0:T(1,128)} %bitcast.14, f32[64,96,128]{2,1,0:T(8,128)} %bitcast.10, f32[15,96,128]{2,1,0:T(8,128)} %bitcast.12, f32[16,8,256]{2,1,0:T(8,128)S(1)} %get-tuple-element.36.gate_ref.om_ref), custom_call_target="tpu_custom_call" | custom-call | tf_op jit(solution)/shard_map/gram/pallas_call | solution.py:632
  13.4 0.0 collective-permute-done.xa_ref.ra_ref
  13.4 0.0 collective-permute-done.1.xb_ref.rb_ref
  13.5 1.6 %collective-permute-start.2 = (f32[80,256]{1,0:T(8,128)S(1)}, f32[80,256]{1,0:T(8,128)S(1)}, u32[]{:S(2)}, u32[]{:S(2)}) collective-permute-start(f32[80,256]{1,0:T(8,128)S(1)} %get-tuple-element.38), channel_id=1, source_target_pairs={{0,1},{1,0},{2,3},{3,2},{4,5},{5,4},{6,7},{7,6},{8,9},{9,8},{10,11... | collective-permute-start | bytes 245768 | tf_op jit(solution)/shard_map/ppermute | solution.py:60
  15.0 1.5 %collective-permute-start.3 = (f32[80,256]{1,0:T(8,128)S(1)}, f32[80,256]{1,0:T(8,128)S(1)}, u32[]{:S(2)}, u32[]{:S(2)}) collective-permute-start(f32[80,256]{1,0:T(8,128)S(1)} %get-tuple-element.39), channel_id=1, source_target_pairs={{0,3},{1,2},{2,1},{3,0},{4,7},{5,6},{6,5},{7,4},{8,11},{9,10},{10,... | collective-permute-start | bytes 245768 | tf_op jit(solution)/shard_map/ppermute | solution.py:60
  16.5 0.0 collective-permute-start.4
  16.5 1.2 %collective-permute-done.4 = f32[80,80]{1,0:T(8,128)S(1)} collective-permute-done((f32[80,80]{1,0:T(8,128)S(1)}, f32[80,80]{1,0:T(8,128)S(1)}, u32[]{:S(2)}, u32[]{:S(2)}) %collective-permute-start.4) | collective-permute-done | bytes 25632 | tf_op jit(solution)/shard_map/ppermute | solution.py:598
  17.7 0.0 collective-permute-start.5
  17.7 4.0 %collective-permute-done.5 = f32[80,80]{1,0:T(8,128)S(1)} collective-permute-done((f32[80,80]{1,0:T(8,128)S(1)}, f32[80,80]{1,0:T(8,128)S(1)}, u32[]{:S(2)}, u32[]{:S(2)}) %collective-permute-start.5) | collective-permute-done | bytes 25632 | tf_op jit(solution)/shard_map/ppermute | solution.py:598
  21.7 0.0 collective-permute-start.8
  21.7 0.0 collective-permute-done.2.sa_ref
  21.8 0.0 collective-permute-done.3.sb_ref
  21.8 1.5 %second.1 = (f32[19,16,8,256]{3,2,1,0:T(8,128)S(1)}, f32[5,8,256]{2,1,0:T(8,128)S(1)}, f32[5,8,256]{2,1,0:T(8,128)S(1)}, f32[80,256]{1,0:T(8,128)S(1)}, f32[80,256]{1,0:T(8,128)S(1)}) custom-call(f32[19,16,8,256]{3,2,1,0:T(8,128)S(1)} %get-tuple-element.31.p_ref, f32[5,8,256]{2,1,0:T(8,128)S(1)} %collective-permute-done.xa_ref.ra_ref, ...), custom_call_target="tpu_custom_call" | custom-call | tf_op jit(solution)/shard_map/second/pallas_call | solution.py:656
  23.3 0.1 collective-permute-start.6
  23.4 2.4 %collective-permute-start.7 = (f32[5,8,256]{2,1,0:T(8,128)S(1)}, f32[5,8,256]{2,1,0:T(8,128)S(1)}, u32[]{:S(2)}, u32[]{:S(2)}) collective-permute-start(f32[5,8,256]{2,1,0:T(8,128)S(1)} %get-tuple-element.43), channel_id=1, source_target_pairs={{0,28},{4,8},{8,4},{12,16},{16,12},{20,24},{24,20},{28,0},{1,29},{... | collective-permute-start | bytes 122888 | tf_op jit(solution)/shard_map/ppermute | solution.py:60
  25.8 0.8 %collective-permute-done.8 = f32[80,80]{1,0:T(8,128)S(1)} collective-permute-done((f32[80,80]{1,0:T(8,128)S(1)}, f32[80,80]{1,0:T(8,128)S(1)}, u32[]{:S(2)}, u32[]{:S(2)}) %collective-permute-start.8) | collective-permute-done | bytes 25632 | tf_op jit(solution)/shard_map/ppermute | solution.py:598
  26.6 1.5 %collective-permute-start.9 = (f32[80,80]{1,0:T(8,128)S(1)}, f32[80,80]{1,0:T(8,128)S(1)}, u32[]{:S(2)}, u32[]{:S(2)}) collective-permute-start(f32[80,80]{1,0:T(8,128)S(1)} %add.17), channel_id=1, source_target_pairs={{0,1},{1,0},{2,3},{3,2},{4,5},{5,4},{6,7},{7,6},{8,9},{9,8},{10,11... | collective-permute-start | bytes 76808 | tf_op jit(solution)/shard_map/ppermute | solution.py:598
  28.1 2.9 %collective-permute-done.9 = f32[80,80]{1,0:T(8,128)S(1)} collective-permute-done((f32[80,80]{1,0:T(8,128)S(1)}, f32[80,80]{1,0:T(8,128)S(1)}, u32[]{:S(2)}, u32[]{:S(2)}) %collective-permute-start.9) | collective-permute-done | bytes 25632 | tf_op jit(solution)/shard_map/ppermute | solution.py:598
  31.0 0.0 collective-permute-done.6.xa_ref.ra_ref
  31.0 0.0 collective-permute-done.7.xb_ref.rb_ref
  31.1 1.6 %collective-permute-start.10 = (f32[80,256]{1,0:T(8,128)S(1)}, f32[80,256]{1,0:T(8,128)S(1)}, u32[]{:S(2)}, u32[]{:S(2)}) collective-permute-start(f32[80,256]{1,0:T(8,128)S(1)} %get-tuple-element.46), channel_id=1, source_target_pairs={{0,1},{1,0},{2,3},{3,2},{4,5},{5,4},{6,7},{7,6},{8,9},{9,8},{10,11... | collective-permute-start | bytes 245768 | tf_op jit(solution)/shard_map/ppermute | solution.py:60
  32.6 0.1 collective-permute-start.11
  32.8 1.9 %collective-permute-start.12 = (f32[80,80]{1,0:T(8,128)S(1)}, f32[80,80]{1,0:T(8,128)S(1)}, u32[]{:S(2)}, u32[]{:S(2)}) collective-permute-start(f32[80,80]{1,0:T(8,128)S(1)} %add.18.gate_ref), channel_id=1, source_target_pairs={{0,2},{1,3},{2,0},{3,1},{4,6},{5,7},{6,4},{7,5},{8,10},{9,11},{10,... | collective-permute-start | bytes 76808 | tf_op jit(solution)/shard_map/ppermute | solution.py:598
  34.6 2.1 %collective-permute-done.12 = f32[80,80]{1,0:T(8,128)S(1)} collective-permute-done((f32[80,80]{1,0:T(8,128)S(1)}, f32[80,80]{1,0:T(8,128)S(1)}, u32[]{:S(2)}, u32[]{:S(2)}) %collective-permute-start.12) | collective-permute-done | bytes 25632 | tf_op jit(solution)/shard_map/ppermute | solution.py:598
  36.8 2.3 %factor.1 = (f32[80,80]{1,0:T(8,128)S(1)}, f32[80,80]{1,0:T(8,128)S(1)}, f32[80,240]{1,0:T(8,128)S(1)}) custom-call(f32[80,80]{1,0:T(8,128)S(1)} %add.19.refs_0_), custom_call_target="tpu_custom_call" | custom-call | tf_op jit(solution)/shard_map/factor/pallas_call | solution.py:668
  39.1 0.0 collective-permute-done.10.sa_ref
  39.1 0.0 collective-permute-done.11.sb_ref
  39.1 2.2 %final.1 = (f32[19,16,8,256]{3,2,1,0:T(8,128)}, f32[96,128]{1,0:T(8,128)S(1)}, f32[32,128]{1,0:T(8,128)}) custom-call(f32[19,16,8,256]{3,2,1,0:T(8,128)S(1)} %get-tuple-element.41.p_ref, f32[5,8,256]{2,1,0:T(8,128)S(1)} %collective-permute-done.6.xa_ref.ra_ref, f32[5,8,256]{2,1,0:T(8,128)S(1)} %collective-permute-done.7.xb_ref.rb_ref, ...), custom_call_target="tpu_custom_call" | custom-call | tf_op jit(solution)/shard_map/final/pallas_call | solution.py:674
  41.3 3.5 %all-to-all-start = ((f32[32,1,128]{2,1,0:T(1,128)}), f32[32,1,128]{2,1,0:T(1,128)S(1)}, u32[]{:S(2)}, u32[]{:S(2)}) async-start(f32[32,1,128]{2,1,0:T(1,128)} %bitcast.4), calls=%async_computation | async-start | bytes 32768 | tf_op jit(solution)/shard_map/all_to_all | solution.py:688
  44.9 4.9 %rotate.1.refs_7_ = f32[80,96,128]{2,1,0:T(8,128)} custom-call(f32[80,240]{1,0:T(8,128)S(1)} %get-tuple-element.55.w_ref, bf16[160,12288]{1,0:T(8,128)(2,1)} %get-tuple-element.56.h_hbm), custom_call_target="tpu_custom_call" | custom-call | tf_op jit(solution)/shard_map/rotate/pallas_call | solution.py:689
  49.8 2.2 %all-to-all-done = f32[32,1,128]{2,1,0:T(1,128)S(1)} async-done(((f32[32,1,128]{2,1,0:T(1,128)}), f32[32,1,128]{2,1,0:T(1,128)S(1)}, u32[]{:S(2)}, u32[]{:S(2)}) %all-to-all-start) | async-done | bytes 16416 | tf_op jit(solution)/shard_map/all_to_all | solution.py:688
  52.0 3.0 %last.1 = (f32[80,80]{1,0:T(8,128)}, f32[80,96,128]{2,1,0:T(8,128)}) custom-call(f32[32,128]{1,0:T(8,128)S(1)} %bitcast.8, f32[80,80]{1,0:T(8,128)S(1)} %get-tuple-element.49.gate_ref.refs_1_, f32[80,80]{1,0:T(8,128)S(1)} %get-tuple-element.52.refs_2_, f32[80,128]{1,0:T(8,128)S(1)} %get-tuple-element.53.refs_3_, ...), custom_call_target="tpu_custom_call", output_to_operand_aliasing={{1}: (7, {})} | custom-call | tf_op jit(solution)/shard_map/last/pallas_call | solution.py:703
  (7 shorter events, 0.1 us)
Async XLA Ops:
  3.2 10.1 %collective-permute-start = (f32[5,8,256]{2,1,0:T(8,128)S(1)}, f32[5,8,256]{2,1,0:T(8,128)S(1)}, u32[]{:S(2)}, u32[]{:S(2)}) collective-permute-start(f32[5,8,256]{2,1,0:T(8,128)S(1)} %get-tuple-element.32), channel_id=1, source_target_pairs={{0,4},{4,0},{8,12},{12,8},{16,20},{20,16},{24,28},{28,24},{1,5},{5... | collective-permute-start | bytes 122888 | tf_op jit(solution)/shard_map/ppermute | solution.py:60
  3.8 9.6 %collective-permute-start.1 = (f32[5,8,256]{2,1,0:T(8,128)S(1)}, f32[5,8,256]{2,1,0:T(8,128)S(1)}, u32[]{:S(2)}, u32[]{:S(2)}) collective-permute-start(f32[5,8,256]{2,1,0:T(8,128)S(1)} %get-tuple-element.33), channel_id=1, source_target_pairs={{0,28},{4,8},{8,4},{12,16},{16,12},{20,24},{24,20},{28,0},{1,29},{... | collective-permute-start | bytes 122888 | tf_op jit(solution)/shard_map/ppermute | solution.py:60
  13.5 8.3 %collective-permute-start.2 = (f32[80,256]{1,0:T(8,128)S(1)}, f32[80,256]{1,0:T(8,128)S(1)}, u32[]{:S(2)}, u32[]{:S(2)}) collective-permute-start(f32[80,256]{1,0:T(8,128)S(1)} %get-tuple-element.38), channel_id=1, source_target_pairs={{0,1},{1,0},{2,3},{3,2},{4,5},{5,4},{6,7},{7,6},{8,9},{9,8},{10,11... | collective-permute-start | bytes 245768 | tf_op jit(solution)/shard_map/ppermute | solution.py:60
  15.0 6.8 %collective-permute-start.3 = (f32[80,256]{1,0:T(8,128)S(1)}, f32[80,256]{1,0:T(8,128)S(1)}, u32[]{:S(2)}, u32[]{:S(2)}) collective-permute-start(f32[80,256]{1,0:T(8,128)S(1)} %get-tuple-element.39), channel_id=1, source_target_pairs={{0,3},{1,2},{2,1},{3,0},{4,7},{5,6},{6,5},{7,4},{8,11},{9,10},{10,... | collective-permute-start | bytes 245768 | tf_op jit(solution)/shard_map/ppermute | solution.py:60
  16.5 1.2 %collective-permute-start.4 = (f32[80,80]{1,0:T(8,128)S(1)}, f32[80,80]{1,0:T(8,128)S(1)}, u32[]{:S(2)}, u32[]{:S(2)}) collective-permute-start(f32[80,80]{1,0:T(8,128)S(1)} %get-tuple-element.37.gate_ref), channel_id=1, source_target_pairs={{0,4},{4,0},{8,12},{12,8},{16,20},{20,16},{24,28},{28,24},{1,5},{5... | collective-permute-start | bytes 76808 | tf_op jit(solution)/shard_map/ppermute | solution.py:598
  17.7 4.0 %collective-permute-start.5 = (f32[80,80]{1,0:T(8,128)S(1)}, f32[80,80]{1,0:T(8,128)S(1)}, u32[]{:S(2)}, u32[]{:S(2)}) collective-permute-start(f32[80,80]{1,0:T(8,128)S(1)} %add.15), channel_id=1, source_target_pairs={{0,8},{4,12},{8,0},{12,4},{16,24},{20,28},{24,16},{28,20},{1,9},{5... | collective-permute-start | bytes 76808 | tf_op jit(solution)/shard_map/ppermute | solution.py:598
  21.7 4.9 %collective-permute-start.8 = (f32[80,80]{1,0:T(8,128)S(1)}, f32[80,80]{1,0:T(8,128)S(1)}, u32[]{:S(2)}, u32[]{:S(2)}) collective-permute-start(f32[80,80]{1,0:T(8,128)S(1)} %add.16.gate_ref), channel_id=1, source_target_pairs={{0,16},{4,20},{8,24},{12,28},{16,0},{20,4},{24,8},{28,12},{1,17},{... | collective-permute-start | bytes 76808 | tf_op jit(solution)/shard_map/ppermute | solution.py:598
  23.3 7.7 %collective-permute-start.6 = (f32[5,8,256]{2,1,0:T(8,128)S(1)}, f32[5,8,256]{2,1,0:T(8,128)S(1)}, u32[]{:S(2)}, u32[]{:S(2)}) collective-permute-start(f32[5,8,256]{2,1,0:T(8,128)S(1)} %get-tuple-element.42), channel_id=1, source_target_pairs={{0,4},{4,0},{8,12},{12,8},{16,20},{20,16},{24,28},{28,24},{1,5},{5... | collective-permute-start | bytes 122888 | tf_op jit(solution)/shard_map/ppermute | solution.py:60
  23.4 7.6 %collective-permute-start.7 = (f32[5,8,256]{2,1,0:T(8,128)S(1)}, f32[5,8,256]{2,1,0:T(8,128)S(1)}, u32[]{:S(2)}, u32[]{:S(2)}) collective-permute-start(f32[5,8,256]{2,1,0:T(8,128)S(1)} %get-tuple-element.43), channel_id=1, source_target_pairs={{0,28},{4,8},{8,4},{12,16},{16,12},{20,24},{24,20},{28,0},{1,29},{... | collective-permute-start | bytes 122888 | tf_op jit(solution)/shard_map/ppermute | solution.py:60
  26.6 4.4 %collective-permute-start.9 = (f32[80,80]{1,0:T(8,128)S(1)}, f32[80,80]{1,0:T(8,128)S(1)}, u32[]{:S(2)}, u32[]{:S(2)}) collective-permute-start(f32[80,80]{1,0:T(8,128)S(1)} %add.17), channel_id=1, source_target_pairs={{0,1},{1,0},{2,3},{3,2},{4,5},{5,4},{6,7},{7,6},{8,9},{9,8},{10,11... | collective-permute-start | bytes 76808 | tf_op jit(solution)/shard_map/ppermute | solution.py:598
  31.1 8.0 %collective-permute-start.10 = (f32[80,256]{1,0:T(8,128)S(1)}, f32[80,256]{1,0:T(8,128)S(1)}, u32[]{:S(2)}, u32[]{:S(2)}) collective-permute-start(f32[80,256]{1,0:T(8,128)S(1)} %get-tuple-element.46), channel_id=1, source_target_pairs={{0,1},{1,0},{2,3},{3,2},{4,5},{5,4},{6,7},{7,6},{8,9},{9,8},{10,11... | collective-permute-start | bytes 245768 | tf_op jit(solution)/shard_map/ppermute | solution.py:60
  32.6 6.5 %collective-permute-start.11 = (f32[80,256]{1,0:T(8,128)S(1)}, f32[80,256]{1,0:T(8,128)S(1)}, u32[]{:S(2)}, u32[]{:S(2)}) collective-permute-start(f32[80,256]{1,0:T(8,128)S(1)} %get-tuple-element.47), channel_id=1, source_target_pairs={{0,3},{1,2},{2,1},{3,0},{4,7},{5,6},{6,5},{7,4},{8,11},{9,10},{10,... | collective-permute-start | bytes 245768 | tf_op jit(solution)/shard_map/ppermute | solution.py:60
  32.8 4.0 %collective-permute-start.12 = (f32[80,80]{1,0:T(8,128)S(1)}, f32[80,80]{1,0:T(8,128)S(1)}, u32[]{:S(2)}, u32[]{:S(2)}) collective-permute-start(f32[80,80]{1,0:T(8,128)S(1)} %add.18.gate_ref), channel_id=1, source_target_pairs={{0,2},{1,3},{2,0},{3,1},{4,6},{5,7},{6,4},{7,5},{8,10},{9,11},{10,... | collective-permute-start | bytes 76808 | tf_op jit(solution)/shard_map/ppermute | solution.py:598
  41.3 10.7 %all-to-all-start = ((f32[32,1,128]{2,1,0:T(1,128)}), f32[32,1,128]{2,1,0:T(1,128)S(1)}, u32[]{:S(2)}, u32[]{:S(2)}) async-start(f32[32,1,128]{2,1,0:T(1,128)} %bitcast.4), calls=%async_computation | async-start | bytes 32768 | tf_op jit(solution)/shard_map/all_to_all | solution.py:688

commit v4 on v3

--- a/solution.py
+++ b/solution.py
@@ -4,6 +4,7 @@
 from jax.experimental import pallas as pl
 from jax.experimental.pallas import tpu as pltpu
 from jax.sharding import PartitionSpec as P
+
 
 velocity_table = [
     (0, 0, 0),
@@ -35,6 +36,14 @@
 DOWN_Y = [i for i in range(NVEL) if velocity_table[i][1] == -1]
 SPEED_SCALE = 10.0
 UNROLL = 4
+ROUND_AXES = ("gy", "gx")
+CUTS = (1, 3, 4)
+
+
+def cuts(count):
+    return tuple(count * cut // 5 for cut in CUTS)
+
+
 UNROLL_F = 1
 HIGHEST = lax.Precision.HIGHEST
 F32 = jnp.float32
@@ -116,22 +125,18 @@
         cz = velocity_table[i][2]
         value = post[i] if cz == 0 else pltpu.roll(post[i], cz % post[i].shape[1], 1)
         post_ref[i, x] = value
-        cx = velocity_table[i][0]
-        row = lax.rem(x + (cx + nx), nx)
         if i in UP_Y:
-            yup_ref[pl.ds(UP_Y.index(i) * nx + row, 1), :] = value[ny - 1 : ny, :]
+            yup_ref[pl.ds(UP_Y.index(i) * nx + x, 1), :] = value[ny - 1 : ny, :]
         if i in DOWN_Y:
-            ydn_ref[pl.ds(DOWN_Y.index(i) * nx + row, 1), :] = value[0:1, :]
-
-
-def emit_faces(nx, post_ref, faces):
+            ydn_ref[pl.ds(DOWN_Y.index(i) * nx + x, 1), :] = value[0:1, :]
+
+
+def emit_edges(yup_ref, ydn_ref, edges):
     def place(odd):
-        for k, i in enumerate(UP_X):
-            faces[odd][k] = post_ref[i, nx - 1]
-        for k, i in enumerate(DOWN_X):
-            faces[1 - odd][k] = post_ref[i, 0]
-
-    by_parity("gx", place)
+        edges[odd][...] = yup_ref[...]
+        edges[1 - odd][...] = ydn_ref[...]
+
+    by_parity("gy", place)
 
 
 def sort_halos(xa_ref, xb_ref, ya_ref, yb_ref, xup_ref, xdn_ref, yup_ref, ydn_ref):
@@ -148,7 +153,7 @@
 
 
 def first_kernel(
-    f_hbm, om_hbm, so_hbm, post_ref, xa_ref, xb_ref, yup_ref, ydn_ref, om_ref, so_ref, f_ref, sem
+    f_hbm, om_hbm, so_hbm, post_ref, ya_ref, yb_ref, om_ref, so_ref, f_ref, yup_ref, ydn_ref, sem
 ):
     nx = f_ref.shape[1]
     parts = sem.shape[0] - 2
@@ -177,29 +182,32 @@
             omega.wait()
             solid.wait()
         lax.fori_loop(k * rows, (k + 1) * rows, step, 0, unroll=UNROLL)
-    emit_faces(nx, post_ref, (xa_ref, xb_ref))
+    emit_edges(yup_ref, ydn_ref, (ya_ref, yb_ref))
+
+
+def shift_y(i, value, src, nx, yup_ref, ydn_ref):
+    ny = value.shape[0]
+    cy = velocity_table[i][1]
+    if cy == 0:
+        return value
+    row_id = lax.broadcasted_iota(jnp.int32, value.shape, 0)
+    if cy == 1:
+        edge = yup_ref[pl.ds(UP_Y.index(i) * nx + src, 1), :]
+        return jnp.where(row_id == 0, edge, pltpu.roll(value, 1, 0))
+    edge = ydn_ref[pl.ds(DOWN_Y.index(i) * nx + src, 1), :]
+    return jnp.where(row_id == ny - 1, edge, pltpu.roll(value, ny - 1, 0))
 
 
 def streamed(x, nx, post_ref, xup_ref, xdn_ref, yup_ref, ydn_ref):
-    ny = post_ref.shape[2]
-    row_id = lax.broadcasted_iota(jnp.int32, (ny, post_ref.shape[3]), 0)
     f = []
     for i in range(NVEL):
-        cx, cy, _ = velocity_table[i]
+        cx = velocity_table[i][0]
+        src = x if cx == 0 else lax.rem(x + (nx - cx), nx)
+        value = shift_y(i, post_ref[i, src], src, nx, yup_ref, ydn_ref)
         if cx == 1:
-            value = jnp.where(x == 0, xup_ref[UP_X.index(i)], post_ref[i, lax.rem(x + nx - 1, nx)])
+            value = jnp.where(x == 0, xup_ref[UP_X.index(i)], value)
         elif cx == -1:
-            value = jnp.where(
-                x == nx - 1, xdn_ref[DOWN_X.index(i)], post_ref[i, lax.rem(x + 1, nx)]
-            )
-        else:
-            value = post_ref[i, x]
-        if cy == 1:
-            edge = yup_ref[pl.ds(UP_Y.index(i) * nx + x, 1), :]
-            value = jnp.where(row_id == 0, edge, pltpu.roll(value, 1, 0))
-        elif cy == -1:
-            edge = ydn_ref[pl.ds(DOWN_Y.index(i) * nx + x, 1), :]
-            value = jnp.where(row_id == ny - 1, edge, pltpu.roll(value, ny - 1, 0))
+            value = jnp.where(x == nx - 1, xdn_ref[DOWN_X.index(i)], value)
         f.append(value)
     return f
 
@@ -214,8 +222,8 @@
     so_ref,
     gate_ref,
     post_ref,
-    xa_ref,
-    xb_ref,
+    ya_ref,
+    yb_ref,
     yup_ref,
     ydn_ref,
     *halos,
@@ -230,28 +238,23 @@
         return carry
 
     lax.fori_loop(0, nx, step, 0, unroll=UNROLL)
-    emit_faces(nx, post_ref, (xa_ref, xb_ref))
-
-
-def pack_kernel(xa_ref, xb_ref, yup_ref, ydn_ref, gate_ref, oa_ref, ob_ref):
-    nx = yup_ref.shape[0] // len(UP_Y)
-    ny = xa_ref.shape[1]
-
-    def corners(ids, out, row, odd):
-        xu_ref, xd_ref = ((xb_ref, xa_ref), (xa_ref, xb_ref))[odd]
-        for k, i in enumerate(ids):
-            if velocity_table[i][0] == 1:
-                out[k * nx : k * nx + 1, :] = xu_ref[UP_X.index(i), row : row + 1, :]
-            elif velocity_table[i][0] == -1:
-                at = k * nx + nx - 1
-                out[at : at + 1, :] = xd_ref[DOWN_X.index(i), row : row + 1, :]
-
-    def place(odd):
-        up, down = (oa_ref, ob_ref)[odd], (ob_ref, oa_ref)[odd]
-        up[...] = yup_ref[...]
-        down[...] = ydn_ref[...]
-        by_parity("gx", lambda x_odd: corners(UP_Y, up, ny - 1, x_odd))
-        by_parity("gx", lambda x_odd: corners(DOWN_Y, down, 0, x_odd))
+    emit_edges(yup_ref, ydn_ref, (ya_ref, yb_ref))
+
+
+def pack_kernel(ya_ref, yb_ref, post_ref, gate_ref, xa_ref, xb_ref):
+    nx = post_ref.shape[1]
+
+    def place(odd_y):
+        yup_ref, ydn_ref = ((yb_ref, ya_ref), (ya_ref, yb_ref))[odd_y]
+
+        def faces(odd_x):
+            up_ref, down_ref = ((xa_ref, xb_ref), (xb_ref, xa_ref))[odd_x]
+            for k, i in enumerate(UP_X):
+                up_ref[k] = shift_y(i, post_ref[i, nx - 1], nx - 1, nx, yup_ref, ydn_ref)
+            for k, i in enumerate(DOWN_X):
+                down_ref[k] = shift_y(i, post_ref[i, 0], 0, nx, yup_ref, ydn_ref)
+
+        by_parity("gx", faces)
 
     by_parity("gy", place)
 
@@ -496,13 +499,12 @@
     u_ref,
     s_ref,
     c_ref,
-    basis_hbm,
+    basis_ref,
     snap_hbm,
     q_ref,
     uo_hbm,
     o_ref,
     uo_ref,
-    basis_ref,
     snap_ref,
     tall_ref,
     row_ref,
@@ -513,19 +515,8 @@
     known = cols - 1
     rank, depth = basis_ref.shape[:2]
     extra = snap_ref.shape[0]
-    parts = ins.shape[1] - 1
-    size = depth // parts
-    loads = []
-    for k in range(parts):
-        at = pl.ds(k * size, size)
-        loads.append(
-            (
-                pltpu.make_async_copy(basis_hbm.at[:, at], basis_ref.at[:, at], ins.at[0, k]),
-                pltpu.make_async_copy(snap_hbm.at[:, at], snap_ref.at[:, at], ins.at[1, k]),
-            )
-        )
-        for copy in loads[-1]:
-            copy.start()
+    load = pltpu.make_async_copy(snap_hbm, snap_ref, ins.at[0])
+    load.start()
     line = jnp.sum(v_ref[...], axis=0, keepdims=True)[:, :cols] * inv_rows
     across = lax.broadcasted_iota(jnp.int32, (1, cols), 1)
     norm = jnp.sum(jnp.where(across == known, line, 0.0), axis=1, keepdims=True)
@@ -537,7 +528,7 @@
     row_id = lax.broadcasted_iota(jnp.int32, (cols, cols), 0)
     edge = jnp.where(row_id == known, left * pivot, coef)
     uo_ref[...] = jnp.where(col_id == known, edge, u_ref[...])
-    factor = pltpu.make_async_copy(uo_ref, uo_hbm, ins.at[0, parts])
+    factor = pltpu.make_async_copy(uo_ref, uo_hbm, ins.at[1])
     factor.start()
     weight = jnp.sum(inverse * coef, axis=0, keepdims=True) * (-pivot)
     diag = jnp.where(row_id == col_id, weight, 0.0)
@@ -553,10 +544,8 @@
         row_ref[at, :] = (total[0] + total[1]) + (total[2] + total[3])
         return carry
 
-    for k in range(parts):
-        for copy in loads[k]:
-            copy.wait()
-        lax.fori_loop(k * size // 16, (k + 1) * size // 16, step, 0)
+    load.wait()
+    lax.fori_loop(0, depth // 16, step, 0)
     copy = pltpu.make_async_copy(row_ref, o_ref.at[known], sem)
     copy.start()
     factor.wait()
@@ -567,24 +556,30 @@
     return pltpu.with_memory_space_constraint(value, pltpu.HBM)
 
 
+def in_vmem(value):
+    return pltpu.with_memory_space_constraint(value, pltpu.VMEM)
+
+
 def shape(dims, dtype=F32):
     return jax.ShapeDtypeStruct(dims, dtype)
 
 
-def halo_y(xa, xb, yup, ydn, gate):
-    sends = pl.pallas_call(
+def halo_x(ya, yb, post, gate):
+    _, _, ny, nz = post.shape
+    pack_call = pl.pallas_call(
         pack_kernel,
-        out_shape=(shape(yup.shape), shape(ydn.shape)),
-        in_specs=[VMEM] * 4 + [ANY],
+        out_shape=(shape((len(UP_X), ny, nz)), shape((len(DOWN_X), ny, nz))),
+        in_specs=[VMEM] * 3 + [ANY],
         name="pack",
-        compiler_params=params(2),
-    )(xa, xb, yup, ydn, gate)
-    return swap(sends, "gy")
+        compiler_params=params(4),
+    )
+    faces = pack_call(ya, yb, post, gate)
+    return swap(faces, "gx")
 
 
 def rounds():
     steps = []
-    for axis in ("gx", "gy"):
+    for axis in ROUND_AXES:
         bit = 1
         while bit < lax.axis_size(axis):
             steps.append((axis, bit))
@@ -592,10 +587,12 @@
     return steps
 
 
-def exchange(value, steps):
-    for axis, bit in steps:
+def exchange(value, steps, begin, end):
+    for k in range(begin, end):
+        axis, bit = steps[k]
         pairs = [(s, s ^ bit) for s in range(lax.axis_size(axis))]
-        value = value + lax.ppermute(value, axis, pairs)
+        other = lax.ppermute(value, axis, pairs)
+        value = value + other
     return value
 
 
@@ -608,23 +605,20 @@
     n_dev = lax.axis_size("gx") * lax.axis_size("gy")
     inv_rows = 1.0 / (depth * tail[3] * n_dev)
     edges = len(UP_Y) * nx
-    post_shapes = (
-        shape((NVEL, nx, ny, nz)),
-        shape((len(UP_X), ny, nz)),
-        shape((len(DOWN_X), ny, nz)),
-        shape((edges, nz)),
-        shape((edges, nz)),
-    )
-    halos = [pltpu.VMEM(post_shapes[k].shape, F32) for k in range(1, 5)]
-    post, xa, xb, yup, ydn, omega, solid = pl.pallas_call(
+    post_shapes = (shape((NVEL, nx, ny, nz)), shape((edges, nz)), shape((edges, nz)))
+    edge_rows = [pltpu.VMEM((edges, nz), F32)] * 2
+    halos = [pltpu.VMEM((len(UP_X), ny, nz), F32)] * 2 + edge_rows
+    post, ya, yb, omega, solid = pl.pallas_call(
         first_kernel,
         out_shape=post_shapes + (shape((nx, ny, nz)), shape((nx, ny, nz), jnp.int32)),
         in_specs=[HBM] * 3,
-        scratch_shapes=[pltpu.VMEM((NVEL, nx, ny, nz), F32), pltpu.SemaphoreType.DMA((6,))],
+        scratch_shapes=[pltpu.VMEM((NVEL, nx, ny, nz), F32)]
+        + edge_rows
+        + [pltpu.SemaphoreType.DMA((6,))],
         name="first",
         compiler_params=params(6),
     )(*[in_hbm(value) for value in (populations, relax_rate, solid_mask)])
-    xa, xb = swap((xa, xb), "gx")
+    ya, yb = swap((ya, yb), "gy")
     weights = in_hbm(singular_values.reshape(1, rank))
     modes = in_hbm(basis.reshape(rank, depth, 128))
     earlier = in_hbm(snapshots.reshape(extra, depth, 128))
@@ -650,28 +644,24 @@
         name="gram",
         compiler_params=params(12),
     )(weights, modes, earlier, omega)
-    ya, yb = halo_y(xa, xb, yup, ydn, gram)
+    xa, xb = halo_x(ya, yb, post, gram)
     steps = rounds()
-    gram = exchange(gram, steps[:2])
-    post, xa, xb, yup, ydn = pl.pallas_call(
+    first, second, third = cuts(len(steps))
+    gram = exchange(gram, steps, 0, first)
+    second_call = pl.pallas_call(
         second_kernel,
         out_shape=post_shapes,
         in_specs=[VMEM] * 7 + [ANY],
-        scratch_shapes=halos,
+        scratch_shapes=edge_rows + halos,
         name="second",
         compiler_params=params(4),
-    )(post, xa, xb, ya, yb, omega, solid, gram)
-    xa, xb = swap((xa, xb), "gx")
-    gram = exchange(gram, steps[2:-1])
-    ya, yb = halo_y(xa, xb, yup, ydn, gram)
-    gram = exchange(gram, steps[-1:])
-    upper, inverse, split = pl.pallas_call(
-        lambda *refs: factor_kernel(inv_rows, *refs),
-        out_shape=(shape((cols, cols)), shape((cols, cols)), shape((cols, 3 * cols))),
-        name="factor",
-        compiler_params=params(4),
-    )(gram)
-    field, coarse, line = pl.pallas_call(
+    )
+    post, ya, yb = second_call(post, xa, xb, ya, yb, omega, solid, gram)
+    ya, yb = swap((ya, yb), "gy")
+    gram = exchange(gram, steps, first, second)
+    xa, xb = halo_x(ya, yb, post, gram)
+    gram = exchange(gram, steps, second, third)
+    final_call = pl.pallas_call(
         final_kernel,
         out_shape=(shape((NVEL, nx, ny, nz)), shape((depth, 128)), pltpu.VMEM((n_dev, 128), F32)),
         in_specs=[VMEM] * 7 + [ANY],
@@ -684,8 +674,16 @@
         + halos,
         name="final",
         compiler_params=params(6),
-    )(post, xa, xb, ya, yb, solid, rows, inverse)
+    )
+    field, coarse, line = final_call(post, xa, xb, ya, yb, solid, rows, gram)
     lines = lax.all_to_all(line, ("gx", "gy"), 0, 0, tiled=True)
+    gram = exchange(gram, steps, third, len(steps))
+    upper, inverse, split = pl.pallas_call(
+        lambda *refs: factor_kernel(inv_rows, *refs),
+        out_shape=(shape((cols, cols)), shape((cols, cols)), shape((cols, 3 * cols))),
+        name="factor",
+        compiler_params=params(4),
+    )(gram)
     rotated = pl.pallas_call(
         rotate_kernel,
         out_shape=shape((cols, depth, 128)),
@@ -703,21 +701,20 @@
     upper, rotated = pl.pallas_call(
         lambda *refs: last_kernel(inv_rows, *refs),
         out_shape=(shape((cols, cols)), shape((cols, depth, 128))),
-        in_specs=[VMEM] * 5 + [HBM] * 2 + [ANY],
+        in_specs=[VMEM] * 6 + [HBM, ANY],
         out_specs=(ANY, ANY),
         scratch_shapes=[
             pltpu.VMEM((cols, cols), F32),
-            pltpu.VMEM((rank, depth, 128), F32),
             pltpu.VMEM((extra, depth, 128), F32),
             pltpu.VMEM((cols, 128), F32),
             pltpu.VMEM((depth, 128), F32),
-            pltpu.SemaphoreType.DMA((2, 4)),
+            pltpu.SemaphoreType.DMA((2,)),
             pltpu.SemaphoreType.DMA,
         ],
         input_output_aliases={7: 1},
         name="last",
-        compiler_params=params(8),
-    )(lines, inverse, upper, scale, coarse, modes, earlier, rotated)
+        compiler_params=params(2),
+    )(lines, inverse, upper, scale, coarse, in_vmem(basis.reshape(rank, depth, 128)), earlier, rotated)
     return field, upper, rotated.reshape((cols,) + tail)
 
 

time: 55.2 us -> 57.1 us (1.034)
  starting transfers between devices: 19.4 us -> 21.9 us
    ppermute x5, starting transfers between devices: 3.38 us -> 5.76 us  [exchange(): other = lax.ppermute(value, axis, pairs)]
    all_to_all x1, waiting for transfers between devices: 2.23 us -> 0.01 us  [on_device(): lines = lax.all_to_all(line, ('gx', 'gy'), 0, 0, tiled=True)]
    ppermute x5, waiting for transfers between devices: 11 us -> 13 us  [exchange(): other = lax.ppermute(value, axis, pairs)]
    ppermute x4, starting transfers between devices: 3.74 us -> 4.9 us  [swap(): lax.ppermute(values[0], axis, partner)]
    ppermute x4, starting transfers between devices: 8.73 us -> 7.83 us  [swap(): lax.ppermute(values[1], axis, other)]
    pallas_call x1, Pallas kernels: 3.05 us -> 2.44 us  [on_device(): pl.pallas_call(lambda *refs: last_kernel(inv_rows, *refs), out_shape=(sha...]
  transfers between devices with their start and end apart: 14 -> 14, of which waited for: 6 -> 5; matrix products, arithmetic and copies ran while one was open for 0% -> 0% of each run, Pallas kernels for 25% -> 22%
where the time goes in v4:
time: 57.1 us; the launch traced here: 56.9 us
  starting transfers between devices  21.9 us (38%)
  Pallas kernels  21.1 us (37%)
  waiting for transfers between devices  13.1 us (23%)
  between operations  0.79 us (1%)
    ppermute x5, waiting for transfers between devices, exchange(): other = lax.ppermute(value, axis, pairs)  13 us
    ppermute x4, starting transfers between devices, swap(): lax.ppermute(values[1], axis, other)  7.83 us
    ppermute x5, starting transfers between devices, exchange(): other = lax.ppermute(value, axis, pairs)  5.76 us
    pallas_call x1, Pallas kernels, on_device(): pl.pallas_call(rotate_kernel, out_shape=shape((cols, depth, 128)), in_spe...  5.04 us
    ppermute x4, starting transfers between devices, swap(): lax.ppermute(values[0], axis, partner)  4.9 us
    pallas_call x1, Pallas kernels, on_device(): pl.pallas_call(gram_kernel, out_shape=(shape((depth, cols, 128)), pltpu.H...  4.87 us
    all_to_all x1, starting transfers between devices, on_device(): lines = lax.all_to_all(line, ('gx', 'gy'), 0, 0, tiled=True)  3.43 us
    pallas_call x1, Pallas kernels, on_device(): pl.pallas_call(first_kernel, out_shape=post_shapes + (shape((nx, ny, nz))...  2.6 us
  transfers between devices with their start and end apart: 14, of which 5 were waited for; matrix products, arithmetic and copies ran while one was open for 0% of the time, Pallas kernels for 22%

profile of v4, /device:TPU:0, one launch (start us, length us, event | category | flops | bytes accessed | tf_op | source)
XLA Modules:
  0.0 56.9 jit_solution(5746878650487840364)
XLA Ops:
  0.6 2.6 %first.1 = (f32[19,16,8,256]{3,2,1,0:T(8,128)S(1)}, f32[80,256]{1,0:T(8,128)S(1)}, f32[80,256]{1,0:T(8,128)S(1)}, f32[16,8,256]{2,1,0:T(8,128)S(1)}, s32[16,8,256]{2,1,0:T(8,128)S(1)}) custom-call(f32[19,16,8,256]{3,2,1,0:T(8,128)} %f_hbm.1, f32[16,8,256]{2,1,0:T(8,128)} %om_hbm.1, s32[16,8,256]{2,1,0:T(8,128)} %so_hbm.1), custom_call_target="tpu_custom_call" | custom-call | tf_op jit(solution)/shard_map/first/pallas_call | solution.py:611
  3.2 3.0 %collective-permute-start = (f32[80,256]{1,0:T(8,128)S(1)}, f32[80,256]{1,0:T(8,128)S(1)}, u32[]{:S(2)}, u32[]{:S(2)}) collective-permute-start(f32[80,256]{1,0:T(8,128)S(1)} %get-tuple-element.28), channel_id=1, source_target_pairs={{0,1},{1,0},{2,3},{3,2},{4,5},{5,4},{6,7},{7,6},{8,9},{9,8},{10,11... | collective-permute-start | bytes 245768 | tf_op jit(solution)/shard_map/ppermute | solution.py:69
  6.3 1.5 %collective-permute-start.1 = (f32[80,256]{1,0:T(8,128)S(1)}, f32[80,256]{1,0:T(8,128)S(1)}, u32[]{:S(2)}, u32[]{:S(2)}) collective-permute-start(f32[80,256]{1,0:T(8,128)S(1)} %get-tuple-element.29), channel_id=1, source_target_pairs={{0,3},{1,2},{2,1},{3,0},{4,7},{5,6},{6,5},{7,4},{8,11},{9,10},{10,... | collective-permute-start | bytes 245768 | tf_op jit(solution)/shard_map/ppermute | solution.py:69
  7.8 4.9 %gram.1 = (f32[96,80,128]{2,1,0:T(8,128)S(1)}, bf16[160,12288]{1,0:T(8,128)(2,1)}, f32[80,80]{1,0:T(8,128)S(1)}, f32[80,128]{1,0:T(8,128)S(1)}) custom-call(f32[1,64]{1,0:T(1,128)} %bitcast.14, f32[64,96,128]{2,1,0:T(8,128)} %bitcast.8, f32[15,96,128]{2,1,0:T(8,128)} %bitcast.12, f32[16,8,256]{2,1,0:T(8,128)S(1)} %get-tuple-element.30.gate_ref.om_ref), custom_call_target="tpu_custom_call" | custom-call | tf_op jit(solution)/shard_map/gram/pallas_call | solution.py:626
  12.6 0.0 collective-permute-done.ya_ref.sa_ref
  12.7 0.0 collective-permute-done.1.yb_ref.sb_ref
  12.7 0.1 collective-permute-start.2
  12.8 3.7 %collective-permute-start.3 = (f32[5,8,256]{2,1,0:T(8,128)S(1)}, f32[5,8,256]{2,1,0:T(8,128)S(1)}, u32[]{:S(2)}, u32[]{:S(2)}) collective-permute-start(f32[5,8,256]{2,1,0:T(8,128)S(1)} %get-tuple-element.33), channel_id=1, source_target_pairs={{0,28},{4,8},{8,4},{12,16},{16,12},{20,24},{24,20},{28,0},{1,29},{... | collective-permute-start | bytes 122888 | tf_op jit(solution)/shard_map/ppermute | solution.py:69
  16.5 1.5 %collective-permute-start.4 = (f32[80,80]{1,0:T(8,128)S(1)}, f32[80,80]{1,0:T(8,128)S(1)}, u32[]{:S(2)}, u32[]{:S(2)}) collective-permute-start(f32[80,80]{1,0:T(8,128)S(1)} %get-tuple-element.31.gate_ref), channel_id=1, source_target_pairs={{0,1},{1,0},{2,3},{3,2},{4,5},{5,4},{6,7},{7,6},{8,9},{9,8},{10,11... | collective-permute-start | bytes 76808 | tf_op jit(solution)/shard_map/ppermute | solution.py:594
  18.0 2.5 %collective-permute-done.4 = f32[80,80]{1,0:T(8,128)S(1)} collective-permute-done((f32[80,80]{1,0:T(8,128)S(1)}, f32[80,80]{1,0:T(8,128)S(1)}, u32[]{:S(2)}, u32[]{:S(2)}) %collective-permute-start.4) | collective-permute-done | bytes 25632 | tf_op jit(solution)/shard_map/ppermute | solution.py:594
  20.5 0.0 collective-permute-done.2.ra_ref
  20.5 0.0 collective-permute-done.3.rb_ref
  20.5 1.5 %second.1 = (f32[19,16,8,256]{3,2,1,0:T(8,128)S(1)}, f32[80,256]{1,0:T(8,128)S(1)}, f32[80,256]{1,0:T(8,128)S(1)}) custom-call(f32[19,16,8,256]{3,2,1,0:T(8,128)S(1)} %get-tuple-element.27.post_ref.p_ref, f32[5,8,256]{2,1,0:T(8,128)S(1)} %collective-permute-done.2.ra_ref, f32[5,8,256]{2,1,0:T(8,128)S(1)} %collective-permute-done.3.rb_ref, ...), custom_call_target="tpu_custom_call" | custom-call | tf_op jit(solution)/shard_map/second/pallas_call | solution.py:659
  22.1 1.6 %collective-permute-start.5 = (f32[80,256]{1,0:T(8,128)S(1)}, f32[80,256]{1,0:T(8,128)S(1)}, u32[]{:S(2)}, u32[]{:S(2)}) collective-permute-start(f32[80,256]{1,0:T(8,128)S(1)} %get-tuple-element.36), channel_id=1, source_target_pairs={{0,1},{1,0},{2,3},{3,2},{4,5},{5,4},{6,7},{7,6},{8,9},{9,8},{10,11... | collective-permute-start | bytes 245768 | tf_op jit(solution)/shard_map/ppermute | solution.py:69
  23.6 0.5 collective-permute-start.6
  24.1 1.5 %collective-permute-start.7 = (f32[80,80]{1,0:T(8,128)S(1)}, f32[80,80]{1,0:T(8,128)S(1)}, u32[]{:S(2)}, u32[]{:S(2)}) collective-permute-start(f32[80,80]{1,0:T(8,128)S(1)} %add.15.gate_ref), channel_id=1, source_target_pairs={{0,2},{1,3},{2,0},{3,1},{4,6},{5,7},{6,4},{7,5},{8,10},{9,11},{10,... | collective-permute-start | bytes 76808 | tf_op jit(solution)/shard_map/ppermute | solution.py:594
  25.6 2.5 %collective-permute-done.7 = f32[80,80]{1,0:T(8,128)S(1)} collective-permute-done((f32[80,80]{1,0:T(8,128)S(1)}, f32[80,80]{1,0:T(8,128)S(1)}, u32[]{:S(2)}, u32[]{:S(2)}) %collective-permute-start.7) | collective-permute-done | bytes 25632 | tf_op jit(solution)/shard_map/ppermute | solution.py:594
  28.1 0.0 collective-permute-start.8
  28.1 1.2 %collective-permute-done.8 = f32[80,80]{1,0:T(8,128)S(1)} collective-permute-done((f32[80,80]{1,0:T(8,128)S(1)}, f32[80,80]{1,0:T(8,128)S(1)}, u32[]{:S(2)}, u32[]{:S(2)}) %collective-permute-start.8) | collective-permute-done | bytes 25632 | tf_op jit(solution)/shard_map/ppermute | solution.py:594
  29.4 0.0 collective-permute-done.5.ya_ref.sa_ref
  29.4 0.0 collective-permute-done.6.yb_ref.sb_ref
  29.4 0.2 collective-permute-start.9
  29.6 2.2 %collective-permute-start.10 = (f32[5,8,256]{2,1,0:T(8,128)S(1)}, f32[5,8,256]{2,1,0:T(8,128)S(1)}, u32[]{:S(2)}, u32[]{:S(2)}) collective-permute-start(f32[5,8,256]{2,1,0:T(8,128)S(1)} %get-tuple-element.39), channel_id=1, source_target_pairs={{0,28},{4,8},{8,4},{12,16},{16,12},{20,24},{24,20},{28,0},{1,29},{... | collective-permute-start | bytes 122888 | tf_op jit(solution)/shard_map/ppermute | solution.py:69
  31.8 0.0 collective-permute-start.11
  31.8 4.0 %collective-permute-done.11 = f32[80,80]{1,0:T(8,128)S(1)} collective-permute-done((f32[80,80]{1,0:T(8,128)S(1)}, f32[80,80]{1,0:T(8,128)S(1)}, u32[]{:S(2)}, u32[]{:S(2)}) %collective-permute-start.11) | collective-permute-done | bytes 25632 | tf_op jit(solution)/shard_map/ppermute | solution.py:594
  35.8 0.0 collective-permute-done.9.ra_ref
  35.8 0.0 collective-permute-done.10.rb_ref
  35.8 2.2 %final.1 = (f32[19,16,8,256]{3,2,1,0:T(8,128)}, f32[96,128]{1,0:T(8,128)S(1)}, f32[32,128]{1,0:T(8,128)}) custom-call(f32[19,16,8,256]{3,2,1,0:T(8,128)S(1)} %get-tuple-element.35.post_ref.p_ref, f32[5,8,256]{2,1,0:T(8,128)S(1)} %collective-permute-done.9.ra_ref, f32[5,8,256]{2,1,0:T(8,128)S(1)} %collective-permute-done.10.rb_ref, ...), custom_call_target="tpu_custom_call" | custom-call | tf_op jit(solution)/shard_map/final/pallas_call | solution.py:678
  38.1 3.4 %all-to-all-start = ((f32[32,1,128]{2,1,0:T(1,128)}), f32[32,1,128]{2,1,0:T(1,128)S(1)}, u32[]{:S(2)}, u32[]{:S(2)}) async-start(f32[32,1,128]{2,1,0:T(1,128)} %bitcast.4), calls=%async_computation | async-start | bytes 32768 | tf_op jit(solution)/shard_map/all_to_all | solution.py:679
  41.5 2.7 %collective-permute-start.12 = (f32[80,80]{1,0:T(8,128)S(1)}, f32[80,80]{1,0:T(8,128)S(1)}, u32[]{:S(2)}, u32[]{:S(2)}) collective-permute-start(f32[80,80]{1,0:T(8,128)S(1)} %add.18.gate_ref), channel_id=1, source_target_pairs={{0,16},{4,20},{8,24},{12,28},{16,0},{20,4},{24,8},{28,12},{1,17},{... | collective-permute-start | bytes 76808 | tf_op jit(solution)/shard_map/ppermute | solution.py:594
  44.2 2.8 %collective-permute-done.12 = f32[80,80]{1,0:T(8,128)S(1)} collective-permute-done((f32[80,80]{1,0:T(8,128)S(1)}, f32[80,80]{1,0:T(8,128)S(1)}, u32[]{:S(2)}, u32[]{:S(2)}) %collective-permute-start.12) | collective-permute-done | bytes 25632 | tf_op jit(solution)/shard_map/ppermute | solution.py:594
  47.1 2.3 %factor.1 = (f32[80,80]{1,0:T(8,128)S(1)}, f32[80,80]{1,0:T(8,128)S(1)}, f32[80,240]{1,0:T(8,128)S(1)}) custom-call(f32[80,80]{1,0:T(8,128)S(1)} %add.19.refs_0_), custom_call_target="tpu_custom_call" | custom-call | tf_op jit(solution)/shard_map/factor/pallas_call | solution.py:681
  49.4 0.0 copy-start
  49.4 5.0 %rotate.1.refs_7_ = f32[80,96,128]{2,1,0:T(8,128)} custom-call(f32[80,240]{1,0:T(8,128)S(1)} %get-tuple-element.47.w_ref, bf16[160,12288]{1,0:T(8,128)(2,1)} %get-tuple-element.48.h_hbm), custom_call_target="tpu_custom_call" | custom-call | tf_op jit(solution)/shard_map/rotate/pallas_call | solution.py:687
  54.5 0.0 all-to-all-done
  54.5 0.0 copy-done
  54.5 2.4 %last.1 = (f32[80,80]{1,0:T(8,128)}, f32[80,96,128]{2,1,0:T(8,128)}) custom-call(f32[32,128]{1,0:T(8,128)S(1)} %bitcast.10, f32[80,80]{1,0:T(8,128)S(1)} %get-tuple-element.43.refs_1_, f32[80,80]{1,0:T(8,128)S(1)} %get-tuple-element.44.refs_2_, f32[80,128]{1,0:T(8,128)S(1)} %get-tuple-element.45.refs_3_, ...), custom_call_target="tpu_custom_call", output_to_operand_aliasing={{1}: (7, {})} | custom-call | tf_op jit(solution)/shard_map/last/pallas_call | solution.py:701
  (7 shorter events, 0.1 us)
Async XLA Ops:
  3.2 9.4 %collective-permute-start = (f32[80,256]{1,0:T(8,128)S(1)}, f32[80,256]{1,0:T(8,128)S(1)}, u32[]{:S(2)}, u32[]{:S(2)}) collective-permute-start(f32[80,256]{1,0:T(8,128)S(1)} %get-tuple-element.28), channel_id=1, source_target_pairs={{0,1},{1,0},{2,3},{3,2},{4,5},{5,4},{6,7},{7,6},{8,9},{9,8},{10,11... | collective-permute-start | bytes 245768 | tf_op jit(solution)/shard_map/ppermute | solution.py:69
  6.3 6.4 %collective-permute-start.1 = (f32[80,256]{1,0:T(8,128)S(1)}, f32[80,256]{1,0:T(8,128)S(1)}, u32[]{:S(2)}, u32[]{:S(2)}) collective-permute-start(f32[80,256]{1,0:T(8,128)S(1)} %get-tuple-element.29), channel_id=1, source_target_pairs={{0,3},{1,2},{2,1},{3,0},{4,7},{5,6},{6,5},{7,4},{8,11},{9,10},{10,... | collective-permute-start | bytes 245768 | tf_op jit(solution)/shard_map/ppermute | solution.py:69
  12.7 7.8 %collective-permute-start.2 = (f32[5,8,256]{2,1,0:T(8,128)S(1)}, f32[5,8,256]{2,1,0:T(8,128)S(1)}, u32[]{:S(2)}, u32[]{:S(2)}) collective-permute-start(f32[5,8,256]{2,1,0:T(8,128)S(1)} %get-tuple-element.32), channel_id=1, source_target_pairs={{0,4},{4,0},{8,12},{12,8},{16,20},{20,16},{24,28},{28,24},{1,5},{5... | collective-permute-start | bytes 122888 | tf_op jit(solution)/shard_map/ppermute | solution.py:69
  12.8 7.7 %collective-permute-start.3 = (f32[5,8,256]{2,1,0:T(8,128)S(1)}, f32[5,8,256]{2,1,0:T(8,128)S(1)}, u32[]{:S(2)}, u32[]{:S(2)}) collective-permute-start(f32[5,8,256]{2,1,0:T(8,128)S(1)} %get-tuple-element.33), channel_id=1, source_target_pairs={{0,28},{4,8},{8,4},{12,16},{16,12},{20,24},{24,20},{28,0},{1,29},{... | collective-permute-start | bytes 122888 | tf_op jit(solution)/shard_map/ppermute | solution.py:69
  16.5 4.0 %collective-permute-start.4 = (f32[80,80]{1,0:T(8,128)S(1)}, f32[80,80]{1,0:T(8,128)S(1)}, u32[]{:S(2)}, u32[]{:S(2)}) collective-permute-start(f32[80,80]{1,0:T(8,128)S(1)} %get-tuple-element.31.gate_ref), channel_id=1, source_target_pairs={{0,1},{1,0},{2,3},{3,2},{4,5},{5,4},{6,7},{7,6},{8,9},{9,8},{10,11... | collective-permute-start | bytes 76808 | tf_op jit(solution)/shard_map/ppermute | solution.py:594
  22.1 7.3 %collective-permute-start.5 = (f32[80,256]{1,0:T(8,128)S(1)}, f32[80,256]{1,0:T(8,128)S(1)}, u32[]{:S(2)}, u32[]{:S(2)}) collective-permute-start(f32[80,256]{1,0:T(8,128)S(1)} %get-tuple-element.36), channel_id=1, source_target_pairs={{0,1},{1,0},{2,3},{3,2},{4,5},{5,4},{6,7},{7,6},{8,9},{9,8},{10,11... | collective-permute-start | bytes 245768 | tf_op jit(solution)/shard_map/ppermute | solution.py:69
  23.6 5.7 %collective-permute-start.6 = (f32[80,256]{1,0:T(8,128)S(1)}, f32[80,256]{1,0:T(8,128)S(1)}, u32[]{:S(2)}, u32[]{:S(2)}) collective-permute-start(f32[80,256]{1,0:T(8,128)S(1)} %get-tuple-element.37), channel_id=1, source_target_pairs={{0,3},{1,2},{2,1},{3,0},{4,7},{5,6},{6,5},{7,4},{8,11},{9,10},{10,... | collective-permute-start | bytes 245768 | tf_op jit(solution)/shard_map/ppermute | solution.py:69
  24.1 4.0 %collective-permute-start.7 = (f32[80,80]{1,0:T(8,128)S(1)}, f32[80,80]{1,0:T(8,128)S(1)}, u32[]{:S(2)}, u32[]{:S(2)}) collective-permute-start(f32[80,80]{1,0:T(8,128)S(1)} %add.15.gate_ref), channel_id=1, source_target_pairs={{0,2},{1,3},{2,0},{3,1},{4,6},{5,7},{6,4},{7,5},{8,10},{9,11},{10,... | collective-permute-start | bytes 76808 | tf_op jit(solution)/shard_map/ppermute | solution.py:594
  28.1 1.2 %collective-permute-start.8 = (f32[80,80]{1,0:T(8,128)S(1)}, f32[80,80]{1,0:T(8,128)S(1)}, u32[]{:S(2)}, u32[]{:S(2)}) collective-permute-start(f32[80,80]{1,0:T(8,128)S(1)} %add.16), channel_id=1, source_target_pairs={{0,4},{4,0},{8,12},{12,8},{16,20},{20,16},{24,28},{28,24},{1,5},{5... | collective-permute-start | bytes 76808 | tf_op jit(solution)/shard_map/ppermute | solution.py:594
  29.4 6.4 %collective-permute-start.9 = (f32[5,8,256]{2,1,0:T(8,128)S(1)}, f32[5,8,256]{2,1,0:T(8,128)S(1)}, u32[]{:S(2)}, u32[]{:S(2)}) collective-permute-start(f32[5,8,256]{2,1,0:T(8,128)S(1)} %get-tuple-element.38), channel_id=1, source_target_pairs={{0,4},{4,0},{8,12},{12,8},{16,20},{20,16},{24,28},{28,24},{1,5},{5... | collective-permute-start | bytes 122888 | tf_op jit(solution)/shard_map/ppermute | solution.py:69
  29.6 6.2 %collective-permute-start.10 = (f32[5,8,256]{2,1,0:T(8,128)S(1)}, f32[5,8,256]{2,1,0:T(8,128)S(1)}, u32[]{:S(2)}, u32[]{:S(2)}) collective-permute-start(f32[5,8,256]{2,1,0:T(8,128)S(1)} %get-tuple-element.39), channel_id=1, source_target_pairs={{0,28},{4,8},{8,4},{12,16},{16,12},{20,24},{24,20},{28,0},{1,29},{... | collective-permute-start | bytes 122888 | tf_op jit(solution)/shard_map/ppermute | solution.py:69
  31.8 4.0 %collective-permute-start.11 = (f32[80,80]{1,0:T(8,128)S(1)}, f32[80,80]{1,0:T(8,128)S(1)}, u32[]{:S(2)}, u32[]{:S(2)}) collective-permute-start(f32[80,80]{1,0:T(8,128)S(1)} %add.17.gate_ref), channel_id=1, source_target_pairs={{0,8},{4,12},{8,0},{12,4},{16,24},{20,28},{24,16},{28,20},{1,9},{5... | collective-permute-start | bytes 76808 | tf_op jit(solution)/shard_map/ppermute | solution.py:594
  38.1 16.4 %all-to-all-start = ((f32[32,1,128]{2,1,0:T(1,128)}), f32[32,1,128]{2,1,0:T(1,128)S(1)}, u32[]{:S(2)}, u32[]{:S(2)}) async-start(f32[32,1,128]{2,1,0:T(1,128)} %bitcast.4), calls=%async_computation | async-start | bytes 32768 | tf_op jit(solution)/shard_map/all_to_all | solution.py:679
  41.5 5.6 %collective-permute-start.12 = (f32[80,80]{1,0:T(8,128)S(1)}, f32[80,80]{1,0:T(8,128)S(1)}, u32[]{:S(2)}, u32[]{:S(2)}) collective-permute-start(f32[80,80]{1,0:T(8,128)S(1)} %add.18.gate_ref), channel_id=1, source_target_pairs={{0,16},{4,20},{8,24},{12,28},{16,0},{20,4},{24,8},{28,12},{1,17},{... | collective-permute-start | bytes 76808 | tf_op jit(solution)/shard_map/ppermute | solution.py:594
  49.4 5.1 %copy-start = (f32[64,3,8,4,128]{4,3,2,1,0:T(4,128)S(1)}, f32[64,3,8,4,128]{4,3,2,1,0:T(4,128)}, u32[]{:S(2)}) copy-start(f32[64,3,8,4,128]{4,3,2,1,0:T(4,128)} %param.10) | copy-start | bytes 9437188

commit v5 on v4

--- a/solution.py
+++ b/solution.py
@@ -36,7 +36,6 @@
 DOWN_Y = [i for i in range(NVEL) if velocity_table[i][1] == -1]
 SPEED_SCALE = 10.0
 UNROLL = 4
-ROUND_AXES = ("gy", "gx")
 CUTS = (1, 3, 4)
 
 
@@ -388,22 +387,22 @@
     weight = w_ref[...].astype(BF16)
 
     def copy(q):
-        at = pl.ds(pl.multiple_of(q * 8, 8), 8)
+        at = pl.ds(pl.multiple_of(q * 16, 16), 16)
         return pltpu.make_async_copy(out_ref.at[:, at, :], o_ref.at[:, at, :], sem.at[q])
 
     def load(q):
-        at = pl.ds(pl.multiple_of(q * 1024, 1024), 1024)
+        at = pl.ds(pl.multiple_of(q * 2048, 2048), 2048)
         return pltpu.make_async_copy(h_hbm.at[:, at], h_ref.at[:, at], ins.at[q])
 
     def begin(q, carry):
         load(q).start()
         return carry
 
-    lax.fori_loop(0, depth // 8, begin, 0)
+    lax.fori_loop(0, depth // 16, begin, 0)
 
     def step(q, carry):
         load(q).wait()
-        at = pl.ds(pl.multiple_of(q * 1024, 1024), 1024)
+        at = pl.ds(pl.multiple_of(q * 2048, 2048), 2048)
         high = h_ref[0:cols, at]
         low = h_ref[cols : 2 * cols, at]
         res = lax.dot_general(
@@ -412,22 +411,22 @@
             (((1,), (0,)), ((), ())),
             preferred_element_type=F32,
         )
-        res = jnp.stack([res[:, t * 128 : (t + 1) * 128] for t in range(8)], axis=0)
-        out_ref[:, pl.ds(pl.multiple_of(q * 8, 8), 8), :] = jnp.swapaxes(res, 0, 1)
+        res = jnp.stack([res[:, t * 128 : (t + 1) * 128] for t in range(16)], axis=0)
+        out_ref[:, pl.ds(pl.multiple_of(q * 16, 16), 16), :] = jnp.swapaxes(res, 0, 1)
         copy(q).start()
         return carry
 
-    lax.fori_loop(0, depth // 8, step, 0)
+    lax.fori_loop(0, depth // 16, step, 0)
 
     def finish(q, carry):
         copy(q).wait()
         return carry
 
-    lax.fori_loop(0, depth // 8, finish, 0)
+    lax.fori_loop(0, depth // 16, finish, 0)
 
 
 def final_kernel(
-    p_ref, ra_ref, rb_ref, sa_ref, sb_ref, so_ref, a_ref, gate_ref, f_hbm, c_ref, v_ref, vel_ref, f_ref, sem, *halos
+    p_ref, ra_ref, rb_ref, sa_ref, sb_ref, so_ref, a_ref, gate_ref, f_hbm, c_ref, v_hbm, vel_ref, f_ref, v_ref, sem, *halos
 ):
     nx, ny, nz = p_ref.shape[1:]
     nxc, nyc = nx // 2, ny // 2
@@ -489,7 +488,10 @@
     diag = jnp.where(across == lax.broadcasted_iota(jnp.int32, (cols, 128), 0), dots, 0.0)
     line = jnp.sum(diag, axis=0, keepdims=True)
     v_ref[...] = jnp.broadcast_to(line, v_ref.shape)
+    send = pltpu.make_async_copy(v_ref, v_hbm, sem.at[nxc])
+    send.start()
     lax.fori_loop(0, nxc, finish, 0)
+    send.wait()
 
 
 def last_kernel(
@@ -515,8 +517,13 @@
     known = cols - 1
     rank, depth = basis_ref.shape[:2]
     extra = snap_ref.shape[0]
-    load = pltpu.make_async_copy(snap_hbm, snap_ref, ins.at[0])
-    load.start()
+    parts = ins.shape[0] - 1
+    size = extra // parts
+    loads = []
+    for k in range(parts):
+        at = pl.ds(k * size, size if k < parts - 1 else extra - k * size)
+        loads.append(pltpu.make_async_copy(snap_hbm.at[at], snap_ref.at[at], ins.at[k]))
+        loads[k].start()
     line = jnp.sum(v_ref[...], axis=0, keepdims=True)[:, :cols] * inv_rows
     across = lax.broadcasted_iota(jnp.int32, (1, cols), 1)
     norm = jnp.sum(jnp.where(across == known, line, 0.0), axis=1, keepdims=True)
@@ -528,24 +535,32 @@
     row_id = lax.broadcasted_iota(jnp.int32, (cols, cols), 0)
     edge = jnp.where(row_id == known, left * pivot, coef)
     uo_ref[...] = jnp.where(col_id == known, edge, u_ref[...])
-    factor = pltpu.make_async_copy(uo_ref, uo_hbm, ins.at[1])
+    factor = pltpu.make_async_copy(uo_ref, uo_hbm, ins.at[parts])
     factor.start()
     weight = jnp.sum(inverse * coef, axis=0, keepdims=True) * (-pivot)
     diag = jnp.where(row_id == col_id, weight, 0.0)
     tall_ref[...] = jnp.sum(diag, axis=1, keepdims=True) * s_ref[...]
 
-    def step(q, carry):
+    def weighted(source, first, count, total, at):
+        for k in range(count):
+            value = source[k, at, :] * tall_ref[first + k : first + k + 1, :]
+            total[k % 4] = value if total[k % 4] is None else total[k % 4] + value
+        return (total[0] + total[1]) + (total[2] + total[3])
+
+    def begin(q, carry):
         at = pl.ds(pl.multiple_of(q * 16, 16), 16)
-        total = [c_ref[at, :] * pivot] + [None] * 3
-        for k in range(rank + extra):
-            value = basis_ref[k, at, :] if k < rank else snap_ref[k - rank, at, :]
-            value = value * tall_ref[k : k + 1, :]
-            total[k % 4] = value if total[k % 4] is None else total[k % 4] + value
-        row_ref[at, :] = (total[0] + total[1]) + (total[2] + total[3])
-        return carry
-
-    load.wait()
-    lax.fori_loop(0, depth // 16, step, 0)
+        row_ref[at, :] = weighted(basis_ref, 0, rank, [c_ref[at, :] * pivot] + [None] * 3, at)
+        return carry
+
+    def finish(q, carry):
+        at = pl.ds(pl.multiple_of(q * 16, 16), 16)
+        row_ref[at, :] = weighted(snap_ref, rank, extra, [row_ref[at, :]] + [None] * 3, at)
+        return carry
+
+    lax.fori_loop(0, depth // 16, begin, 0)
+    for load in loads:
+        load.wait()
+    lax.fori_loop(0, depth // 16, finish, 0)
     copy = pltpu.make_async_copy(row_ref, o_ref.at[known], sem)
     copy.start()
     factor.wait()
@@ -578,13 +593,14 @@
 
 
 def rounds():
-    steps = []
-    for axis in ROUND_AXES:
+    bits = {axis: [] for axis in ("gx", "gy")}
+    for axis, steps in bits.items():
         bit = 1
         while bit < lax.axis_size(axis):
             steps.append((axis, bit))
             bit *= 2
-    return steps
+    gx, gy = bits["gx"], bits["gy"]
+    return gx[:1] + gy[:1] + gx[1:] + gy[1:]
 
 
 def exchange(value, steps, begin, end):
@@ -663,13 +679,14 @@
     gram = exchange(gram, steps, second, third)
     final_call = pl.pallas_call(
         final_kernel,
-        out_shape=(shape((NVEL, nx, ny, nz)), shape((depth, 128)), pltpu.VMEM((n_dev, 128), F32)),
+        out_shape=(shape((NVEL, nx, ny, nz)), shape((depth, 128)), shape((n_dev, 128))),
         in_specs=[VMEM] * 7 + [ANY],
-        out_specs=(ANY, VMEM, VMEM),
+        out_specs=(ANY, VMEM, ANY),
         scratch_shapes=[
             pltpu.VMEM((nz // 128, 3 * (nx // 2) * ny, 128), F32),
             pltpu.VMEM((NVEL, nx, ny, nz), F32),
-            pltpu.SemaphoreType.DMA((nx // 2,)),
+            pltpu.VMEM((n_dev, 128), F32),
+            pltpu.SemaphoreType.DMA((nx // 2 + 1,)),
         ]
         + halos,
         name="final",

time: 57.1 us -> 56.3 us (0.986)
  waiting for transfers between devices: 13.1 us -> 15.9 us
  starting transfers between devices: 21.9 us -> 19.7 us
  Pallas kernels: 21.1 us -> 19.7 us
    ppermute x5, waiting for transfers between devices: 13 us -> 15.3 us  [exchange(): other = lax.ppermute(value, axis, pairs)]
    ppermute x5, starting transfers between devices: 5.76 us -> 3.85 us  [exchange(): other = lax.ppermute(value, axis, pairs)]
    pallas_call x1, Pallas kernels: 5.04 us -> 4.37 us  [on_device(): pl.pallas_call(rotate_kernel, out_shape=shape((cols, depth, 128)), in_spe...]
  transfers between devices with their start and end apart: 14 -> 14, of which waited for: 5 -> 6; matrix products, arithmetic and copies ran while one was open for 0% -> 0% of each run, Pallas kernels for 22% -> 21%
where the time goes in v5:
time: 56.3 us; the launch traced here: 56.1 us
  Pallas kernels  19.7 us (35%)
  starting transfers between devices  19.7 us (35%)
  waiting for transfers between devices  15.9 us (28%)
  between operations  0.78 us (1%)
    ppermute x5, waiting for transfers between devices, exchange(): other = lax.ppermute(value, axis, pairs)  15.3 us
    ppermute x4, starting transfers between devices, swap(): lax.ppermute(values[1], axis, other)  8.08 us
    pallas_call x1, Pallas kernels, on_device(): pl.pallas_call(gram_kernel, out_shape=(shape((depth, cols, 128)), pltpu.H...  4.87 us
    ppermute x4, starting transfers between devices, swap(): lax.ppermute(values[0], axis, partner)  4.75 us
    pallas_call x1, Pallas kernels, on_device(): pl.pallas_call(rotate_kernel, out_shape=shape((cols, depth, 128)), in_spe...  4.37 us
    ppermute x5, starting transfers between devices, exchange(): other = lax.ppermute(value, axis, pairs)  3.85 us
    all_to_all x1, starting transfers between devices, on_device(): lines = lax.all_to_all(line, ('gx', 'gy'), 0, 0, tiled=True)  3.04 us
    pallas_call x1, Pallas kernels, on_device(): pl.pallas_call(first_kernel, out_shape=post_shapes + (shape((nx, ny, nz))...  2.6 us
  transfers between devices with their start and end apart: 14, of which 6 were waited for; matrix products, arithmetic and copies ran while one was open for 0% of the time, Pallas kernels for 21%

profile of v5, /device:TPU:0, one launch (start us, length us, event | category | flops | bytes accessed | tf_op | source)
XLA Modules:
  0.0 56.1 jit_solution(17449801509431274252)
XLA Ops:
  0.6 2.6 %first.1 = (f32[19,16,8,256]{3,2,1,0:T(8,128)S(1)}, f32[80,256]{1,0:T(8,128)S(1)}, f32[80,256]{1,0:T(8,128)S(1)}, f32[16,8,256]{2,1,0:T(8,128)S(1)}, s32[16,8,256]{2,1,0:T(8,128)S(1)}) custom-call(f32[19,16,8,256]{3,2,1,0:T(8,128)} %f_hbm.1, f32[16,8,256]{2,1,0:T(8,128)} %om_hbm.1, s32[16,8,256]{2,1,0:T(8,128)} %so_hbm.1), custom_call_target="tpu_custom_call" | custom-call | tf_op jit(solution)/shard_map/first/pallas_call | solution.py:627
  3.2 3.0 %collective-permute-start = (f32[80,256]{1,0:T(8,128)S(1)}, f32[80,256]{1,0:T(8,128)S(1)}, u32[]{:S(2)}, u32[]{:S(2)}) collective-permute-start(f32[80,256]{1,0:T(8,128)S(1)} %get-tuple-element.28), channel_id=1, source_target_pairs={{0,1},{1,0},{2,3},{3,2},{4,5},{5,4},{6,7},{7,6},{8,9},{9,8},{10,11... | collective-permute-start | bytes 245768 | tf_op jit(solution)/shard_map/ppermute | solution.py:68
  6.3 1.5 %collective-permute-start.1 = (f32[80,256]{1,0:T(8,128)S(1)}, f32[80,256]{1,0:T(8,128)S(1)}, u32[]{:S(2)}, u32[]{:S(2)}) collective-permute-start(f32[80,256]{1,0:T(8,128)S(1)} %get-tuple-element.29), channel_id=1, source_target_pairs={{0,3},{1,2},{2,1},{3,0},{4,7},{5,6},{6,5},{7,4},{8,11},{9,10},{10,... | collective-permute-start | bytes 245768 | tf_op jit(solution)/shard_map/ppermute | solution.py:68
  7.8 4.9 %gram.1 = (f32[96,80,128]{2,1,0:T(8,128)S(1)}, bf16[160,12288]{1,0:T(8,128)(2,1)}, f32[80,80]{1,0:T(8,128)S(1)}, f32[80,128]{1,0:T(8,128)S(1)}) custom-call(f32[1,64]{1,0:T(1,128)} %bitcast.14, f32[64,96,128]{2,1,0:T(8,128)} %bitcast.8, f32[15,96,128]{2,1,0:T(8,128)} %bitcast.12, f32[16,8,256]{2,1,0:T(8,128)S(1)} %get-tuple-element.30.gate_ref.om_ref), custom_call_target="tpu_custom_call" | custom-call | tf_op jit(solution)/shard_map/gram/pallas_call | solution.py:642
  12.6 0.0 collective-permute-done.ya_ref.sa_ref
  12.7 0.0 collective-permute-done.1.yb_ref.sb_ref
  12.7 0.1 collective-permute-start.2
  12.8 3.7 %collective-permute-start.3 = (f32[5,8,256]{2,1,0:T(8,128)S(1)}, f32[5,8,256]{2,1,0:T(8,128)S(1)}, u32[]{:S(2)}, u32[]{:S(2)}) collective-permute-start(f32[5,8,256]{2,1,0:T(8,128)S(1)} %get-tuple-element.33), channel_id=1, source_target_pairs={{0,28},{4,8},{8,4},{12,16},{16,12},{20,24},{24,20},{28,0},{1,29},{... | collective-permute-start | bytes 122888 | tf_op jit(solution)/shard_map/ppermute | solution.py:68
  16.5 0.0 collective-permute-start.4
  16.5 1.2 %collective-permute-done.4 = f32[80,80]{1,0:T(8,128)S(1)} collective-permute-done((f32[80,80]{1,0:T(8,128)S(1)}, f32[80,80]{1,0:T(8,128)S(1)}, u32[]{:S(2)}, u32[]{:S(2)}) %collective-permute-start.4) | collective-permute-done | bytes 25632 | tf_op jit(solution)/shard_map/ppermute | solution.py:610
  17.7 0.0 collective-permute-done.2.ra_ref
  17.7 0.6 collective-permute-done.3.rb_ref
  18.3 1.5 %second.1 = (f32[19,16,8,256]{3,2,1,0:T(8,128)S(1)}, f32[80,256]{1,0:T(8,128)S(1)}, f32[80,256]{1,0:T(8,128)S(1)}) custom-call(f32[19,16,8,256]{3,2,1,0:T(8,128)S(1)} %get-tuple-element.27.post_ref.p_ref, f32[5,8,256]{2,1,0:T(8,128)S(1)} %collective-permute-done.2.ra_ref, f32[5,8,256]{2,1,0:T(8,128)S(1)} %collective-permute-done.3.rb_ref, ...), custom_call_target="tpu_custom_call" | custom-call | tf_op jit(solution)/shard_map/second/pallas_call | solution.py:675
  19.8 1.6 %collective-permute-start.5 = (f32[80,256]{1,0:T(8,128)S(1)}, f32[80,256]{1,0:T(8,128)S(1)}, u32[]{:S(2)}, u32[]{:S(2)}) collective-permute-start(f32[80,256]{1,0:T(8,128)S(1)} %get-tuple-element.36), channel_id=1, source_target_pairs={{0,1},{1,0},{2,3},{3,2},{4,5},{5,4},{6,7},{7,6},{8,9},{9,8},{10,11... | collective-permute-start | bytes 245768 | tf_op jit(solution)/shard_map/ppermute | solution.py:68
  21.4 0.5 collective-permute-start.6
  21.8 1.5 %collective-permute-start.7 = (f32[80,80]{1,0:T(8,128)S(1)}, f32[80,80]{1,0:T(8,128)S(1)}, u32[]{:S(2)}, u32[]{:S(2)}) collective-permute-start(f32[80,80]{1,0:T(8,128)S(1)} %add.15.gate_ref), channel_id=1, source_target_pairs={{0,1},{1,0},{2,3},{3,2},{4,5},{5,4},{6,7},{7,6},{8,9},{9,8},{10,11... | collective-permute-start | bytes 76808 | tf_op jit(solution)/shard_map/ppermute | solution.py:610
  23.3 3.4 %collective-permute-done.7 = f32[80,80]{1,0:T(8,128)S(1)} collective-permute-done((f32[80,80]{1,0:T(8,128)S(1)}, f32[80,80]{1,0:T(8,128)S(1)}, u32[]{:S(2)}, u32[]{:S(2)}) %collective-permute-start.7) | collective-permute-done | bytes 25632 | tf_op jit(solution)/shard_map/ppermute | solution.py:610
  26.8 0.5 collective-permute-start.8
  27.3 3.5 %collective-permute-done.8 = f32[80,80]{1,0:T(8,128)S(1)} collective-permute-done((f32[80,80]{1,0:T(8,128)S(1)}, f32[80,80]{1,0:T(8,128)S(1)}, u32[]{:S(2)}, u32[]{:S(2)}) %collective-permute-start.8) | collective-permute-done | bytes 25632 | tf_op jit(solution)/shard_map/ppermute | solution.py:610
  30.8 0.0 collective-permute-done.5.ya_ref.sa_ref
  30.8 0.0 collective-permute-done.6.yb_ref.sb_ref
  30.9 0.1 collective-permute-start.9
  30.9 2.4 %collective-permute-start.10 = (f32[5,8,256]{2,1,0:T(8,128)S(1)}, f32[5,8,256]{2,1,0:T(8,128)S(1)}, u32[]{:S(2)}, u32[]{:S(2)}) collective-permute-start(f32[5,8,256]{2,1,0:T(8,128)S(1)} %get-tuple-element.39), channel_id=1, source_target_pairs={{0,28},{4,8},{8,4},{12,16},{16,12},{20,24},{24,20},{28,0},{1,29},{... | collective-permute-start | bytes 122888 | tf_op jit(solution)/shard_map/ppermute | solution.py:68
  33.4 0.0 collective-permute-start.11
  33.4 4.9 %collective-permute-done.11 = f32[80,80]{1,0:T(8,128)S(1)} collective-permute-done((f32[80,80]{1,0:T(8,128)S(1)}, f32[80,80]{1,0:T(8,128)S(1)}, u32[]{:S(2)}, u32[]{:S(2)}) %collective-permute-start.11) | collective-permute-done | bytes 25632 | tf_op jit(solution)/shard_map/ppermute | solution.py:610
  38.3 0.0 collective-permute-done.9.ra_ref
  38.3 0.0 collective-permute-done.10.rb_ref
  38.3 2.0 %final.1 = (f32[19,16,8,256]{3,2,1,0:T(8,128)}, f32[96,128]{1,0:T(8,128)S(1)}, f32[32,128]{1,0:T(8,128)}) custom-call(f32[19,16,8,256]{3,2,1,0:T(8,128)S(1)} %get-tuple-element.35.post_ref.p_ref, f32[5,8,256]{2,1,0:T(8,128)S(1)} %collective-permute-done.9.ra_ref, f32[5,8,256]{2,1,0:T(8,128)S(1)} %collective-permute-done.10.rb_ref, ...), custom_call_target="tpu_custom_call" | custom-call | tf_op jit(solution)/shard_map/final/pallas_call | solution.py:695
  40.3 3.0 %all-to-all-start = ((f32[32,1,128]{2,1,0:T(1,128)}), f32[32,1,128]{2,1,0:T(1,128)S(1)}, u32[]{:S(2)}, u32[]{:S(2)}) async-start(f32[32,1,128]{2,1,0:T(1,128)} %bitcast.4), calls=%async_computation | async-start | bytes 32768 | tf_op jit(solution)/shard_map/all_to_all | solution.py:696
  43.3 1.8 %collective-permute-start.12 = (f32[80,80]{1,0:T(8,128)S(1)}, f32[80,80]{1,0:T(8,128)S(1)}, u32[]{:S(2)}, u32[]{:S(2)}) collective-permute-start(f32[80,80]{1,0:T(8,128)S(1)} %add.18.gate_ref), channel_id=1, source_target_pairs={{0,2},{1,3},{2,0},{3,1},{4,6},{5,7},{6,4},{7,5},{8,10},{9,11},{10,... | collective-permute-start | bytes 76808 | tf_op jit(solution)/shard_map/ppermute | solution.py:610
  45.2 2.3 %collective-permute-done.12 = f32[80,80]{1,0:T(8,128)S(1)} collective-permute-done((f32[80,80]{1,0:T(8,128)S(1)}, f32[80,80]{1,0:T(8,128)S(1)}, u32[]{:S(2)}, u32[]{:S(2)}) %collective-permute-start.12) | collective-permute-done | bytes 25632 | tf_op jit(solution)/shard_map/ppermute | solution.py:610
  47.4 2.3 %factor.1 = (f32[80,80]{1,0:T(8,128)S(1)}, f32[80,80]{1,0:T(8,128)S(1)}, f32[80,240]{1,0:T(8,128)S(1)}) custom-call(f32[80,80]{1,0:T(8,128)S(1)} %add.19.refs_0_), custom_call_target="tpu_custom_call" | custom-call | tf_op jit(solution)/shard_map/factor/pallas_call | solution.py:698
  49.7 0.0 copy-start
  49.8 4.4 %rotate.1.refs_7_ = f32[80,96,128]{2,1,0:T(8,128)} custom-call(f32[80,240]{1,0:T(8,128)S(1)} %get-tuple-element.47.w_ref, bf16[160,12288]{1,0:T(8,128)(2,1)} %get-tuple-element.48.h_hbm), custom_call_target="tpu_custom_call" | custom-call | tf_op jit(solution)/shard_map/rotate/pallas_call | solution.py:704
  54.1 0.0 all-to-all-done
  54.1 0.0 copy-done
  54.2 2.0 %last.1 = (f32[80,80]{1,0:T(8,128)}, f32[80,96,128]{2,1,0:T(8,128)}) custom-call(f32[32,128]{1,0:T(8,128)S(1)} %bitcast.10, f32[80,80]{1,0:T(8,128)S(1)} %get-tuple-element.43.refs_1_, f32[80,80]{1,0:T(8,128)S(1)} %get-tuple-element.44.refs_2_, f32[80,128]{1,0:T(8,128)S(1)} %get-tuple-element.45.refs_3_, ...), custom_call_target="tpu_custom_call", output_to_operand_aliasing={{1}: (7, {})} | custom-call | tf_op jit(solution)/shard_map/last/pallas_call | solution.py:718
  (7 shorter events, 0.1 us)
Async XLA Ops:
  3.2 9.4 %collective-permute-start = (f32[80,256]{1,0:T(8,128)S(1)}, f32[80,256]{1,0:T(8,128)S(1)}, u32[]{:S(2)}, u32[]{:S(2)}) collective-permute-start(f32[80,256]{1,0:T(8,128)S(1)} %get-tuple-element.28), channel_id=1, source_target_pairs={{0,1},{1,0},{2,3},{3,2},{4,5},{5,4},{6,7},{7,6},{8,9},{9,8},{10,11... | collective-permute-start | bytes 245768 | tf_op jit(solution)/shard_map/ppermute | solution.py:68
  6.3 6.4 %collective-permute-start.1 = (f32[80,256]{1,0:T(8,128)S(1)}, f32[80,256]{1,0:T(8,128)S(1)}, u32[]{:S(2)}, u32[]{:S(2)}) collective-permute-start(f32[80,256]{1,0:T(8,128)S(1)} %get-tuple-element.29), channel_id=1, source_target_pairs={{0,3},{1,2},{2,1},{3,0},{4,7},{5,6},{6,5},{7,4},{8,11},{9,10},{10,... | collective-permute-start | bytes 245768 | tf_op jit(solution)/shard_map/ppermute | solution.py:68
  12.7 5.0 %collective-permute-start.2 = (f32[5,8,256]{2,1,0:T(8,128)S(1)}, f32[5,8,256]{2,1,0:T(8,128)S(1)}, u32[]{:S(2)}, u32[]{:S(2)}) collective-permute-start(f32[5,8,256]{2,1,0:T(8,128)S(1)} %get-tuple-element.32), channel_id=1, source_target_pairs={{0,4},{4,0},{8,12},{12,8},{16,20},{20,16},{24,28},{28,24},{1,5},{5... | collective-permute-start | bytes 122888 | tf_op jit(solution)/shard_map/ppermute | solution.py:68
  12.8 5.5 %collective-permute-start.3 = (f32[5,8,256]{2,1,0:T(8,128)S(1)}, f32[5,8,256]{2,1,0:T(8,128)S(1)}, u32[]{:S(2)}, u32[]{:S(2)}) collective-permute-start(f32[5,8,256]{2,1,0:T(8,128)S(1)} %get-tuple-element.33), channel_id=1, source_target_pairs={{0,28},{4,8},{8,4},{12,16},{16,12},{20,24},{24,20},{28,0},{1,29},{... | collective-permute-start | bytes 122888 | tf_op jit(solution)/shard_map/ppermute | solution.py:68
  16.5 1.2 %collective-permute-start.4 = (f32[80,80]{1,0:T(8,128)S(1)}, f32[80,80]{1,0:T(8,128)S(1)}, u32[]{:S(2)}, u32[]{:S(2)}) collective-permute-start(f32[80,80]{1,0:T(8,128)S(1)} %get-tuple-element.31.gate_ref), channel_id=1, source_target_pairs={{0,4},{4,0},{8,12},{12,8},{16,20},{20,16},{24,28},{28,24},{1,5},{5... | collective-permute-start | bytes 76808 | tf_op jit(solution)/shard_map/ppermute | solution.py:610
  19.8 11.0 %collective-permute-start.5 = (f32[80,256]{1,0:T(8,128)S(1)}, f32[80,256]{1,0:T(8,128)S(1)}, u32[]{:S(2)}, u32[]{:S(2)}) collective-permute-start(f32[80,256]{1,0:T(8,128)S(1)} %get-tuple-element.36), channel_id=1, source_target_pairs={{0,1},{1,0},{2,3},{3,2},{4,5},{5,4},{6,7},{7,6},{8,9},{9,8},{10,11... | collective-permute-start | bytes 245768 | tf_op jit(solution)/shard_map/ppermute | solution.py:68
  21.4 9.4 %collective-permute-start.6 = (f32[80,256]{1,0:T(8,128)S(1)}, f32[80,256]{1,0:T(8,128)S(1)}, u32[]{:S(2)}, u32[]{:S(2)}) collective-permute-start(f32[80,256]{1,0:T(8,128)S(1)} %get-tuple-element.37), channel_id=1, source_target_pairs={{0,3},{1,2},{2,1},{3,0},{4,7},{5,6},{6,5},{7,4},{8,11},{9,10},{10,... | collective-permute-start | bytes 245768 | tf_op jit(solution)/shard_map/ppermute | solution.py:68
  21.8 4.9 %collective-permute-start.7 = (f32[80,80]{1,0:T(8,128)S(1)}, f32[80,80]{1,0:T(8,128)S(1)}, u32[]{:S(2)}, u32[]{:S(2)}) collective-permute-start(f32[80,80]{1,0:T(8,128)S(1)} %add.15.gate_ref), channel_id=1, source_target_pairs={{0,1},{1,0},{2,3},{3,2},{4,5},{5,4},{6,7},{7,6},{8,9},{9,8},{10,11... | collective-permute-start | bytes 76808 | tf_op jit(solution)/shard_map/ppermute | solution.py:610
  26.8 4.0 %collective-permute-start.8 = (f32[80,80]{1,0:T(8,128)S(1)}, f32[80,80]{1,0:T(8,128)S(1)}, u32[]{:S(2)}, u32[]{:S(2)}) collective-permute-start(f32[80,80]{1,0:T(8,128)S(1)} %add.16), channel_id=1, source_target_pairs={{0,8},{4,12},{8,0},{12,4},{16,24},{20,28},{24,16},{28,20},{1,9},{5... | collective-permute-start | bytes 76808 | tf_op jit(solution)/shard_map/ppermute | solution.py:610
  30.9 7.4 %collective-permute-start.9 = (f32[5,8,256]{2,1,0:T(8,128)S(1)}, f32[5,8,256]{2,1,0:T(8,128)S(1)}, u32[]{:S(2)}, u32[]{:S(2)}) collective-permute-start(f32[5,8,256]{2,1,0:T(8,128)S(1)} %get-tuple-element.38), channel_id=1, source_target_pairs={{0,4},{4,0},{8,12},{12,8},{16,20},{20,16},{24,28},{28,24},{1,5},{5... | collective-permute-start | bytes 122888 | tf_op jit(solution)/shard_map/ppermute | solution.py:68
  30.9 7.3 %collective-permute-start.10 = (f32[5,8,256]{2,1,0:T(8,128)S(1)}, f32[5,8,256]{2,1,0:T(8,128)S(1)}, u32[]{:S(2)}, u32[]{:S(2)}) collective-permute-start(f32[5,8,256]{2,1,0:T(8,128)S(1)} %get-tuple-element.39), channel_id=1, source_target_pairs={{0,28},{4,8},{8,4},{12,16},{16,12},{20,24},{24,20},{28,0},{1,29},{... | collective-permute-start | bytes 122888 | tf_op jit(solution)/shard_map/ppermute | solution.py:68
  33.4 4.9 %collective-permute-start.11 = (f32[80,80]{1,0:T(8,128)S(1)}, f32[80,80]{1,0:T(8,128)S(1)}, u32[]{:S(2)}, u32[]{:S(2)}) collective-permute-start(f32[80,80]{1,0:T(8,128)S(1)} %add.17.gate_ref), channel_id=1, source_target_pairs={{0,16},{4,20},{8,24},{12,28},{16,0},{20,4},{24,8},{28,12},{1,17},{... | collective-permute-start | bytes 76808 | tf_op jit(solution)/shard_map/ppermute | solution.py:610
  40.3 13.9 %all-to-all-start = ((f32[32,1,128]{2,1,0:T(1,128)}), f32[32,1,128]{2,1,0:T(1,128)S(1)}, u32[]{:S(2)}, u32[]{:S(2)}) async-start(f32[32,1,128]{2,1,0:T(1,128)} %bitcast.4), calls=%async_computation | async-start | bytes 32768 | tf_op jit(solution)/shard_map/all_to_all | solution.py:696
  43.3 4.1 %collective-permute-start.12 = (f32[80,80]{1,0:T(8,128)S(1)}, f32[80,80]{1,0:T(8,128)S(1)}, u32[]{:S(2)}, u32[]{:S(2)}) collective-permute-start(f32[80,80]{1,0:T(8,128)S(1)} %add.18.gate_ref), channel_id=1, source_target_pairs={{0,2},{1,3},{2,0},{3,1},{4,6},{5,7},{6,4},{7,5},{8,10},{9,11},{10,... | collective-permute-start | bytes 76808 | tf_op jit(solution)/shard_map/ppermute | solution.py:610
  49.7 4.4 %copy-start = (f32[64,3,8,4,128]{4,3,2,1,0:T(4,128)S(1)}, f32[64,3,8,4,128]{4,3,2,1,0:T(4,128)}, u32[]{:S(2)}) copy-start(f32[64,3,8,4,128]{4,3,2,1,0:T(4,128)} %param.10) | copy-start | bytes 9437188

commit v6 on v5

--- a/solution.py
+++ b/solution.py
@@ -327,20 +327,34 @@
     flipped = lax.dot_general(
         eye, cross, (((1,), (1,)), ((), ())), precision=HIGHEST, preferred_element_type=F32
     )
-    g_ref[...] = acc[:cols, :] + cross + flipped
+    total = acc[:cols, :] + cross + flipped
+    half, width = g_ref.shape
+    total = jnp.concatenate([total, jnp.zeros((cols, width - cols), F32)], axis=1)
+    lane = lax.broadcasted_iota(jnp.int32, (half, width), 1)
+    g_ref[...] = jnp.where(lane < cols, total[:half], pltpu.roll(total[half:], half, 1))
     lax.fori_loop(0, depth // 8, finish, 0)
 
 
 def factor_kernel(inv_rows, g_ref, u_ref, li_ref, w_ref):
-    cols = g_ref.shape[0]
+    half, width = g_ref.shape
+    cols = 2 * half
     known = cols - 1
     blocks = cols // 8
-    pad = jnp.zeros((8, 128 - cols), F32)
+    top = g_ref[...] * inv_rows
+    pick = (
+        lax.broadcasted_iota(jnp.int32, (half, width), 1)
+        == lax.broadcasted_iota(jnp.int32, (half, width), 0) + half
+    ).astype(F32)
+    mirror = lax.dot_general(
+        pick, top, (((1,), (1,)), ((), ())), precision=HIGHEST, preferred_element_type=F32
+    )
+    mirror = jnp.concatenate([mirror, jnp.zeros((half, width - half), F32)], axis=1)
+    across = lax.broadcasted_iota(jnp.int32, (half, width), 1)
+    bottom = jnp.where(across < half, mirror, pltpu.roll(top, width - half, 1))
+    gram = jnp.concatenate([top, bottom], axis=0)
     sub = lax.broadcasted_iota(jnp.int32, (8, 128), 0)
     lane = lax.broadcasted_iota(jnp.int32, (8, 128), 1)
-    left = [
-        jnp.concatenate([g_ref[8 * b : 8 * b + 8, :] * inv_rows, pad], axis=1) for b in range(blocks)
-    ]
+    left = [gram[8 * b : 8 * b + 8, :] for b in range(blocks)]
     right = [(sub + 8 * b == lane).astype(F32) for b in range(blocks)]
     for p in range(blocks):
         live = range(p, blocks)
@@ -644,7 +658,7 @@
         out_shape=(
             shape((depth, cols, 128)),
             pltpu.HBM((2 * cols, depth * 128), BF16),
-            shape((cols, cols)),
+            shape((cols // 2, 128)),
             shape((cols, 128)),
         ),
         in_specs=[HBM, HBM, HBM, ANY],

time: 56.3 us -> 54.8 us (0.973)
  waiting for transfers between devices: 15.9 us -> 14.8 us
    ppermute x5, waiting for transfers between devices: 15.3 us -> 14.2 us  [exchange(): other = lax.ppermute(value, axis, pairs)]
where the time goes in v6:
time: 54.8 us; the launch traced here: 54.6 us
  Pallas kernels  19.8 us (36%)
  starting transfers between devices  19.2 us (35%)
  waiting for transfers between devices  14.8 us (27%)
  between operations  0.78 us (1%)
    ppermute x5, waiting for transfers between devices, exchange(): other = lax.ppermute(value, axis, pairs)  14.2 us
    ppermute x4, starting transfers between devices, swap(): lax.ppermute(values[1], axis, other)  8.11 us
    pallas_call x1, Pallas kernels, on_device(): pl.pallas_call(gram_kernel, out_shape=(shape((depth, cols, 128)), pltpu.H...  4.92 us
    ppermute x4, starting transfers between devices, swap(): lax.ppermute(values[0], axis, partner)  4.75 us
    pallas_call x1, Pallas kernels, on_device(): pl.pallas_call(rotate_kernel, out_shape=shape((cols, depth, 128)), in_spe...  4.37 us
    ppermute x5, starting transfers between devices, exchange(): other = lax.ppermute(value, axis, pairs)  3.78 us
    pallas_call x1, Pallas kernels, on_device(): pl.pallas_call(first_kernel, out_shape=post_shapes + (shape((nx, ny, nz))...  2.6 us
    all_to_all x1, starting transfers between devices, on_device(): lines = lax.all_to_all(line, ('gx', 'gy'), 0, 0, tiled=True)  2.56 us
  transfers between devices with their start and end apart: 14, of which 6 were waited for; matrix products, arithmetic and copies ran while one was open for 0% of the time, Pallas kernels for 21%

profile of v6, /device:TPU:0, one launch (start us, length us, event | category | flops | bytes accessed | tf_op | source)
XLA Modules:
  0.0 54.6 jit_solution(10663653013979544506)
XLA Ops:
  0.6 2.6 %first.1 = (f32[19,16,8,256]{3,2,1,0:T(8,128)S(1)}, f32[80,256]{1,0:T(8,128)S(1)}, f32[80,256]{1,0:T(8,128)S(1)}, f32[16,8,256]{2,1,0:T(8,128)S(1)}, s32[16,8,256]{2,1,0:T(8,128)S(1)}) custom-call(f32[19,16,8,256]{3,2,1,0:T(8,128)} %f_hbm.1, f32[16,8,256]{2,1,0:T(8,128)} %om_hbm.1, s32[16,8,256]{2,1,0:T(8,128)} %so_hbm.1), custom_call_target="tpu_custom_call" | custom-call | tf_op jit(solution)/shard_map/first/pallas_call | solution.py:641
  3.2 3.0 %collective-permute-start = (f32[80,256]{1,0:T(8,128)S(1)}, f32[80,256]{1,0:T(8,128)S(1)}, u32[]{:S(2)}, u32[]{:S(2)}) collective-permute-start(f32[80,256]{1,0:T(8,128)S(1)} %get-tuple-element.28), channel_id=1, source_target_pairs={{0,1},{1,0},{2,3},{3,2},{4,5},{5,4},{6,7},{7,6},{8,9},{9,8},{10,11... | collective-permute-start | bytes 245768 | tf_op jit(solution)/shard_map/ppermute | solution.py:68
  6.3 1.5 %collective-permute-start.1 = (f32[80,256]{1,0:T(8,128)S(1)}, f32[80,256]{1,0:T(8,128)S(1)}, u32[]{:S(2)}, u32[]{:S(2)}) collective-permute-start(f32[80,256]{1,0:T(8,128)S(1)} %get-tuple-element.29), channel_id=1, source_target_pairs={{0,3},{1,2},{2,1},{3,0},{4,7},{5,6},{6,5},{7,4},{8,11},{9,10},{10,... | collective-permute-start | bytes 245768 | tf_op jit(solution)/shard_map/ppermute | solution.py:68
  7.8 4.9 %gram.1 = (f32[96,80,128]{2,1,0:T(8,128)S(1)}, bf16[160,12288]{1,0:T(8,128)(2,1)}, f32[40,128]{1,0:T(8,128)S(1)}, f32[80,128]{1,0:T(8,128)S(1)}) custom-call(f32[1,64]{1,0:T(1,128)} %bitcast.14, f32[64,96,128]{2,1,0:T(8,128)} %bitcast.8, f32[15,96,128]{2,1,0:T(8,128)} %bitcast.12, f32[16,8,256]{2,1,0:T(8,128)S(1)} %get-tuple-element.30.gate_ref.om_ref), custom_call_target="tpu_custom_call" | custom-call | tf_op jit(solution)/shard_map/gram/pallas_call | solution.py:656
  12.7 0.0 collective-permute-done.ya_ref.sa_ref
  12.7 0.0 collective-permute-done.1.yb_ref.sb_ref
  12.8 0.1 collective-permute-start.2
  12.8 3.7 %collective-permute-start.3 = (f32[5,8,256]{2,1,0:T(8,128)S(1)}, f32[5,8,256]{2,1,0:T(8,128)S(1)}, u32[]{:S(2)}, u32[]{:S(2)}) collective-permute-start(f32[5,8,256]{2,1,0:T(8,128)S(1)} %get-tuple-element.33), channel_id=1, source_target_pairs={{0,28},{4,8},{8,4},{12,16},{16,12},{20,24},{24,20},{28,0},{1,29},{... | collective-permute-start | bytes 122888 | tf_op jit(solution)/shard_map/ppermute | solution.py:68
  16.5 0.0 collective-permute-start.4
  16.5 1.2 %collective-permute-done.4 = f32[40,128]{1,0:T(8,128)S(1)} collective-permute-done((f32[40,128]{1,0:T(8,128)S(1)}, f32[40,128]{1,0:T(8,128)S(1)}, u32[]{:S(2)}, u32[]{:S(2)}) %collective-permute-start.4) | collective-permute-done | bytes 20512 | tf_op jit(solution)/shard_map/ppermute | solution.py:624
  17.7 0.0 collective-permute-done.2.ra_ref
  17.7 0.6 %collective-permute-done.3.rb_ref = f32[5,8,256]{2,1,0:T(8,128)S(1)} collective-permute-done((f32[5,8,256]{2,1,0:T(8,128)S(1)}, f32[5,8,256]{2,1,0:T(8,128)S(1)}, u32[]{:S(2)}, u32[]{:S(2)}) %collective-permute-start.3) | collective-permute-done | bytes 40992 | tf_op jit(solution)/shard_map/ppermute | solution.py:68
  18.3 1.5 %second.1 = (f32[19,16,8,256]{3,2,1,0:T(8,128)S(1)}, f32[80,256]{1,0:T(8,128)S(1)}, f32[80,256]{1,0:T(8,128)S(1)}) custom-call(f32[19,16,8,256]{3,2,1,0:T(8,128)S(1)} %get-tuple-element.27.post_ref.p_ref, f32[5,8,256]{2,1,0:T(8,128)S(1)} %collective-permute-done.2.ra_ref, f32[5,8,256]{2,1,0:T(8,128)S(1)} %collective-permute-done.3.rb_ref, ...), custom_call_target="tpu_custom_call" | custom-call | tf_op jit(solution)/shard_map/second/pallas_call | solution.py:689
  19.9 1.6 %collective-permute-start.5 = (f32[80,256]{1,0:T(8,128)S(1)}, f32[80,256]{1,0:T(8,128)S(1)}, u32[]{:S(2)}, u32[]{:S(2)}) collective-permute-start(f32[80,256]{1,0:T(8,128)S(1)} %get-tuple-element.36), channel_id=1, source_target_pairs={{0,1},{1,0},{2,3},{3,2},{4,5},{5,4},{6,7},{7,6},{8,9},{9,8},{10,11... | collective-permute-start | bytes 245768 | tf_op jit(solution)/shard_map/ppermute | solution.py:68
  21.4 0.5 collective-permute-start.6
  21.9 1.5 %collective-permute-start.7 = (f32[40,128]{1,0:T(8,128)S(1)}, f32[40,128]{1,0:T(8,128)S(1)}, u32[]{:S(2)}, u32[]{:S(2)}) collective-permute-start(f32[40,128]{1,0:T(8,128)S(1)} %add.15.gate_ref), channel_id=1, source_target_pairs={{0,1},{1,0},{2,3},{3,2},{4,5},{5,4},{6,7},{7,6},{8,9},{9,8},{10,11... | collective-permute-start | bytes 61448 | tf_op jit(solution)/shard_map/ppermute | solution.py:624
  23.4 3.0 %collective-permute-done.7 = f32[40,128]{1,0:T(8,128)S(1)} collective-permute-done((f32[40,128]{1,0:T(8,128)S(1)}, f32[40,128]{1,0:T(8,128)S(1)}, u32[]{:S(2)}, u32[]{:S(2)}) %collective-permute-start.7) | collective-permute-done | bytes 20512 | tf_op jit(solution)/shard_map/ppermute | solution.py:624
  26.4 0.6 %collective-permute-start.8 = (f32[40,128]{1,0:T(8,128)S(1)}, f32[40,128]{1,0:T(8,128)S(1)}, u32[]{:S(2)}, u32[]{:S(2)}) collective-permute-start(f32[40,128]{1,0:T(8,128)S(1)} %add.16), channel_id=1, source_target_pairs={{0,8},{4,12},{8,0},{12,4},{16,24},{20,28},{24,16},{28,20},{1,9},{5... | collective-permute-start | bytes 61448 | tf_op jit(solution)/shard_map/ppermute | solution.py:624
  26.9 3.2 %collective-permute-done.8 = f32[40,128]{1,0:T(8,128)S(1)} collective-permute-done((f32[40,128]{1,0:T(8,128)S(1)}, f32[40,128]{1,0:T(8,128)S(1)}, u32[]{:S(2)}, u32[]{:S(2)}) %collective-permute-start.8) | collective-permute-done | bytes 20512 | tf_op jit(solution)/shard_map/ppermute | solution.py:624
  30.2 0.0 collective-permute-done.5.ya_ref.sa_ref
  30.2 0.0 collective-permute-done.6.yb_ref.sb_ref
  30.2 0.1 collective-permute-start.9
  30.3 2.5 %collective-permute-start.10 = (f32[5,8,256]{2,1,0:T(8,128)S(1)}, f32[5,8,256]{2,1,0:T(8,128)S(1)}, u32[]{:S(2)}, u32[]{:S(2)}) collective-permute-start(f32[5,8,256]{2,1,0:T(8,128)S(1)} %get-tuple-element.39), channel_id=1, source_target_pairs={{0,28},{4,8},{8,4},{12,16},{16,12},{20,24},{24,20},{28,0},{1,29},{... | collective-permute-start | bytes 122888 | tf_op jit(solution)/shard_map/ppermute | solution.py:68
  32.8 0.0 collective-permute-start.11
  32.8 4.7 %collective-permute-done.11 = f32[40,128]{1,0:T(8,128)S(1)} collective-permute-done((f32[40,128]{1,0:T(8,128)S(1)}, f32[40,128]{1,0:T(8,128)S(1)}, u32[]{:S(2)}, u32[]{:S(2)}) %collective-permute-start.11) | collective-permute-done | bytes 20512 | tf_op jit(solution)/shard_map/ppermute | solution.py:624
  37.5 0.0 collective-permute-done.9.ra_ref
  37.5 0.0 collective-permute-done.10.rb_ref
  37.5 2.0 %final.1 = (f32[19,16,8,256]{3,2,1,0:T(8,128)}, f32[96,128]{1,0:T(8,128)S(1)}, f32[32,128]{1,0:T(8,128)}) custom-call(f32[19,16,8,256]{3,2,1,0:T(8,128)S(1)} %get-tuple-element.35.post_ref.p_ref, f32[5,8,256]{2,1,0:T(8,128)S(1)} %collective-permute-done.9.ra_ref, f32[5,8,256]{2,1,0:T(8,128)S(1)} %collective-permute-done.10.rb_ref, ...), custom_call_target="tpu_custom_call" | custom-call | tf_op jit(solution)/shard_map/final/pallas_call | solution.py:709
  39.5 2.6 %all-to-all-start = ((f32[32,1,128]{2,1,0:T(1,128)}), f32[32,1,128]{2,1,0:T(1,128)S(1)}, u32[]{:S(2)}, u32[]{:S(2)}) async-start(f32[32,1,128]{2,1,0:T(1,128)} %bitcast.4), calls=%async_computation | async-start | bytes 32768 | tf_op jit(solution)/shard_map/all_to_all | solution.py:710
  42.0 1.7 %collective-permute-start.12 = (f32[40,128]{1,0:T(8,128)S(1)}, f32[40,128]{1,0:T(8,128)S(1)}, u32[]{:S(2)}, u32[]{:S(2)}) collective-permute-start(f32[40,128]{1,0:T(8,128)S(1)} %add.18.gate_ref), channel_id=1, source_target_pairs={{0,2},{1,3},{2,0},{3,1},{4,6},{5,7},{6,4},{7,5},{8,10},{9,11},{10,... | collective-permute-start | bytes 61448 | tf_op jit(solution)/shard_map/ppermute | solution.py:624
  43.8 2.1 %collective-permute-done.12 = f32[40,128]{1,0:T(8,128)S(1)} collective-permute-done((f32[40,128]{1,0:T(8,128)S(1)}, f32[40,128]{1,0:T(8,128)S(1)}, u32[]{:S(2)}, u32[]{:S(2)}) %collective-permute-start.12) | collective-permute-done | bytes 20512 | tf_op jit(solution)/shard_map/ppermute | solution.py:624
  45.9 2.3 %factor.1 = (f32[80,80]{1,0:T(8,128)S(1)}, f32[80,80]{1,0:T(8,128)S(1)}, f32[80,240]{1,0:T(8,128)S(1)}) custom-call(f32[40,128]{1,0:T(8,128)S(1)} %add.19.refs_0_), custom_call_target="tpu_custom_call" | custom-call | tf_op jit(solution)/shard_map/factor/pallas_call | solution.py:712
  48.2 0.0 copy-start
  48.2 4.4 %rotate.1.refs_7_ = f32[80,96,128]{2,1,0:T(8,128)} custom-call(f32[80,240]{1,0:T(8,128)S(1)} %get-tuple-element.47.w_ref, bf16[160,12288]{1,0:T(8,128)(2,1)} %get-tuple-element.48.h_hbm), custom_call_target="tpu_custom_call" | custom-call | tf_op jit(solution)/shard_map/rotate/pallas_call | solution.py:718
  52.6 0.0 all-to-all-done
  52.6 0.0 copy-done
  52.6 2.0 %last.1 = (f32[80,80]{1,0:T(8,128)}, f32[80,96,128]{2,1,0:T(8,128)}) custom-call(f32[32,128]{1,0:T(8,128)S(1)} %bitcast.10, f32[80,80]{1,0:T(8,128)S(1)} %get-tuple-element.43.refs_1_, f32[80,80]{1,0:T(8,128)S(1)} %get-tuple-element.44.refs_2_, f32[80,128]{1,0:T(8,128)S(1)} %get-tuple-element.45.refs_3_, ...), custom_call_target="tpu_custom_call", output_to_operand_aliasing={{1}: (7, {})} | custom-call | tf_op jit(solution)/shard_map/last/pallas_call | solution.py:732
  (7 shorter events, 0.1 us)
Async XLA Ops:
  3.2 9.5 %collective-permute-start = (f32[80,256]{1,0:T(8,128)S(1)}, f32[80,256]{1,0:T(8,128)S(1)}, u32[]{:S(2)}, u32[]{:S(2)}) collective-permute-start(f32[80,256]{1,0:T(8,128)S(1)} %get-tuple-element.28), channel_id=1, source_target_pairs={{0,1},{1,0},{2,3},{3,2},{4,5},{5,4},{6,7},{7,6},{8,9},{9,8},{10,11... | collective-permute-start | bytes 245768 | tf_op jit(solution)/shard_map/ppermute | solution.py:68
  6.3 6.4 %collective-permute-start.1 = (f32[80,256]{1,0:T(8,128)S(1)}, f32[80,256]{1,0:T(8,128)S(1)}, u32[]{:S(2)}, u32[]{:S(2)}) collective-permute-start(f32[80,256]{1,0:T(8,128)S(1)} %get-tuple-element.29), channel_id=1, source_target_pairs={{0,3},{1,2},{2,1},{3,0},{4,7},{5,6},{6,5},{7,4},{8,11},{9,10},{10,... | collective-permute-start | bytes 245768 | tf_op jit(solution)/shard_map/ppermute | solution.py:68
  12.8 5.0 %collective-permute-start.2 = (f32[5,8,256]{2,1,0:T(8,128)S(1)}, f32[5,8,256]{2,1,0:T(8,128)S(1)}, u32[]{:S(2)}, u32[]{:S(2)}) collective-permute-start(f32[5,8,256]{2,1,0:T(8,128)S(1)} %get-tuple-element.32), channel_id=1, source_target_pairs={{0,4},{4,0},{8,12},{12,8},{16,20},{20,16},{24,28},{28,24},{1,5},{5... | collective-permute-start | bytes 122888 | tf_op jit(solution)/shard_map/ppermute | solution.py:68
  12.8 5.5 %collective-permute-start.3 = (f32[5,8,256]{2,1,0:T(8,128)S(1)}, f32[5,8,256]{2,1,0:T(8,128)S(1)}, u32[]{:S(2)}, u32[]{:S(2)}) collective-permute-start(f32[5,8,256]{2,1,0:T(8,128)S(1)} %get-tuple-element.33), channel_id=1, source_target_pairs={{0,28},{4,8},{8,4},{12,16},{16,12},{20,24},{24,20},{28,0},{1,29},{... | collective-permute-start | bytes 122888 | tf_op jit(solution)/shard_map/ppermute | solution.py:68
  16.5 1.2 %collective-permute-start.4 = (f32[40,128]{1,0:T(8,128)S(1)}, f32[40,128]{1,0:T(8,128)S(1)}, u32[]{:S(2)}, u32[]{:S(2)}) collective-permute-start(f32[40,128]{1,0:T(8,128)S(1)} %get-tuple-element.31.gate_ref), channel_id=1, source_target_pairs={{0,4},{4,0},{8,12},{12,8},{16,20},{20,16},{24,28},{28,24},{1,5},{5... | collective-permute-start | bytes 61448 | tf_op jit(solution)/shard_map/ppermute | solution.py:624
  19.9 10.3 %collective-permute-start.5 = (f32[80,256]{1,0:T(8,128)S(1)}, f32[80,256]{1,0:T(8,128)S(1)}, u32[]{:S(2)}, u32[]{:S(2)}) collective-permute-start(f32[80,256]{1,0:T(8,128)S(1)} %get-tuple-element.36), channel_id=1, source_target_pairs={{0,1},{1,0},{2,3},{3,2},{4,5},{5,4},{6,7},{7,6},{8,9},{9,8},{10,11... | collective-permute-start | bytes 245768 | tf_op jit(solution)/shard_map/ppermute | solution.py:68
  21.4 8.7 %collective-permute-start.6 = (f32[80,256]{1,0:T(8,128)S(1)}, f32[80,256]{1,0:T(8,128)S(1)}, u32[]{:S(2)}, u32[]{:S(2)}) collective-permute-start(f32[80,256]{1,0:T(8,128)S(1)} %get-tuple-element.37), channel_id=1, source_target_pairs={{0,3},{1,2},{2,1},{3,0},{4,7},{5,6},{6,5},{7,4},{8,11},{9,10},{10,... | collective-permute-start | bytes 245768 | tf_op jit(solution)/shard_map/ppermute | solution.py:68
  21.9 4.5 %collective-permute-start.7 = (f32[40,128]{1,0:T(8,128)S(1)}, f32[40,128]{1,0:T(8,128)S(1)}, u32[]{:S(2)}, u32[]{:S(2)}) collective-permute-start(f32[40,128]{1,0:T(8,128)S(1)} %add.15.gate_ref), channel_id=1, source_target_pairs={{0,1},{1,0},{2,3},{3,2},{4,5},{5,4},{6,7},{7,6},{8,9},{9,8},{10,11... | collective-permute-start | bytes 61448 | tf_op jit(solution)/shard_map/ppermute | solution.py:624
  26.4 3.8 %collective-permute-start.8 = (f32[40,128]{1,0:T(8,128)S(1)}, f32[40,128]{1,0:T(8,128)S(1)}, u32[]{:S(2)}, u32[]{:S(2)}) collective-permute-start(f32[40,128]{1,0:T(8,128)S(1)} %add.16), channel_id=1, source_target_pairs={{0,8},{4,12},{8,0},{12,4},{16,24},{20,28},{24,16},{28,20},{1,9},{5... | collective-permute-start | bytes 61448 | tf_op jit(solution)/shard_map/ppermute | solution.py:624
  30.2 7.2 %collective-permute-start.9 = (f32[5,8,256]{2,1,0:T(8,128)S(1)}, f32[5,8,256]{2,1,0:T(8,128)S(1)}, u32[]{:S(2)}, u32[]{:S(2)}) collective-permute-start(f32[5,8,256]{2,1,0:T(8,128)S(1)} %get-tuple-element.38), channel_id=1, source_target_pairs={{0,4},{4,0},{8,12},{12,8},{16,20},{20,16},{24,28},{28,24},{1,5},{5... | collective-permute-start | bytes 122888 | tf_op jit(solution)/shard_map/ppermute | solution.py:68
  30.3 7.2 %collective-permute-start.10 = (f32[5,8,256]{2,1,0:T(8,128)S(1)}, f32[5,8,256]{2,1,0:T(8,128)S(1)}, u32[]{:S(2)}, u32[]{:S(2)}) collective-permute-start(f32[5,8,256]{2,1,0:T(8,128)S(1)} %get-tuple-element.39), channel_id=1, source_target_pairs={{0,28},{4,8},{8,4},{12,16},{16,12},{20,24},{24,20},{28,0},{1,29},{... | collective-permute-start | bytes 122888 | tf_op jit(solution)/shard_map/ppermute | solution.py:68
  32.8 4.7 %collective-permute-start.11 = (f32[40,128]{1,0:T(8,128)S(1)}, f32[40,128]{1,0:T(8,128)S(1)}, u32[]{:S(2)}, u32[]{:S(2)}) collective-permute-start(f32[40,128]{1,0:T(8,128)S(1)} %add.17.gate_ref), channel_id=1, source_target_pairs={{0,16},{4,20},{8,24},{12,28},{16,0},{20,4},{24,8},{28,12},{1,17},{... | collective-permute-start | bytes 61448 | tf_op jit(solution)/shard_map/ppermute | solution.py:624
  39.5 13.1 %all-to-all-start = ((f32[32,1,128]{2,1,0:T(1,128)}), f32[32,1,128]{2,1,0:T(1,128)S(1)}, u32[]{:S(2)}, u32[]{:S(2)}) async-start(f32[32,1,128]{2,1,0:T(1,128)} %bitcast.4), calls=%async_computation | async-start | bytes 32768 | tf_op jit(solution)/shard_map/all_to_all | solution.py:710
  42.0 3.9 %collective-permute-start.12 = (f32[40,128]{1,0:T(8,128)S(1)}, f32[40,128]{1,0:T(8,128)S(1)}, u32[]{:S(2)}, u32[]{:S(2)}) collective-permute-start(f32[40,128]{1,0:T(8,128)S(1)} %add.18.gate_ref), channel_id=1, source_target_pairs={{0,2},{1,3},{2,0},{3,1},{4,6},{5,7},{6,4},{7,5},{8,10},{9,11},{10,... | collective-permute-start | bytes 61448 | tf_op jit(solution)/shard_map/ppermute | solution.py:624
  48.2 4.4 %copy-start = (f32[64,3,8,4,128]{4,3,2,1,0:T(4,128)S(1)}, f32[64,3,8,4,128]{4,3,2,1,0:T(4,128)}, u32[]{:S(2)}) copy-start(f32[64,3,8,4,128]{4,3,2,1,0:T(4,128)} %param.10) | copy-start | bytes 9437188

commit v7 on v6

--- a/solution.py
+++ b/solution.py
@@ -43,7 +43,7 @@
     return tuple(count * cut // 5 for cut in CUTS)
 
 
-UNROLL_F = 1
+UNROLL_F = 2
 HIGHEST = lax.Precision.HIGHEST
 F32 = jnp.float32
 BF16 = jnp.bfloat16
@@ -65,7 +65,9 @@
 
 def swap(values, axis):
     partner, other = ring_pairs(axis)
-    return lax.ppermute(values[0], axis, partner), lax.ppermute(values[1], axis, other)
+    near = lax.ppermute(values[0], axis, partner)
+    far = lax.ppermute(values[1], axis, other)
+    return near, far
 
 
 def by_parity(axis, place):
@@ -236,7 +238,7 @@
         emit_post(post, x, nx, post_ref, yup_ref, ydn_ref)
         return carry
 
-    lax.fori_loop(0, nx, step, 0, unroll=UNROLL)
+    lax.fori_loop(0, nx, step, 0, unroll=2 * UNROLL)
     emit_edges(yup_ref, ydn_ref, (ya_ref, yb_ref))
 
 
@@ -493,7 +495,7 @@
     def inner(r, acc):
         return acc + a_ref[r] * c_ref[pl.ds(r, 1), :]
 
-    acc = lax.fori_loop(0, depth, inner, jnp.zeros((cols, 128), F32), unroll=8)
+    acc = lax.fori_loop(0, depth, inner, jnp.zeros((cols, 128), F32), unroll=16)
     dots = jnp.sum(acc, axis=1, keepdims=True)
     own = jnp.sum(c_ref[...] * c_ref[...])
     down = lax.broadcasted_iota(jnp.int32, (cols, 1), 0)

time: 54.8 us -> 54.6 us (level)
  no operation moved by 1% of the time
where the time goes in v7:
time: 54.6 us; the launch traced here: 54.4 us
  Pallas kernels  19.6 us (36%)
  starting transfers between devices  19.2 us (35%)
  waiting for transfers between devices  14.8 us (27%)
  between operations  0.78 us (1%)
    ppermute x5, waiting for transfers between devices, exchange(): other = lax.ppermute(value, axis, pairs)  14.2 us
    ppermute x4, starting transfers between devices, swap(): far = lax.ppermute(values[1], axis, other)  8.11 us
    pallas_call x1, Pallas kernels, on_device(): pl.pallas_call(gram_kernel, out_shape=(shape((depth, cols, 128)), pltpu.H...  4.92 us
    ppermute x4, starting transfers between devices, swap(): near = lax.ppermute(values[0], axis, partner)  4.75 us
    pallas_call x1, Pallas kernels, on_device(): pl.pallas_call(rotate_kernel, out_shape=shape((cols, depth, 128)), in_spe...  4.37 us
    ppermute x5, starting transfers between devices, exchange(): other = lax.ppermute(value, axis, pairs)  3.78 us
    pallas_call x1, Pallas kernels, on_device(): pl.pallas_call(first_kernel, out_shape=post_shapes + (shape((nx, ny, nz))...  2.6 us
    all_to_all x1, starting transfers between devices, on_device(): lines = lax.all_to_all(line, ('gx', 'gy'), 0, 0, tiled=True)  2.56 us
  transfers between devices with their start and end apart: 14, of which 6 were waited for; matrix products, arithmetic and copies ran while one was open for 0% of the time, Pallas kernels for 21%

profile of v7, /device:TPU:0, one launch (start us, length us, event | category | flops | bytes accessed | tf_op | source)
XLA Modules:
  0.0 54.4 jit_solution(17141539434152297788)
XLA Ops:
  0.6 2.6 %first.1 = (f32[19,16,8,256]{3,2,1,0:T(8,128)S(1)}, f32[80,256]{1,0:T(8,128)S(1)}, f32[80,256]{1,0:T(8,128)S(1)}, f32[16,8,256]{2,1,0:T(8,128)S(1)}, s32[16,8,256]{2,1,0:T(8,128)S(1)}) custom-call(f32[19,16,8,256]{3,2,1,0:T(8,128)} %f_hbm.1, f32[16,8,256]{2,1,0:T(8,128)} %om_hbm.1, s32[16,8,256]{2,1,0:T(8,128)} %so_hbm.1), custom_call_target="tpu_custom_call" | custom-call | tf_op jit(solution)/shard_map/first/pallas_call | solution.py:643
  3.2 3.0 %collective-permute-start = (f32[80,256]{1,0:T(8,128)S(1)}, f32[80,256]{1,0:T(8,128)S(1)}, u32[]{:S(2)}, u32[]{:S(2)}) collective-permute-start(f32[80,256]{1,0:T(8,128)S(1)} %get-tuple-element.28), channel_id=1, source_target_pairs={{0,1},{1,0},{2,3},{3,2},{4,5},{5,4},{6,7},{7,6},{8,9},{9,8},{10,11... | collective-permute-start | bytes 245768 | tf_op jit(solution)/shard_map/ppermute | solution.py:68
  6.3 1.5 %collective-permute-start.1 = (f32[80,256]{1,0:T(8,128)S(1)}, f32[80,256]{1,0:T(8,128)S(1)}, u32[]{:S(2)}, u32[]{:S(2)}) collective-permute-start(f32[80,256]{1,0:T(8,128)S(1)} %get-tuple-element.29), channel_id=1, source_target_pairs={{0,3},{1,2},{2,1},{3,0},{4,7},{5,6},{6,5},{7,4},{8,11},{9,10},{10,... | collective-permute-start | bytes 245768 | tf_op jit(solution)/shard_map/ppermute | solution.py:69
  7.8 4.9 %gram.1 = (f32[96,80,128]{2,1,0:T(8,128)S(1)}, bf16[160,12288]{1,0:T(8,128)(2,1)}, f32[40,128]{1,0:T(8,128)S(1)}, f32[80,128]{1,0:T(8,128)S(1)}) custom-call(f32[1,64]{1,0:T(1,128)} %bitcast.14, f32[64,96,128]{2,1,0:T(8,128)} %bitcast.8, f32[15,96,128]{2,1,0:T(8,128)} %bitcast.12, f32[16,8,256]{2,1,0:T(8,128)S(1)} %get-tuple-element.30.gate_ref.om_ref), custom_call_target="tpu_custom_call" | custom-call | tf_op jit(solution)/shard_map/gram/pallas_call | solution.py:658
  12.7 0.0 collective-permute-done.ya_ref.sa_ref
  12.7 0.0 collective-permute-done.1.yb_ref.sb_ref
  12.8 0.1 collective-permute-start.2
  12.8 3.7 %collective-permute-start.3 = (f32[5,8,256]{2,1,0:T(8,128)S(1)}, f32[5,8,256]{2,1,0:T(8,128)S(1)}, u32[]{:S(2)}, u32[]{:S(2)}) collective-permute-start(f32[5,8,256]{2,1,0:T(8,128)S(1)} %get-tuple-element.33), channel_id=1, source_target_pairs={{0,28},{4,8},{8,4},{12,16},{16,12},{20,24},{24,20},{28,0},{1,29},{... | collective-permute-start | bytes 122888 | tf_op jit(solution)/shard_map/ppermute | solution.py:69
  16.5 0.0 collective-permute-start.4
  16.5 1.2 %collective-permute-done.4 = f32[40,128]{1,0:T(8,128)S(1)} collective-permute-done((f32[40,128]{1,0:T(8,128)S(1)}, f32[40,128]{1,0:T(8,128)S(1)}, u32[]{:S(2)}, u32[]{:S(2)}) %collective-permute-start.4) | collective-permute-done | bytes 20512 | tf_op jit(solution)/shard_map/ppermute | solution.py:626
  17.7 0.0 collective-permute-done.2.ra_ref
  17.7 0.6 %collective-permute-done.3.rb_ref = f32[5,8,256]{2,1,0:T(8,128)S(1)} collective-permute-done((f32[5,8,256]{2,1,0:T(8,128)S(1)}, f32[5,8,256]{2,1,0:T(8,128)S(1)}, u32[]{:S(2)}, u32[]{:S(2)}) %collective-permute-start.3) | collective-permute-done | bytes 40992 | tf_op jit(solution)/shard_map/ppermute | solution.py:69
  18.3 1.4 %second.1 = (f32[19,16,8,256]{3,2,1,0:T(8,128)S(1)}, f32[80,256]{1,0:T(8,128)S(1)}, f32[80,256]{1,0:T(8,128)S(1)}) custom-call(f32[19,16,8,256]{3,2,1,0:T(8,128)S(1)} %get-tuple-element.27.post_ref.p_ref, f32[5,8,256]{2,1,0:T(8,128)S(1)} %collective-permute-done.2.ra_ref, f32[5,8,256]{2,1,0:T(8,128)S(1)} %collective-permute-done.3.rb_ref, ...), custom_call_target="tpu_custom_call" | custom-call | tf_op jit(solution)/shard_map/second/pallas_call | solution.py:691
  19.7 1.6 %collective-permute-start.5 = (f32[80,256]{1,0:T(8,128)S(1)}, f32[80,256]{1,0:T(8,128)S(1)}, u32[]{:S(2)}, u32[]{:S(2)}) collective-permute-start(f32[80,256]{1,0:T(8,128)S(1)} %get-tuple-element.36), channel_id=1, source_target_pairs={{0,1},{1,0},{2,3},{3,2},{4,5},{5,4},{6,7},{7,6},{8,9},{9,8},{10,11... | collective-permute-start | bytes 245768 | tf_op jit(solution)/shard_map/ppermute | solution.py:68
  21.3 0.5 collective-permute-start.6
  21.8 1.5 %collective-permute-start.7 = (f32[40,128]{1,0:T(8,128)S(1)}, f32[40,128]{1,0:T(8,128)S(1)}, u32[]{:S(2)}, u32[]{:S(2)}) collective-permute-start(f32[40,128]{1,0:T(8,128)S(1)} %add.15.gate_ref), channel_id=1, source_target_pairs={{0,1},{1,0},{2,3},{3,2},{4,5},{5,4},{6,7},{7,6},{8,9},{9,8},{10,11... | collective-permute-start | bytes 61448 | tf_op jit(solution)/shard_map/ppermute | solution.py:626
  23.3 3.0 %collective-permute-done.7 = f32[40,128]{1,0:T(8,128)S(1)} collective-permute-done((f32[40,128]{1,0:T(8,128)S(1)}, f32[40,128]{1,0:T(8,128)S(1)}, u32[]{:S(2)}, u32[]{:S(2)}) %collective-permute-start.7) | collective-permute-done | bytes 20512 | tf_op jit(solution)/shard_map/ppermute | solution.py:626
  26.3 0.6 %collective-permute-start.8 = (f32[40,128]{1,0:T(8,128)S(1)}, f32[40,128]{1,0:T(8,128)S(1)}, u32[]{:S(2)}, u32[]{:S(2)}) collective-permute-start(f32[40,128]{1,0:T(8,128)S(1)} %add.16), channel_id=1, source_target_pairs={{0,8},{4,12},{8,0},{12,4},{16,24},{20,28},{24,16},{28,20},{1,9},{5... | collective-permute-start | bytes 61448 | tf_op jit(solution)/shard_map/ppermute | solution.py:626
  26.8 3.2 %collective-permute-done.8 = f32[40,128]{1,0:T(8,128)S(1)} collective-permute-done((f32[40,128]{1,0:T(8,128)S(1)}, f32[40,128]{1,0:T(8,128)S(1)}, u32[]{:S(2)}, u32[]{:S(2)}) %collective-permute-start.8) | collective-permute-done | bytes 20512 | tf_op jit(solution)/shard_map/ppermute | solution.py:626
  30.0 0.0 collective-permute-done.5.ya_ref.sa_ref
  30.0 0.0 collective-permute-done.6.yb_ref.sb_ref
  30.1 0.1 collective-permute-start.9
  30.2 2.5 %collective-permute-start.10 = (f32[5,8,256]{2,1,0:T(8,128)S(1)}, f32[5,8,256]{2,1,0:T(8,128)S(1)}, u32[]{:S(2)}, u32[]{:S(2)}) collective-permute-start(f32[5,8,256]{2,1,0:T(8,128)S(1)} %get-tuple-element.39), channel_id=1, source_target_pairs={{0,28},{4,8},{8,4},{12,16},{16,12},{20,24},{24,20},{28,0},{1,29},{... | collective-permute-start | bytes 122888 | tf_op jit(solution)/shard_map/ppermute | solution.py:69
  32.6 0.0 collective-permute-start.11
  32.6 4.7 %collective-permute-done.11 = f32[40,128]{1,0:T(8,128)S(1)} collective-permute-done((f32[40,128]{1,0:T(8,128)S(1)}, f32[40,128]{1,0:T(8,128)S(1)}, u32[]{:S(2)}, u32[]{:S(2)}) %collective-permute-start.11) | collective-permute-done | bytes 20512 | tf_op jit(solution)/shard_map/ppermute | solution.py:626
  37.3 0.0 collective-permute-done.9.ra_ref
  37.3 0.0 collective-permute-done.10.rb_ref
  37.3 1.9 %final.1 = (f32[19,16,8,256]{3,2,1,0:T(8,128)}, f32[96,128]{1,0:T(8,128)S(1)}, f32[32,128]{1,0:T(8,128)}) custom-call(f32[19,16,8,256]{3,2,1,0:T(8,128)S(1)} %get-tuple-element.35.post_ref.p_ref, f32[5,8,256]{2,1,0:T(8,128)S(1)} %collective-permute-done.9.ra_ref, f32[5,8,256]{2,1,0:T(8,128)S(1)} %collective-permute-done.10.rb_ref, ...), custom_call_target="tpu_custom_call" | custom-call | tf_op jit(solution)/shard_map/final/pallas_call | solution.py:711
  39.3 2.6 %all-to-all-start = ((f32[32,1,128]{2,1,0:T(1,128)}), f32[32,1,128]{2,1,0:T(1,128)S(1)}, u32[]{:S(2)}, u32[]{:S(2)}) async-start(f32[32,1,128]{2,1,0:T(1,128)} %bitcast.4), calls=%async_computation | async-start | bytes 32768 | tf_op jit(solution)/shard_map/all_to_all | solution.py:712
  41.8 1.7 %collective-permute-start.12 = (f32[40,128]{1,0:T(8,128)S(1)}, f32[40,128]{1,0:T(8,128)S(1)}, u32[]{:S(2)}, u32[]{:S(2)}) collective-permute-start(f32[40,128]{1,0:T(8,128)S(1)} %add.18.gate_ref), channel_id=1, source_target_pairs={{0,2},{1,3},{2,0},{3,1},{4,6},{5,7},{6,4},{7,5},{8,10},{9,11},{10,... | collective-permute-start | bytes 61448 | tf_op jit(solution)/shard_map/ppermute | solution.py:626
  43.6 2.1 %collective-permute-done.12 = f32[40,128]{1,0:T(8,128)S(1)} collective-permute-done((f32[40,128]{1,0:T(8,128)S(1)}, f32[40,128]{1,0:T(8,128)S(1)}, u32[]{:S(2)}, u32[]{:S(2)}) %collective-permute-start.12) | collective-permute-done | bytes 20512 | tf_op jit(solution)/shard_map/ppermute | solution.py:626
  45.7 2.3 %factor.1 = (f32[80,80]{1,0:T(8,128)S(1)}, f32[80,80]{1,0:T(8,128)S(1)}, f32[80,240]{1,0:T(8,128)S(1)}) custom-call(f32[40,128]{1,0:T(8,128)S(1)} %add.19.refs_0_), custom_call_target="tpu_custom_call" | custom-call | tf_op jit(solution)/shard_map/factor/pallas_call | solution.py:714
  48.0 0.0 copy-start
  48.0 4.4 %rotate.1.refs_7_ = f32[80,96,128]{2,1,0:T(8,128)} custom-call(f32[80,240]{1,0:T(8,128)S(1)} %get-tuple-element.47.w_ref, bf16[160,12288]{1,0:T(8,128)(2,1)} %get-tuple-element.48.h_hbm), custom_call_target="tpu_custom_call" | custom-call | tf_op jit(solution)/shard_map/rotate/pallas_call | solution.py:720
  52.4 0.0 all-to-all-done
  52.4 0.0 copy-done
  52.4 2.0 %last.1 = (f32[80,80]{1,0:T(8,128)}, f32[80,96,128]{2,1,0:T(8,128)}) custom-call(f32[32,128]{1,0:T(8,128)S(1)} %bitcast.10, f32[80,80]{1,0:T(8,128)S(1)} %get-tuple-element.43.refs_1_, f32[80,80]{1,0:T(8,128)S(1)} %get-tuple-element.44.refs_2_, f32[80,128]{1,0:T(8,128)S(1)} %get-tuple-element.45.refs_3_, ...), custom_call_target="tpu_custom_call", output_to_operand_aliasing={{1}: (7, {})} | custom-call | tf_op jit(solution)/shard_map/last/pallas_call | solution.py:734
  (7 shorter events, 0.1 us)
Async XLA Ops:
  3.2 9.5 %collective-permute-start = (f32[80,256]{1,0:T(8,128)S(1)}, f32[80,256]{1,0:T(8,128)S(1)}, u32[]{:S(2)}, u32[]{:S(2)}) collective-permute-start(f32[80,256]{1,0:T(8,128)S(1)} %get-tuple-element.28), channel_id=1, source_target_pairs={{0,1},{1,0},{2,3},{3,2},{4,5},{5,4},{6,7},{7,6},{8,9},{9,8},{10,11... | collective-permute-start | bytes 245768 | tf_op jit(solution)/shard_map/ppermute | solution.py:68
  6.3 6.4 %collective-permute-start.1 = (f32[80,256]{1,0:T(8,128)S(1)}, f32[80,256]{1,0:T(8,128)S(1)}, u32[]{:S(2)}, u32[]{:S(2)}) collective-permute-start(f32[80,256]{1,0:T(8,128)S(1)} %get-tuple-element.29), channel_id=1, source_target_pairs={{0,3},{1,2},{2,1},{3,0},{4,7},{5,6},{6,5},{7,4},{8,11},{9,10},{10,... | collective-permute-start | bytes 245768 | tf_op jit(solution)/shard_map/ppermute | solution.py:69
  12.8 5.0 %collective-permute-start.2 = (f32[5,8,256]{2,1,0:T(8,128)S(1)}, f32[5,8,256]{2,1,0:T(8,128)S(1)}, u32[]{:S(2)}, u32[]{:S(2)}) collective-permute-start(f32[5,8,256]{2,1,0:T(8,128)S(1)} %get-tuple-element.32), channel_id=1, source_target_pairs={{0,4},{4,0},{8,12},{12,8},{16,20},{20,16},{24,28},{28,24},{1,5},{5... | collective-permute-start | bytes 122888 | tf_op jit(solution)/shard_map/ppermute | solution.py:68
  12.8 5.5 %collective-permute-start.3 = (f32[5,8,256]{2,1,0:T(8,128)S(1)}, f32[5,8,256]{2,1,0:T(8,128)S(1)}, u32[]{:S(2)}, u32[]{:S(2)}) collective-permute-start(f32[5,8,256]{2,1,0:T(8,128)S(1)} %get-tuple-element.33), channel_id=1, source_target_pairs={{0,28},{4,8},{8,4},{12,16},{16,12},{20,24},{24,20},{28,0},{1,29},{... | collective-permute-start | bytes 122888 | tf_op jit(solution)/shard_map/ppermute | solution.py:69
  16.5 1.2 %collective-permute-start.4 = (f32[40,128]{1,0:T(8,128)S(1)}, f32[40,128]{1,0:T(8,128)S(1)}, u32[]{:S(2)}, u32[]{:S(2)}) collective-permute-start(f32[40,128]{1,0:T(8,128)S(1)} %get-tuple-element.31.gate_ref), channel_id=1, source_target_pairs={{0,4},{4,0},{8,12},{12,8},{16,20},{20,16},{24,28},{28,24},{1,5},{5... | collective-permute-start | bytes 61448 | tf_op jit(solution)/shard_map/ppermute | solution.py:626
  19.7 10.3 %collective-permute-start.5 = (f32[80,256]{1,0:T(8,128)S(1)}, f32[80,256]{1,0:T(8,128)S(1)}, u32[]{:S(2)}, u32[]{:S(2)}) collective-permute-start(f32[80,256]{1,0:T(8,128)S(1)} %get-tuple-element.36), channel_id=1, source_target_pairs={{0,1},{1,0},{2,3},{3,2},{4,5},{5,4},{6,7},{7,6},{8,9},{9,8},{10,11... | collective-permute-start | bytes 245768 | tf_op jit(solution)/shard_map/ppermute | solution.py:68
  21.3 8.7 %collective-permute-start.6 = (f32[80,256]{1,0:T(8,128)S(1)}, f32[80,256]{1,0:T(8,128)S(1)}, u32[]{:S(2)}, u32[]{:S(2)}) collective-permute-start(f32[80,256]{1,0:T(8,128)S(1)} %get-tuple-element.37), channel_id=1, source_target_pairs={{0,3},{1,2},{2,1},{3,0},{4,7},{5,6},{6,5},{7,4},{8,11},{9,10},{10,... | collective-permute-start | bytes 245768 | tf_op jit(solution)/shard_map/ppermute | solution.py:69
  21.8 4.5 %collective-permute-start.7 = (f32[40,128]{1,0:T(8,128)S(1)}, f32[40,128]{1,0:T(8,128)S(1)}, u32[]{:S(2)}, u32[]{:S(2)}) collective-permute-start(f32[40,128]{1,0:T(8,128)S(1)} %add.15.gate_ref), channel_id=1, source_target_pairs={{0,1},{1,0},{2,3},{3,2},{4,5},{5,4},{6,7},{7,6},{8,9},{9,8},{10,11... | collective-permute-start | bytes 61448 | tf_op jit(solution)/shard_map/ppermute | solution.py:626
  26.3 3.8 %collective-permute-start.8 = (f32[40,128]{1,0:T(8,128)S(1)}, f32[40,128]{1,0:T(8,128)S(1)}, u32[]{:S(2)}, u32[]{:S(2)}) collective-permute-start(f32[40,128]{1,0:T(8,128)S(1)} %add.16), channel_id=1, source_target_pairs={{0,8},{4,12},{8,0},{12,4},{16,24},{20,28},{24,16},{28,20},{1,9},{5... | collective-permute-start | bytes 61448 | tf_op jit(solution)/shard_map/ppermute | solution.py:626
  30.1 7.2 %collective-permute-start.9 = (f32[5,8,256]{2,1,0:T(8,128)S(1)}, f32[5,8,256]{2,1,0:T(8,128)S(1)}, u32[]{:S(2)}, u32[]{:S(2)}) collective-permute-start(f32[5,8,256]{2,1,0:T(8,128)S(1)} %get-tuple-element.38), channel_id=1, source_target_pairs={{0,4},{4,0},{8,12},{12,8},{16,20},{20,16},{24,28},{28,24},{1,5},{5... | collective-permute-start | bytes 122888 | tf_op jit(solution)/shard_map/ppermute | solution.py:68
  30.2 7.2 %collective-permute-start.10 = (f32[5,8,256]{2,1,0:T(8,128)S(1)}, f32[5,8,256]{2,1,0:T(8,128)S(1)}, u32[]{:S(2)}, u32[]{:S(2)}) collective-permute-start(f32[5,8,256]{2,1,0:T(8,128)S(1)} %get-tuple-element.39), channel_id=1, source_target_pairs={{0,28},{4,8},{8,4},{12,16},{16,12},{20,24},{24,20},{28,0},{1,29},{... | collective-permute-start | bytes 122888 | tf_op jit(solution)/shard_map/ppermute | solution.py:69
  32.6 4.7 %collective-permute-start.11 = (f32[40,128]{1,0:T(8,128)S(1)}, f32[40,128]{1,0:T(8,128)S(1)}, u32[]{:S(2)}, u32[]{:S(2)}) collective-permute-start(f32[40,128]{1,0:T(8,128)S(1)} %add.17.gate_ref), channel_id=1, source_target_pairs={{0,16},{4,20},{8,24},{12,28},{16,0},{20,4},{24,8},{28,12},{1,17},{... | collective-permute-start | bytes 61448 | tf_op jit(solution)/shard_map/ppermute | solution.py:626
  39.3 13.1 %all-to-all-start = ((f32[32,1,128]{2,1,0:T(1,128)}), f32[32,1,128]{2,1,0:T(1,128)S(1)}, u32[]{:S(2)}, u32[]{:S(2)}) async-start(f32[32,1,128]{2,1,0:T(1,128)} %bitcast.4), calls=%async_computation | async-start | bytes 32768 | tf_op jit(solution)/shard_map/all_to_all | solution.py:712
  41.8 3.9 %collective-permute-start.12 = (f32[40,128]{1,0:T(8,128)S(1)}, f32[40,128]{1,0:T(8,128)S(1)}, u32[]{:S(2)}, u32[]{:S(2)}) collective-permute-start(f32[40,128]{1,0:T(8,128)S(1)} %add.18.gate_ref), channel_id=1, source_target_pairs={{0,2},{1,3},{2,0},{3,1},{4,6},{5,7},{6,4},{7,5},{8,10},{9,11},{10,... | collective-permute-start | bytes 61448 | tf_op jit(solution)/shard_map/ppermute | solution.py:626
  48.0 4.4 %copy-start = (f32[64,3,8,4,128]{4,3,2,1,0:T(4,128)S(1)}, f32[64,3,8,4,128]{4,3,2,1,0:T(4,128)}, u32[]{:S(2)}) copy-start(f32[64,3,8,4,128]{4,3,2,1,0:T(4,128)} %param.10) | copy-start | bytes 9437188
